TPU v7x, 32 devices: a whole 2x2x4 slice. The times are simulated.
32 devices in a mesh: dp: 8 (over z, x), group: 4 (over y, core).
Axes of the slice: x: 2, y: 2, z: 4, core: 2. Of those that a mesh axis runs over, the one named last changes fastest.
Arguments:
- latents: bfloat16 [128, 256, 384], P(('dp', 'group')), may hold values from -40 to 40
- cotangent: bfloat16 [128, 256, 384], P(('dp', 'group')), may hold values from -6 to 6
- timestep: int32 [128], P(('dp', 'group')), may hold values from 0 to 999
- labels: int32 [128], P(('dp', 'group')), may hold values from 0 to 1000
- class_table: bfloat16 [1001, 384], replicated, may hold values from -6 to 6
- input_proj: float32 [384, 4992], P('dp'), may hold values from -4 to 4
- attn_proj: float32 [384, 384], P('dp'), may hold values from -0.3125 to 0.3125
- mlp_down: float32 [1536, 384], P('dp'), may hold values from -0.15625 to 0.15625
- biases: float32 [5376], P('dp'), may hold values from -0.18 to 0.18
- mean_input: float32 [384, 4992], P('dp'), may hold values from -108.6116 to 108.6116
- mean_attn: float32 [384, 384], P('dp'), may hold values from -108.6116 to 108.6116
- mean_down: float32 [1536, 384], P('dp'), may hold values from -108.6116 to 108.6116
- mean_biases: float32 [5376], P('dp'), may hold values from -108.6116 to 108.6116
- sq_input: float32 [384, 4992], P('dp'), may hold values from 0.98304 to 98.304
- sq_attn: float32 [384, 384], P('dp'), may hold values from 0.98304 to 98.304
- sq_down: float32 [1536, 384], P('dp'), may hold values from 0.98304 to 98.304
- sq_biases: float32 [5376], P('dp'), may hold values from 0.98304 to 98.304
Outputs:
- block_out: bfloat16 [128, 256, 384], P(('dp', 'group'))
- grad_latents: float32 [128, 256, 384], P(('dp', 'group'))
- grad_cond: float32 [128, 384], P(('dp', 'group'))
- grad_input: float32 [384, 4992], P('dp')
- grad_attn: float32 [384, 384], P('dp')
- grad_down: float32 [1536, 384], P('dp')
- grad_biases: float32 [5376], P('dp')
- new_input: float32 [384, 4992], P('dp')
- new_attn: float32 [384, 384], P('dp')
- new_down: float32 [1536, 384], P('dp')
- new_biases: float32 [5376], P('dp')
- new_mean_input: float32 [384, 4992], P('dp')
- new_mean_attn: float32 [384, 384], P('dp')
- new_mean_down: float32 [1536, 384], P('dp')
- new_mean_biases: float32 [5376], P('dp')
- new_sq_input: float32 [384, 4992], P('dp')
- new_sq_attn: float32 [384, 384], P('dp')
- new_sq_down: float32 [1536, 384], P('dp')
- new_sq_biases: float32 [5376], P('dp')
All inputs are finite; a program needn't handle non-finite values.
Results may differ from a plain program's by a relative error of at most 0.012.
The roundings to bfloat16 on the way count: a program that leaves them out, or rounds other values in their place, can miss the bound.
Values may be sent and summed in bfloat16 or wider, within the bound.
No kernel may reach another device: no remote copies, remote signals or barrier semaphores. Data moves between devices by JAX's collectives and lax.ppermute only.
A program may use at most 128 MiB of HBM per device.

v0:
```python
import functools
import math

import jax
import jax.numpy as jnp
from jax import lax
from jax.experimental import pallas as pl
from jax.experimental.pallas import tpu as pltpu
from jax.sharding import PartitionSpec as P

HEAD = 64
STEP = 2
GROUP = 4

learn_rate = 0.01
beta_one = 0.9
beta_two = 0.999
adam_eps = 1e-08
norm_eps = 1e-06

f32 = jnp.float32
bf16 = jnp.bfloat16

NN = (((1,), (0,)), ((), ()))
NT = (((1,), (1,)), ((), ()))
TN = (((0,), (0,)), ((), ()))


def dot(left, right, dims=NN):
    return lax.dot_general(left, right, dims, preferred_element_type=f32)


def row_mean(values):
    return jnp.sum(values, axis=-1, keepdims=True) * (1.0 / values.shape[-1])


def layer_norm(values):
    centred = values - row_mean(values)
    inv_std = lax.rsqrt(row_mean(centred * centred) + norm_eps)
    return centred * inv_std, inv_std


def norm_back(gradient, normed, inv_std):
    return inv_std * (gradient - row_mean(gradient) - normed * row_mean(gradient * normed))


def token_sum(values):
    return jnp.sum(values, axis=0, keepdims=True)


def time_embed(timestep, model_width):
    half_width = model_width // 2
    frequency = jnp.exp(
        jnp.arange(half_width, dtype=f32) * (-math.log(10000.0) / half_width)
    )
    angles = timestep.astype(f32)[:, None] * frequency[None, :]
    return jnp.concatenate([jnp.cos(angles), jnp.sin(angles)], axis=1)


def unpack_columns(place, pieces, whole):
    owners, rows, width = pieces[0].shape
    me, mine = place[0], place[1]
    for block in range(GROUP):
        for k in range(GROUP):

            @pl.when((mine ^ k) == block)
            def _():
                for owner in range(owners):
                    whole[owner * rows : (owner + 1) * rows, block * width : (block + 1) * width] = (
                        pieces[k][owner ^ me]
                    )


def unpack_rows(place, pieces, whole):
    owners, rows, width = pieces[0].shape
    me, mine = place[0], place[1]
    for block in range(GROUP):
        for k in range(GROUP):

            @pl.when((mine ^ k) == block)
            def _():
                for owner in range(owners):
                    start = (owner * GROUP + block) * rows
                    whole[start : start + rows, :] = pieces[k][owner ^ me]


def pack_block(place, block, owner, value, keep, send):
    k = place[1] ^ block
    spot = place[0] ^ owner
    half = k >> 1

    @pl.when((k & 1) == 0)
    def _():
        keep[half, spot] = value

    @pl.when((k & 1) == 1)
    def _():
        send[half, spot] = value.astype(bf16)


def lane_masks():
    lane = lax.broadcasted_iota(jnp.int32, (1, 2 * HEAD), 1)
    low = (lane < HEAD).astype(f32)
    return low.astype(bf16), (1.0 - low).astype(bf16)


def attn_forward(place, lat, mod, bias, p0, p1, p2, p3, qkv_o, att_o, branch_o, lse_o, whole, att_t):
    width = lat.shape[-1]

    @pl.when(pl.program_id(0) == 0)
    def _():
        unpack_columns(place, (p0, p1, p2, p3), whole)

    normed, _ = layer_norm(lat[0].astype(f32))
    input_a = (normed * (1.0 + mod[0, 1:2]) + mod[0, 0:1]).astype(bf16)
    projected = dot(input_a, whole[:, : 3 * width])
    queries = (projected[:, :width] + bias[0:1, :width]).astype(bf16)
    key_vecs = projected[:, width : 2 * width].astype(bf16)
    values = (projected[:, 2 * width :] + bias[0:1, width : 2 * width]).astype(bf16)
    qkv_o[0, :, :width] = queries
    qkv_o[0, :, width : 2 * width] = key_vecs
    qkv_o[0, :, 2 * width :] = values
    values_t = values.T
    scale = 1.0 / math.sqrt(HEAD)
    masks = lane_masks()
    for pair in range(width // (2 * HEAD)):
        cols = slice(pair * 2 * HEAD, (pair + 1) * 2 * HEAD)
        for side in range(2):
            head = pair * 2 + side
            scores = dot(key_vecs[:, cols] * masks[side], queries[:, cols], NT) * scale
            peak = jnp.max(scores, axis=0, keepdims=True)
            powers = jnp.exp(scores - peak)
            total = jnp.sum(powers, axis=0, keepdims=True)
            lse_o[0, head : head + 1, :] = peak + jnp.log(total)
            probs = (powers * (1.0 / total)).astype(bf16)
            att_t[head * HEAD : (head + 1) * HEAD, :] = dot(
                values_t[head * HEAD : (head + 1) * HEAD, :], probs
            )
    attended = att_t[...].T.astype(bf16)
    att_o[0] = attended
    branch_o[0] = dot(attended, whole[:, 3 * width :]) + bias[0:1, 2 * width : 3 * width]


def mlp_both(
    place, lat, cot, branch, att, mod, bias,
    u0, u1, u2, u3, w0, w1, w2, w3,
    out_o, dmid_o, dmod_o, gattn_o, gbias_o, upk_o, ups_o, dnk_o, dns_o,
    w_up, w_down, gelu_s, slope_s, dpre_s, acc_up, acc_down,
):
    width = lat.shape[-1]
    hidden = w_up.shape[1]
    step = pl.program_id(0)
    first = step == 0

    @pl.when(first)
    def _():
        unpack_columns(place, (u0, u1, u2, u3), w_up)
        unpack_rows(place, (w0, w1, w2, w3), w_down)
        acc_up[...] = jnp.zeros_like(acc_up)
        acc_down[...] = jnp.zeros_like(acc_down)
        gattn_o[...] = jnp.zeros_like(gattn_o)
        gbias_o[...] = jnp.zeros_like(gbias_o)

    b_up = bias[0:1, 3 * width : 3 * width + hidden]
    b_down = bias[0:1, 3 * width + hidden : 4 * width + hidden]
    gate_a, shift_m, scale_m, gate_m = mod[0, 2:3], mod[0, 3:4], mod[0, 4:5], mod[0, 5:6]
    branch_a = branch[0]
    middle = lat[0].astype(f32) + gate_a * branch_a
    normed, inv_std = layer_norm(middle)
    input_m = (normed * (1.0 + scale_m) + shift_m).astype(bf16)
    inner = math.sqrt(2.0 / math.pi)
    chunk = 512
    for start in range(0, hidden, chunk):
        cols = slice(start, start + chunk)
        pre = dot(input_m, w_up[:, cols]) + b_up[:, cols]
        square = pre * pre
        tangent = jnp.tanh(pre * (inner + (inner * 0.044715) * square))
        upper = 0.5 * (1.0 + tangent)
        gelu_s[:, cols] = (pre * upper).astype(bf16)
        slope_s[:, cols] = upper + (0.5 * pre) * (1.0 - tangent * tangent) * (
            inner + (inner * 3.0 * 0.044715) * square
        )
    branch_m = dot(gelu_s[...], w_down[...]) + b_down
    out_o[0] = (middle + gate_m * branch_m).astype(bf16)
    grad_out = cot[0].astype(f32)
    dmod_o[0, 5:6] = token_sum(grad_out * branch_m)
    d_branch_m = grad_out * gate_m
    d_branch_mb = d_branch_m.astype(bf16)
    acc_down[...] += dot(d_branch_mb, gelu_s[...], TN)
    gbias_o[0:1, 3 * width + hidden : 4 * width + hidden] += token_sum(d_branch_m)
    for start in range(0, hidden, chunk):
        cols = slice(start, start + chunk)
        d_pre = dot(d_branch_mb, w_down[cols, :], NT) * slope_s[:, cols]
        gbias_o[0:1, 3 * width + start : 3 * width + start + chunk] += token_sum(d_pre)
        dpre_s[:, cols] = d_pre.astype(bf16)
    acc_up[...] += dot(input_m, dpre_s[...], TN)
    d_input = dot(dpre_s[...], w_up[...], NT)
    dmod_o[0, 4:5] = token_sum(d_input * normed)
    dmod_o[0, 3:4] = token_sum(d_input)
    d_middle = grad_out + norm_back(d_input * (1.0 + scale_m), normed, inv_std)
    dmid_o[0] = d_middle
    dmod_o[0, 2:3] = token_sum(d_middle * branch_a)
    d_branch_a = d_middle * gate_a
    gbias_o[0:1, 2 * width : 3 * width] += token_sum(d_branch_a)
    gattn_o[...] += dot(att[0], d_branch_a.astype(bf16), TN)

    @pl.when(step == pl.num_programs(0) - 1)
    def _():
        owners, rows = upk_o.shape[1], upk_o.shape[2]
        for block in range(GROUP):
            for owner in range(owners):
                value = acc_up[owner * rows : (owner + 1) * rows, block * width : (block + 1) * width]
                pack_block(place, block, owner, value, upk_o, ups_o)
        whole_down = acc_down[...].T
        for block in range(GROUP):
            for owner in range(owners):
                start = (owner * GROUP + block) * rows
                pack_block(place, block, owner, whole_down[start : start + rows, :], dnk_o, dns_o)


def attn_backward(
    place, lat, dmid, qkv, lse, mod, gattn, p0, p1, p2, p3,
    glat_o, dmod_o, gbias_o, keep_o, send_o,
    whole, dq_t, dproj, acc,
):
    width = lat.shape[-1]
    step = pl.program_id(0)

    @pl.when(step == 0)
    def _():
        unpack_columns(place, (p0, p1, p2, p3), whole)
        acc[...] = jnp.zeros_like(acc)
        gbias_o[...] = jnp.zeros_like(gbias_o)

    shift_a, scale_a, gate_a = mod[0, 0:1], mod[0, 1:2], mod[0, 2:3]
    normed, inv_std = layer_norm(lat[0].astype(f32))
    input_a = (normed * (1.0 + scale_a) + shift_a).astype(bf16)
    d_middle = dmid[0]
    d_att = dot((d_middle * gate_a).astype(bf16), whole[:, 3 * width :], NT).astype(bf16)
    scale = 1.0 / math.sqrt(HEAD)
    masks = lane_masks()
    low = lax.broadcasted_iota(jnp.int32, (1, 2 * HEAD), 1) < HEAD
    keys_t = qkv[0, :, width : 2 * width].T
    for pair in range(width // (2 * HEAD)):
        cols = slice(pair * 2 * HEAD, (pair + 1) * 2 * HEAD)
        q_pair = qkv[0, :, pair * 2 * HEAD : (pair + 1) * 2 * HEAD]
        k_pair = qkv[0, :, width + pair * 2 * HEAD : width + (pair + 1) * 2 * HEAD]
        v_pair = qkv[0, :, 2 * width + pair * 2 * HEAD : 2 * width + (pair + 1) * 2 * HEAD]
        do_pair = d_att[:, cols]
        d_keys, d_values = [], []
        for side in range(2):
            head = pair * 2 + side
            scores = dot(k_pair * masks[side], q_pair, NT) * scale
            probs = jnp.exp(scores - lse[0, head : head + 1, :])
            d_values.append(dot(probs.astype(bf16), do_pair))
            d_probs = dot(v_pair * masks[side], do_pair, NT)
            delta = jnp.sum(probs * d_probs, axis=0, keepdims=True)
            d_scores = (probs * (d_probs - delta) * scale).astype(bf16)
            d_keys.append(dot(d_scores, q_pair))
            dq_t[head * HEAD : (head + 1) * HEAD, :] = dot(
                keys_t[head * HEAD : (head + 1) * HEAD, :], d_scores
            )
        d_key = jnp.where(low, d_keys[0], d_keys[1])
        d_value = jnp.where(low, d_values[0], d_values[1])
        dproj[:, width + pair * 2 * HEAD : width + (pair + 1) * 2 * HEAD] = d_key.astype(bf16)
        dproj[:, 2 * width + pair * 2 * HEAD : 2 * width + (pair + 1) * 2 * HEAD] = d_value.astype(
            bf16
        )
        gbias_o[0:1, width + pair * 2 * HEAD : width + (pair + 1) * 2 * HEAD] += token_sum(d_value)
    d_query = dq_t[...].T
    gbias_o[0:1, :width] += token_sum(d_query)
    dproj[:, :width] = d_query.astype(bf16)
    acc[...] += dot(input_a, dproj[...], TN)
    d_input = dot(dproj[...], whole[:, : 3 * width], NT)
    dmod_o[0, 1:2] = token_sum(d_input * normed)
    dmod_o[0, 0:1] = token_sum(d_input)
    glat_o[0] = d_middle + norm_back(d_input * (1.0 + scale_a), normed, inv_std)

    @pl.when(step == pl.num_programs(0) - 1)
    def _():
        owners, rows = keep_o.shape[1], keep_o.shape[2]
        for block in range(GROUP):
            for owner in range(owners):
                span = slice(owner * rows, (owner + 1) * rows)
                if block < GROUP - 1:
                    value = acc[span, block * width : (block + 1) * width]
                else:
                    value = gattn[span, :]
                pack_block(place, block, owner, value, keep_o, send_o)


def adam_parts(weight, moment, second, gradient):
    moment = beta_one * moment + (1.0 - beta_one) * gradient
    second = beta_two * second + (1.0 - beta_two) * gradient * gradient
    first_fix = 1.0 - beta_one**STEP
    second_fix = 1.0 - beta_two**STEP
    weight = weight - (learn_rate / first_fix) * moment / (
        jnp.sqrt(second * (1.0 / second_fix)) + adam_eps
    )
    return weight, moment, second


def adam_kernel(place, *refs):
    (att0, att1, up0, up1, dn0, dn1, gmod, gbias) = refs[:8]
    weights, means, squares = refs[8:12], refs[12:16], refs[16:20]
    grads, new_w, new_m, new_s = refs[20:24], refs[24:28], refs[28:32], refs[32:36]
    width = att0.shape[-1]

    def write(which, where, gradient):
        grads[which][where] = gradient
        result = adam_parts(
            weights[which][where], means[which][where], squares[which][where], gradient
        )
        new_w[which][where], new_m[which][where], new_s[which][where] = result

    def block_of(same, other, block):
        k = place[1] ^ block
        mine = jnp.where((k & 2) == 0, same[0], same[1])
        theirs = jnp.where((k & 2) == 0, other[0], other[1])
        return jnp.where((k & 1) == 0, mine, theirs)

    everything = slice(None)
    for block in range(GROUP):
        g_att = block_of(att0, att1, block)
        if block < GROUP - 1:
            write(0, (everything, slice(block * width, (block + 1) * width)), g_att)
        else:
            write(1, (everything, everything), g_att)
        at = (GROUP - 1 + block) * width
        write(0, (everything, slice(at, at + width)), block_of(up0, up1, block))
        write(2, (block,), block_of(dn0, dn1, block))
    at = (2 * GROUP - 1) * width
    write(0, (everything, slice(at, at + gmod.shape[1])), gmod[...])
    write(3, (everything, everything), gbias[...])


def swap(value, axis, bit):
    size = lax.axis_size(axis)
    return lax.ppermute(value, axis, [(i, i ^ bit) for i in range(size)])


def gather_bits(size):
    bits = [1 << b for b in range(size.bit_length() - 1)]
    return bits[1:][::-1] + bits[:1]


def dp_gather(value):
    owners = lax.axis_size("dp")
    bits = gather_bits(owners)
    held, order = value[None], [0]
    for bit in bits:
        held = jnp.concatenate([held, swap(held, "dp", bit)], axis=0)
        order = order + [o ^ bit for o in order]
    spots = [order.index(i) for i in range(owners)]
    return held, spots


def reorder(held, spots):
    return jnp.concatenate([held[s : s + 1] for s in spots], axis=0)


def group_gather(value):
    two = swap(value, "group", 2)
    one = swap(value, "group", 1)
    three = swap(two, "group", 1)
    return value, one, two, three


def dp_scatter(keep, axis, compress):
    owners = lax.axis_size("dp")
    for bit in [1 << b for b in range(owners.bit_length() - 1)]:
        shape = keep.shape
        pairs = keep.reshape(shape[:axis] + (shape[axis] // 2, 2) + shape[axis + 1 :])
        mine = lax.index_in_dim(pairs, 0, axis + 1, keepdims=False)
        theirs = lax.index_in_dim(pairs, 1, axis + 1, keepdims=False)
        if compress:
            theirs = theirs.astype(bf16)
        keep = mine + swap(theirs, "dp", bit).astype(f32)
    return lax.index_in_dim(keep, 0, axis, keepdims=False)


def reduce_blocks(keep, send):
    keep = keep + swap(send, "group", 1).astype(f32)
    keep = dp_scatter(keep, 1, True)
    sent = keep.astype(bf16)
    received = swap(sent[::-1], "group", 2)
    own = sent.astype(f32) + received.astype(f32)
    return own, swap(own, "group", 1)


def sum_all(value):
    value = value + swap(value, "group", 1)
    value = value + swap(value, "group", 2)
    owners = lax.axis_size("dp")
    for bit in [1 << b for b in range(owners.bit_length() - 1)]:
        value = value + swap(value, "dp", bit)
    return value


def compiler(limit=56):
    return pltpu.CompilerParams(
        dimension_semantics=("arbitrary",), vmem_limit_bytes=limit * 1024 * 1024
    )


def whole_spec(array):
    zeros = (0,) * len(array.shape)
    return pl.BlockSpec(tuple(array.shape), lambda l, *_: zeros)


def latent_spec(array):
    zeros = (0,) * (len(array.shape) - 1)
    return pl.BlockSpec((1,) + tuple(array.shape[1:]), lambda l, *_: (l,) + zeros)


def call(kernel, place, latent_args, whole_args, latent_outs, whole_outs, scratch, grid, flip=False):
    ins = [latent_spec(a) for a in latent_args] + [whole_spec(a) for a in whole_args]
    outs = [latent_spec(a) for a in latent_outs] + [whole_spec(a) for a in whole_outs]
    return pl.pallas_call(
        kernel,
        grid_spec=pltpu.PrefetchScalarGridSpec(
            num_scalar_prefetch=1,
            grid=(grid,),
            in_specs=ins,
            out_specs=outs,
            scratch_shapes=scratch,
        ),
        out_shape=list(latent_outs) + list(whole_outs),
        compiler_params=compiler(),
        name=kernel.__name__,
    )(place, *latent_args, *whole_args)


def like(shape, dtype):
    return jax.ShapeDtypeStruct(shape, dtype)


def body(
    latents, cotangent, timestep, labels, class_table,
    input_proj, attn_proj, mlp_down, biases,
    mean_input, mean_attn, mean_down, mean_biases,
    sq_input, sq_attn, sq_down, sq_biases,
):
    count, seq_len, width = latents.shape
    rows = input_proj.shape[0]
    owners = lax.axis_size("dp")
    hidden = mlp_down.shape[0] * owners
    heads = width // HEAD
    me = lax.axis_index("dp")
    mine = lax.axis_index("group")
    place = jnp.stack([me, mine]).astype(jnp.int32)

    class_count = class_table.shape[0]
    one_hot = (labels[:, None] == jnp.arange(class_count, dtype=jnp.int32)[None, :]).astype(bf16)
    condition = time_embed(timestep, width) + dot(one_hot, class_table)
    sigmoid_c = jax.nn.sigmoid(condition)
    cond_act = (condition * sigmoid_c).astype(bf16)
    bias_shard = biases.shape[0]
    bias_rows = -(-bias_shard // width)
    bias_b = jnp.pad(biases.astype(bf16), (0, bias_rows * width - bias_shard)).reshape(-1, width)
    small, spots = dp_gather(jnp.concatenate([cond_act, bias_b], axis=0))
    small = reorder(small, spots)
    cond_rel = small[:, :count]
    bias_rel = small[:, count:].reshape(owners, -1)[:, :bias_shard]
    absolute = jnp.arange(owners, dtype=jnp.int32) ^ me
    bias_all = jnp.take(bias_rel, absolute, axis=0).reshape(1, -1).astype(f32)
    mod_at = 3 * width + hidden
    w_mod = input_proj[:, mod_at:].astype(bf16)
    cond_cols = lax.dynamic_slice_in_dim(cond_rel.reshape(owners * count, width), me * rows, rows, 1)
    partial = dot(cond_cols, w_mod).reshape(owners, count, -1)
    bias_mod_at = 4 * width + hidden
    modulation = dp_scatter(partial, 0, False) + bias_all[:, bias_mod_at:]
    mod = modulation.reshape(count, 6, width)

    att_blocks = jnp.stack(
        [input_proj[:, b * width : (b + 1) * width] for b in range(3)] + [attn_proj]
    )
    up_blocks = jnp.stack(
        [input_proj[:, (3 + b) * width : (4 + b) * width] for b in range(hidden // width)]
    )
    down_blocks = mlp_down.reshape(GROUP, rows, width)

    def pick(blocks):
        return lax.dynamic_index_in_dim(blocks, mine, 0, keepdims=False).astype(bf16)

    def weights_of(blocks):
        held, spots = dp_gather(pick(blocks))
        return [reorder(part, spots) for part in group_gather(held)]

    att_parts = weights_of(att_blocks)
    up_parts = weights_of(up_blocks)
    down_parts = weights_of(down_blocks)

    qkv, attended, branch_a, lse = call(
        attn_forward, place,
        [latents, mod], [bias_all] + att_parts,
        [
            like((count, seq_len, 3 * width), bf16),
            like((count, seq_len, width), bf16),
            like((count, seq_len, width), f32),
            like((count, heads, seq_len), f32),
        ],
        [],
        [pltpu.VMEM((width, 4 * width), bf16), pltpu.VMEM((width, seq_len), f32)],
        count,
    )
    kept = like((2, owners, rows, width), f32)
    sent = like((2, owners, rows, width), bf16)
    bias_like = like((1, bias_mod_at), f32)
    block_out, d_middle, d_mod_m, g_attn, g_bias_m, up_keep, up_send, dn_keep, dn_send = call(
        mlp_both, place,
        [latents, cotangent, branch_a, attended, mod], [bias_all] + up_parts + down_parts,
        [
            like((count, seq_len, width), bf16),
            like((count, seq_len, width), f32),
            like((count, 6, width), f32),
        ],
        [like((width, width), f32), bias_like, kept, sent, kept, sent],
        [
            pltpu.VMEM((width, hidden), bf16),
            pltpu.VMEM((hidden, width), bf16),
            pltpu.VMEM((seq_len, hidden), bf16),
            pltpu.VMEM((seq_len, hidden), f32),
            pltpu.VMEM((seq_len, hidden), bf16),
            pltpu.VMEM((width, hidden), f32),
            pltpu.VMEM((width, hidden), f32),
        ],
        count,
    )
    grad_latents, d_mod_a, g_bias_a, at_keep, at_send = call(
        attn_backward, place,
        [latents, d_middle, qkv, lse, mod], [g_attn] + att_parts,
        [like((count, seq_len, width), f32), like((count, 2, width), f32)],
        [like((1, 2 * width), f32), kept, sent],
        [
            pltpu.VMEM((width, 4 * width), bf16),
            pltpu.VMEM((width, seq_len), f32),
            pltpu.VMEM((seq_len, 3 * width), bf16),
            pltpu.VMEM((width, 3 * width), f32),
        ],
        count,
    )

    d_modulation = jnp.concatenate([d_mod_a, d_mod_m[:, 2:]], axis=1).reshape(count, 6 * width)
    d_modulation_b = d_modulation.astype(bf16)
    bias_grad = jnp.concatenate(
        [
            g_bias_a[0],
            g_bias_m[0, 2 * width :],
            jnp.sum(d_modulation, axis=0),
        ]
    )
    dm_rel = reorder(*dp_gather(d_modulation_b))
    dm_parts = group_gather(dm_rel)
    cond_parts = group_gather(cond_rel)
    dm_all = jnp.concatenate(dm_parts, axis=0).reshape(-1, 6 * width)
    cond_all = jnp.concatenate(cond_parts, axis=0).reshape(-1, width)
    g_mod = dot(lax.dynamic_slice_in_dim(cond_all, me * rows, rows, 1), dm_all, TN)

    back = dot(dm_rel.reshape(owners * count, 6 * width), w_mod, NT).reshape(owners, count, rows)
    for bit in [1 << b for b in range(owners.bit_length() - 1)]:
        shaped = back.reshape(owners // (2 * bit), 2, bit, count, rows)
        received = swap(shaped[:, 1], "dp", bit)
        back = jnp.stack([shaped[:, 0], received], axis=1).reshape(owners, count, rows)
    back = jnp.take(back, absolute, axis=0)
    d_cond = back.transpose(1, 0, 2).reshape(count, width)
    grad_cond = d_cond * (sigmoid_c * (1.0 + condition * (1.0 - sigmoid_c)))

    up_own, up_other = reduce_blocks(up_keep, up_send)
    dn_own, dn_other = reduce_blocks(dn_keep, dn_send)
    at_own, at_other = reduce_blocks(at_keep, at_send)
    bias_sum = lax.dynamic_slice_in_dim(sum_all(bias_grad), me * bias_shard, bias_shard, 0)

    steps = rows // 16 if rows % 16 == 0 else 1
    block_rows = rows // steps

    def spec_of(array):
        if array.ndim == 3:
            return pl.BlockSpec((array.shape[0], block_rows, width), lambda s, *_: (0, s, 0))
        if array.shape[0] == 1:
            return pl.BlockSpec(tuple(array.shape), lambda s, *_: (0, 0))
        return pl.BlockSpec((block_rows, array.shape[1]), lambda s, *_: (s, 0))

    def shaped(four):
        return [four[0], four[1], four[2].reshape(GROUP, rows, width), four[3].reshape(1, -1)]

    state = (
        shaped((input_proj, attn_proj, mlp_down, biases))
        + shaped((mean_input, mean_attn, mean_down, mean_biases))
        + shaped((sq_input, sq_attn, sq_down, sq_biases))
    )
    args = [at_own, at_other, up_own, up_other, dn_own, dn_other, g_mod, bias_sum.reshape(1, -1)]
    args = args + state
    results = [like(a.shape, f32) for a in state[:4]] * 4
    outs = pl.pallas_call(
        adam_kernel,
        grid_spec=pltpu.PrefetchScalarGridSpec(
            num_scalar_prefetch=1,
            grid=(steps,),
            in_specs=[spec_of(a) for a in args],
            out_specs=[spec_of(a) for a in results],
        ),
        out_shape=results,
        compiler_params=compiler(),
        name="adam",
    )(place, *args)

    def flat(four):
        return (four[0], four[1], four[2].reshape(mlp_down.shape), four[3].reshape(-1))

    return (
        (block_out, grad_latents, grad_cond)
        + flat(outs[:4]) + flat(outs[4:8]) + flat(outs[8:12]) + flat(outs[12:16])
    )


def solution(mesh):
    tokens = P(("dp", "group"), None, None)
    four = (P("dp", None), P("dp", None), P("dp", None), P("dp"))
    in_specs = (tokens, tokens, P(("dp", "group")), P(("dp", "group")), P()) + four * 3
    out_specs = (tokens, tokens, P(("dp", "group"), None)) + four * 4
    return jax.shard_map(body, mesh=mesh, in_specs=in_specs, out_specs=out_specs, check_vma=False)
```

profile of v0, /device:TPU:0, one launch (start us, length us, event | category | flops | bytes accessed | tf_op | source)
XLA Modules:
  0.0 227.9 jit_solution(4163925197936303594)
XLA Ops:
  1.7 4.1 %collective-permute-start.18 = (bf16[1,48,384]{2,1,0:T(8,128)(2,1)S(1)}, bf16[1,48,384]{2,1,0:T(8,128)(2,1)S(1)}, u32[]{:S(2)}, u32[]{:S(2)}) collective-permute-start(bf16[1,48,384]{2,1,0:T(8,128)(2,1)S(1)} %get-tuple-element.88), channel_id=1, source_target_pairs={{0,16},{4,20},{8,24},{12,28},{16,0},{20,4},{24,8},{28,12},{1,17},{... | collective-permute-start | bytes 110600 | tf_op jit(solution)/shard_map/ppermute | solution.py:339
  7.2 3.0 %collective-permute-start.6 = (bf16[1,48,384]{2,1,0:T(8,128)(2,1)S(1)}, bf16[1,48,384]{2,1,0:T(8,128)(2,1)S(1)}, u32[]{:S(2)}, u32[]{:S(2)}) collective-permute-start(bf16[1,48,384]{2,1,0:T(8,128)(2,1)S(1)} %get-tuple-element.92), channel_id=1, source_target_pairs={{0,16},{4,20},{8,24},{12,28},{16,0},{20,4},{24,8},{28,12},{1,17},{... | collective-permute-start | bytes 110600 | tf_op jit(solution)/shard_map/ppermute | solution.py:339
  12.7 4.5 %collective-permute-done = bf16[1,6,384]{2,1,0:T(8,128)(2,1)S(1)} collective-permute-done((bf16[1,6,384]{2,1,0:T(8,128)(2,1)S(1)}, bf16[1,6,384]{2,1,0:T(8,128)(2,1)S(1)}, u32[]{:S(2)}, u32[]{:S(2)}) %collective-permute-start) | collective-permute-done | bytes 4640 | tf_op jit(solution)/shard_map/ppermute | solution.py:339
  17.2 1.6 collective-permute-start.1
  18.9 2.1 collective-permute-done.1
  23.1 1.8 collective-permute-done.2
  25.0 1.6 collective-permute-start.49
  29.9 1.6 collective-permute-start.19
  32.1 1.6 collective-permute-start.7
  40.8 1.9 collective-permute-done.4
  77.3 14.8 %attn_forward.1 = (bf16[4,256,1152]{2,1,0:T(8,128)(2,1)}, bf16[4,256,384]{2,1,0:T(8,128)(2,1)}, f32[4,256,384]{2,1,0:T(8,128)}, f32[4,6,256]{2,1,0:T(8,128)}) custom-call(s32[2]{0:T(128)} %pad_add_fusion.place, bf16[4,256,384]{2,1,0:T(8,128)(2,1)} %lat.5, f32[4,6,384]{2,1,0:T(8,128)} %broadcast_add_fusion.mod, f32[1,5376]{1,0:T(1,128)} %copy-done.20, ...), custom_call_target="tpu_custom_call" | custom-call | tf_op jit(solution)/shard_map/attn_forward/pallas_call | solution.py:419
  93.0 21.1 %mlp_both.1 = (bf16[4,256,384]{2,1,0:T(8,128)(2,1)}, f32[4,256,384]{2,1,0:T(8,128)}, f32[4,6,384]{2,1,0:T(8,128)}, f32[384,384]{1,0:T(8,128)}, f32[1,3072]{1,0:T...) custom-call(s32[2]{0:T(128)} %pad_add_fusion.place, ...), custom_call_target="tpu_custom_call" | custom-call | tf_op jit(solution)/shard_map/mlp_both/pallas_call | solution.py:419
  114.9 19.8 %attn_backward.1 = (f32[4,256,384]{2,1,0:T(8,128)}, f32[4,2,384]{2,1,0:T(2,128)}, f32[1,768]{1,0:T(1,128)}, f32[2,8,48,384]{3,2,1,0:T(8,128)}, bf16[2,8,48,384]{3,2,1,0:T(8,128)(2,1)}) custom-call(s32[2]{0:T(128)} %pad_add_fusion.place, bf16[4,256,384]{2,1,0:T(8,128)(2,1)} %lat.5, f32[4,256,384]{2,1,0:T(8,128)} %get-tuple-element.56.dmid, ...), custom_call_target="tpu_custom_call" | custom-call | tf_op jit(solution)/shard_map/attn_backward/pallas_call | solution.py:419
  136.4 2.7 %collective-permute-start.24 = (bf16[1,4,2304]{2,1,0:T(4,128)(2,1)S(1)}, bf16[1,4,2304]{2,1,0:T(4,128)(2,1)S(1)}, u32[]{:S(2)}, u32[]{:S(2)}) collective-permute-start(bf16[1,4,2304]{2,1,0:T(4,128)(2,1)S(1)} %convert_element_type.184), channel_id=1, source_target_pairs={{0,16},{4,20},{8,24},{12,28},{16,0},{20,4},{24,8},{28,12},{1,17},{... | collective-permute-start | bytes 55304 | tf_op jit(solution)/shard_map/ppermute | solution.py:339
  143.5 1.6 collective-permute-done.25
  147.4 2.2 collective-permute-done.26
  157.3 2.5 %collective-permute-start.58 = (f32[5376]{0:T(1024)S(1)}, f32[5376]{0:T(1024)S(1)}, u32[]{:S(2)}, u32[]{:S(2)}) collective-permute-start(f32[5376]{0:T(1024)S(1)} %add.152), channel_id=1, source_target_pairs={{0,16},{4,20},{8,24},{12,28},{16,0},{20,4},{24,8},{28,12},{1,17},{... | collective-permute-start | bytes 64520 | tf_op jit(solution)/shard_map/ppermute | solution.py:339
  162.8 1.6 collective-permute-done.29
  167.3 2.3 collective-permute-done.52
  178.5 3.9 %collective-permute-done.43 = bf16[2,4,48,384]{3,2,1,0:T(8,128)(2,1)S(1)} collective-permute-done((bf16[2,4,48,384]{3,2,1,0:T(8,128)(2,1)S(1)}, bf16[2,4,48,384]{3,2,1,0:T(8,128)(2,1)S(1)}, u32[]{:S(2)}, u32[]{:S(2)}) %collective-permute-start.43) | collective-permute-done | bytes 294944 | tf_op jit(solution)/shard_map/ppermute | solution.py:339
  182.6 1.7 collective-permute-start.44
  184.3 4.5 %collective-permute-done.37 = bf16[2,4,48,384]{3,2,1,0:T(8,128)(2,1)S(1)} collective-permute-done((bf16[2,4,48,384]{3,2,1,0:T(8,128)(2,1)S(1)}, bf16[2,4,48,384]{3,2,1,0:T(8,128)(2,1)S(1)}, u32[]{:S(2)}, u32[]{:S(2)}) %collective-permute-start.37) | collective-permute-done | bytes 294944 | tf_op jit(solution)/shard_map/ppermute | solution.py:339
  188.9 1.7 collective-permute-start.38
  190.6 3.7 %collective-permute-done.31 = bf16[2,4,48,384]{3,2,1,0:T(8,128)(2,1)S(1)} collective-permute-done((bf16[2,4,48,384]{3,2,1,0:T(8,128)(2,1)S(1)}, bf16[2,4,48,384]{3,2,1,0:T(8,128)(2,1)S(1)}, u32[]{:S(2)}, u32[]{:S(2)}) %collective-permute-start.31) | collective-permute-done | bytes 294944 | tf_op jit(solution)/shard_map/ppermute | solution.py:339
  194.4 1.7 collective-permute-start.32
  196.1 2.0 collective-permute-start.45
  200.4 2.9 %collective-permute-start.33 = (bf16[2,1,48,384]{3,2,0,1:T(8,128)(2,1)S(1)}, bf16[2,1,48,384]{3,2,0,1:T(8,128)(2,1)S(1)}, u32[]{:S(2)}, u32[]{:S(2)}) collective-permute-start(bf16[2,1,48,384]{3,2,0,1:T(8,128)(2,1)S(1)} %fusion.25), channel_id=1, source_target_pairs={{0,16},{4,20},{8,24},{12,28},{16,0},{20,4},{24,8},{28,12},{1,17},{... | collective-permute-start | bytes 221192 | tf_op jit(solution)/shard_map/ppermute | solution.py:339
  203.4 2.0 collective-permute-done.45
  205.5 1.6 collective-permute-start.46
  207.7 1.6 collective-permute-start.40
  210.2 2.0 collective-permute-done.40
  215.9 6.9 %adam.1 = (f32[48,4992]{1,0:T(8,128)}, f32[48,384]{1,0:T(8,128)}, f32[4,48,384]{2,1,0:T(8,128)}, f32[1,672]{1,0:T(1,128)}, f32[48,4992]{1,0:T(8,128)}, /*index=5...) custom-call(s32[2]{0:T(128)} %pad_add_fusion.place, ...), custom_call_target="tpu_custom_call" | custom-call | tf_op jit(solution)/shard_map/adam/pallas_call | solution.py:595
  (369 shorter events, 97.4 us)
Async XLA Ops:
  1.7 28.2 %collective-permute-start.18 = (bf16[1,48,384]{2,1,0:T(8,128)(2,1)S(1)}, bf16[1,48,384]{2,1,0:T(8,128)(2,1)S(1)}, u32[]{:S(2)}, u32[]{:S(2)}) collective-permute-start(bf16[1,48,384]{2,1,0:T(8,128)(2,1)S(1)} %get-tuple-element.88), channel_id=1, source_target_pairs={{0,16},{4,20},{8,24},{12,28},{16,0},{20,4},{24,8},{28,12},{1,17},{... | collective-permute-start | bytes 110600 | tf_op jit(solution)/shard_map/ppermute | solution.py:339
  7.0 24.5 %collective-permute-start.12 = (bf16[1,48,384]{2,1,0:T(8,128)(2,1)S(1)}, bf16[1,48,384]{2,1,0:T(8,128)(2,1)S(1)}, u32[]{:S(2)}, u32[]{:S(2)}) collective-permute-start(bf16[1,48,384]{2,1,0:T(8,128)(2,1)S(1)} %get-tuple-element.90), channel_id=1, source_target_pairs={{0,16},{4,20},{8,24},{12,28},{16,0},{20,4},{24,8},{28,12},{1,17},{... | collective-permute-start | bytes 110600 | tf_op jit(solution)/shard_map/ppermute | solution.py:339
  7.2 24.9 %collective-permute-start.6 = (bf16[1,48,384]{2,1,0:T(8,128)(2,1)S(1)}, bf16[1,48,384]{2,1,0:T(8,128)(2,1)S(1)}, u32[]{:S(2)}, u32[]{:S(2)}) collective-permute-start(bf16[1,48,384]{2,1,0:T(8,128)(2,1)S(1)} %get-tuple-element.92), channel_id=1, source_target_pairs={{0,16},{4,20},{8,24},{12,28},{16,0},{20,4},{24,8},{28,12},{1,17},{... | collective-permute-start | bytes 110600 | tf_op jit(solution)/shard_map/ppermute | solution.py:339
  25.0 127.8 %collective-permute-start.49 = (bf16[8,4,384]{2,1,0:T(4,128)(2,1)S(1)}, bf16[8,4,384]{2,1,0:T(4,128)(2,1)S(1)}, u32[]{:S(2)}, u32[]{:S(2)}) collective-permute-start(bf16[8,4,384]{2,1,0:T(4,128)(2,1)S(1)} %slice.604), channel_id=1, source_target_pairs={{0,2},{1,3},{2,0},{3,1},{4,6},{5,7},{6,4},{7,5},{8,10},{9,11},{10,... | collective-permute-start | bytes 73736 | tf_op jit(solution)/shard_map/ppermute | solution.py:339
  27.6 9.7 %collective-permute-start.3 = (f32[4,4,2304]{2,1,0:T(4,128)}, f32[4,4,2304]{2,1,0:T(4,128)}, u32[]{:S(2)}, u32[]{:S(2)}) collective-permute-start(f32[4,4,2304]{2,1,0:T(4,128)} %slice_bitcast_fusion.3), channel_id=1, source_target_pairs={{0,4},{4,0},{8,12},{12,8},{16,20},{20,16},{24,28},{28,24},{1,5},{5... | collective-permute-start | bytes 442376 | tf_op jit(solution)/shard_map/ppermute | solution.py:339
  32.1 7.1 %collective-permute-start.7 = (bf16[2,48,384]{2,1,0:T(8,128)(2,1)S(1)}, bf16[2,48,384]{2,1,0:T(8,128)(2,1)S(1)}, u32[]{:S(2)}, u32[]{:S(2)}) collective-permute-start(bf16[2,48,384]{2,1,0:T(8,128)(2,1)S(1)} %pad_maximum_fusion.7), channel_id=1, source_target_pairs={{0,8},{4,12},{8,0},{12,4},{16,24},{20,28},{24,16},{28,20},{1,9},{5... | collective-permute-start | bytes 221192 | tf_op jit(solution)/shard_map/ppermute | solution.py:339
  34.4 8.7 %collective-permute-start.20 = (bf16[4,48,384]{2,1,0:T(8,128)(2,1)S(1)}, bf16[4,48,384]{2,1,0:T(8,128)(2,1)S(1)}, u32[]{:S(2)}, u32[]{:S(2)}) collective-permute-start(bf16[4,48,384]{2,1,0:T(8,128)(2,1)S(1)} %pad_maximum_fusion.5), channel_id=1, source_target_pairs={{0,4},{4,0},{8,12},{12,8},{16,20},{20,16},{24,28},{28,24},{1,5},{5... | collective-permute-start | bytes 442376 | tf_op jit(solution)/shard_map/ppermute | solution.py:339
  36.0 8.5 %collective-permute-start.14 = (bf16[4,48,384]{2,1,0:T(8,128)(2,1)S(1)}, bf16[4,48,384]{2,1,0:T(8,128)(2,1)S(1)}, u32[]{:S(2)}, u32[]{:S(2)}) collective-permute-start(bf16[4,48,384]{2,1,0:T(8,128)(2,1)S(1)} %pad_maximum_fusion.4), channel_id=1, source_target_pairs={{0,4},{4,0},{8,12},{12,8},{16,20},{20,16},{24,28},{28,24},{1,5},{5... | collective-permute-start | bytes 442376 | tf_op jit(solution)/shard_map/ppermute | solution.py:339
  39.2 6.2 %collective-permute-start.8 = (bf16[4,48,384]{2,1,0:T(8,128)(2,1)S(1)}, bf16[4,48,384]{2,1,0:T(8,128)(2,1)S(1)}, u32[]{:S(2)}, u32[]{:S(2)}) collective-permute-start(bf16[4,48,384]{2,1,0:T(8,128)(2,1)S(1)} %pad_maximum_fusion.3), channel_id=1, source_target_pairs={{0,4},{4,0},{8,12},{12,8},{16,20},{20,16},{24,28},{28,24},{1,5},{5... | collective-permute-start | bytes 442376 | tf_op jit(solution)/shard_map/ppermute | solution.py:339
  42.7 5.2 %collective-permute-start.5 = (f32[1,4,2304]{2,1,0:T(4,128)S(1)}, f32[1,4,2304]{2,1,0:T(4,128)S(1)}, u32[]{:S(2)}, u32[]{:S(2)}) collective-permute-start(f32[1,4,2304]{2,1,0:T(4,128)S(1)} %slice_bitcast_fusion.14), channel_id=1, source_target_pairs={{0,16},{4,20},{8,24},{12,28},{16,0},{20,4},{24,8},{28,12},{1,17},{... | collective-permute-start | bytes 110600 | tf_op jit(solution)/shard_map/ppermute | solution.py:339
  43.9 11.8 %collective-permute-start.22 = (bf16[8,48,384]{2,1,0:T(8,128)(2,1)}, bf16[8,48,384]{2,1,0:T(8,128)(2,1)}, u32[]{:S(2)}, u32[]{:S(2)}) collective-permute-start(bf16[8,48,384]{2,1,0:T(8,128)(2,1)} %pad_maximum_fusion.2), channel_id=1, source_target_pairs={{0,2},{1,3},{2,0},{3,1},{4,6},{5,7},{6,4},{7,5},{8,10},{9,11},{10,... | collective-permute-start | bytes 884744 | tf_op jit(solution)/shard_map/ppermute | solution.py:339
  45.4 16.6 %collective-permute-start.16 = (bf16[8,48,384]{2,1,0:T(8,128)(2,1)}, bf16[8,48,384]{2,1,0:T(8,128)(2,1)}, u32[]{:S(2)}, u32[]{:S(2)}) collective-permute-start(bf16[8,48,384]{2,1,0:T(8,128)(2,1)} %pad_maximum_fusion.1), channel_id=1, source_target_pairs={{0,2},{1,3},{2,0},{3,1},{4,6},{5,7},{6,4},{7,5},{8,10},{9,11},{10,... | collective-permute-start | bytes 884744 | tf_op jit(solution)/shard_map/ppermute | solution.py:339
  47.9 21.0 %collective-permute-start.15 = (bf16[8,48,384]{2,1,0:T(8,128)(2,1)}, bf16[8,48,384]{2,1,0:T(8,128)(2,1)}, u32[]{:S(2)}, u32[]{:S(2)}) collective-permute-start(bf16[8,48,384]{2,1,0:T(8,128)(2,1)} %pad_maximum_fusion.1), channel_id=1, source_target_pairs={{0,1},{1,0},{2,3},{3,2},{4,5},{5,4},{6,7},{7,6},{8,9},{9,8},{10,11... | collective-permute-start | bytes 884744 | tf_op jit(solution)/shard_map/ppermute | solution.py:339
  48.8 20.0 %collective-permute-start.10 = (bf16[8,48,384]{2,1,0:T(8,128)(2,1)}, bf16[8,48,384]{2,1,0:T(8,128)(2,1)S(1)}, u32[]{:S(2)}, u32[]{:S(2)}) collective-permute-start(bf16[8,48,384]{2,1,0:T(8,128)(2,1)} %pad_maximum_fusion), channel_id=1, source_target_pairs={{0,2},{1,3},{2,0},{3,1},{4,6},{5,7},{6,4},{7,5},{8,10},{9,11},{10,... | collective-permute-start | bytes 884744 | tf_op jit(solution)/shard_map/ppermute | solution.py:339
  55.6 20.1 %collective-permute-start.9 = (bf16[8,48,384]{2,1,0:T(8,128)(2,1)}, bf16[8,48,384]{2,1,0:T(8,128)(2,1)S(1)}, u32[]{:S(2)}, u32[]{:S(2)}) collective-permute-start(bf16[8,48,384]{2,1,0:T(8,128)(2,1)} %pad_maximum_fusion), channel_id=1, source_target_pairs={{0,1},{1,0},{2,3},{3,2},{4,5},{5,4},{6,7},{7,6},{8,9},{9,8},{10,11... | collective-permute-start | bytes 884744 | tf_op jit(solution)/shard_map/ppermute | solution.py:339
  62.0 13.9 %collective-permute-start.23 = (bf16[8,48,384]{2,1,0:T(8,128)(2,1)}, bf16[8,48,384]{2,1,0:T(8,128)(2,1)S(1)}, u32[]{:S(2)}, u32[]{:S(2)}) collective-permute-start(bf16[8,48,384]{2,1,0:T(8,128)(2,1)} %collective-permute-done.22), channel_id=1, source_target_pairs={{0,1},{1,0},{2,3},{3,2},{4,5},{5,4},{6,7},{7,6},{8,9},{9,8},{10,11... | collective-permute-start | bytes 884744 | tf_op jit(solution)/shard_map/ppermute | solution.py:339
  68.8 23.4 %collective-permute-start.17 = (bf16[8,48,384]{2,1,0:T(8,128)(2,1)}, bf16[8,48,384]{2,1,0:T(8,128)(2,1)S(1)}, u32[]{:S(2)}, u32[]{:S(2)}) collective-permute-start(bf16[8,48,384]{2,1,0:T(8,128)(2,1)} %collective-permute-done.16), channel_id=1, source_target_pairs={{0,1},{1,0},{2,3},{3,2},{4,5},{5,4},{6,7},{7,6},{8,9},{9,8},{10,11... | collective-permute-start | bytes 884744 | tf_op jit(solution)/shard_map/ppermute | solution.py:339
  68.9 7.2 %collective-permute-start.11 = (bf16[8,48,384]{2,1,0:T(8,128)(2,1)S(1)}, bf16[8,48,384]{2,1,0:T(8,128)(2,1)S(1)}, u32[]{:S(2)}, u32[]{:S(2)}) collective-permute-start(bf16[8,48,384]{2,1,0:T(8,128)(2,1)S(1)} %collective-permute-done.10), channel_id=1, source_target_pairs={{0,1},{1,0},{2,3},{3,2},{4,5},{5,4},{6,7},{7,6},{8,9},{9,8},{10,11... | collective-permute-start | bytes 884744 | tf_op jit(solution)/shard_map/ppermute | solution.py:339
  146.3 7.1 %collective-permute-start.56 = (f32[5376]{0:T(1024)S(1)}, f32[5376]{0:T(1024)S(1)}, u32[]{:S(2)}, u32[]{:S(2)}) collective-permute-start(f32[5376]{0:T(1024)S(1)} %add.150), channel_id=1, source_target_pairs={{0,4},{4,0},{8,12},{12,8},{16,20},{20,16},{24,28},{28,24},{1,5},{5... | collective-permute-start | bytes 64520 | tf_op jit(solution)/shard_map/ppermute | solution.py:339
  155.6 15.5 %collective-permute-start.42 = (bf16[2,8,48,384]{3,2,1,0:T(8,128)(2,1)}, bf16[2,8,48,384]{3,2,1,0:T(8,128)(2,1)}, u32[]{:S(2)}, u32[]{:S(2)}) collective-permute-start(bf16[2,8,48,384]{3,2,1,0:T(8,128)(2,1)} %get-tuple-element.68), channel_id=1, source_target_pairs={{0,1},{1,0},{2,3},{3,2},{4,5},{5,4},{6,7},{7,6},{8,9},{9,8},{10,11... | collective-permute-start | bytes 1769480 | tf_op jit(solution)/shard_map/ppermute | solution.py:339
  155.7 18.1 %collective-permute-start.36 = (bf16[2,8,48,384]{3,2,1,0:T(8,128)(2,1)}, bf16[2,8,48,384]{3,2,1,0:T(8,128)(2,1)}, u32[]{:S(2)}, u32[]{:S(2)}) collective-permute-start(bf16[2,8,48,384]{3,2,1,0:T(8,128)(2,1)} %get-tuple-element.66), channel_id=1, source_target_pairs={{0,1},{1,0},{2,3},{3,2},{4,5},{5,4},{6,7},{7,6},{8,9},{9,8},{10,11... | collective-permute-start | bytes 1769480 | tf_op jit(solution)/shard_map/ppermute | solution.py:339
  156.2 19.8 %collective-permute-start.30 = (bf16[2,8,48,384]{3,2,1,0:T(8,128)(2,1)}, bf16[2,8,48,384]{3,2,1,0:T(8,128)(2,1)}, u32[]{:S(2)}, u32[]{:S(2)}) collective-permute-start(bf16[2,8,48,384]{3,2,1,0:T(8,128)(2,1)} %get-tuple-element.64), channel_id=1, source_target_pairs={{0,1},{1,0},{2,3},{3,2},{4,5},{5,4},{6,7},{7,6},{8,9},{9,8},{10,11... | collective-permute-start | bytes 1769480 | tf_op jit(solution)/shard_map/ppermute | solution.py:339
  162.8 6.8 %collective-permute-start.51 = (bf16[8,4,2304]{2,1,0:T(4,128)(2,1)S(1)}, bf16[8,4,2304]{2,1,0:T(4,128)(2,1)S(1)}, u32[]{:S(2)}, u32[]{:S(2)}) collective-permute-start(bf16[8,4,2304]{2,1,0:T(4,128)(2,1)S(1)} %get-tuple-element.101), channel_id=1, source_target_pairs={{0,1},{1,0},{2,3},{3,2},{4,5},{5,4},{6,7},{7,6},{8,9},{9,8},{10,11... | collective-permute-start | bytes 442376 | tf_op jit(solution)/shard_map/ppermute | solution.py:339
  172.5 9.9 %collective-permute-start.43 = (bf16[2,4,48,384]{3,2,1,0:T(8,128)(2,1)S(1)}, bf16[2,4,48,384]{3,2,1,0:T(8,128)(2,1)S(1)}, u32[]{:S(2)}, u32[]{:S(2)}) collective-permute-start(bf16[2,4,48,384]{3,2,1,0:T(8,128)(2,1)S(1)} %fusion.5), channel_id=1, source_target_pairs={{0,4},{4,0},{8,12},{12,8},{16,20},{20,16},{24,28},{28,24},{1,5},{5... | collective-permute-start | bytes 884744 | tf_op jit(solution)/shard_map/ppermute | solution.py:339
  175.1 13.6 %collective-permute-start.37 = (bf16[2,4,48,384]{3,2,1,0:T(8,128)(2,1)S(1)}, bf16[2,4,48,384]{3,2,1,0:T(8,128)(2,1)S(1)}, u32[]{:S(2)}, u32[]{:S(2)}) collective-permute-start(bf16[2,4,48,384]{3,2,1,0:T(8,128)(2,1)S(1)} %fusion.4), channel_id=1, source_target_pairs={{0,4},{4,0},{8,12},{12,8},{16,20},{20,16},{24,28},{28,24},{1,5},{5... | collective-permute-start | bytes 884744 | tf_op jit(solution)/shard_map/ppermute | solution.py:339
  177.2 17.1 %collective-permute-start.31 = (bf16[2,4,48,384]{3,2,1,0:T(8,128)(2,1)S(1)}, bf16[2,4,48,384]{3,2,1,0:T(8,128)(2,1)S(1)}, u32[]{:S(2)}, u32[]{:S(2)}) collective-permute-start(bf16[2,4,48,384]{3,2,1,0:T(8,128)(2,1)S(1)} %fusion.3), channel_id=1, source_target_pairs={{0,4},{4,0},{8,12},{12,8},{16,20},{20,16},{24,28},{28,24},{1,5},{5... | collective-permute-start | bytes 884744 | tf_op jit(solution)/shard_map/ppermute | solution.py:339
  182.6 13.5 %collective-permute-start.44 = (bf16[2,2,48,384]{3,2,0,1:T(8,128)(2,1)S(1)}, bf16[2,2,48,384]{3,2,0,1:T(8,128)(2,1)S(1)}, u32[]{:S(2)}, u32[]{:S(2)}) collective-permute-start(bf16[2,2,48,384]{3,2,0,1:T(8,128)(2,1)S(1)} %fusion.15), channel_id=1, source_target_pairs={{0,8},{4,12},{8,0},{12,4},{16,24},{20,28},{24,16},{28,20},{1,9},{5... | collective-permute-start | bytes 442376 | tf_op jit(solution)/shard_map/ppermute | solution.py:339
  188.9 9.3 %collective-permute-start.38 = (bf16[2,2,48,384]{3,2,0,1:T(8,128)(2,1)S(1)}, bf16[2,2,48,384]{3,2,0,1:T(8,128)(2,1)S(1)}, u32[]{:S(2)}, u32[]{:S(2)}) collective-permute-start(bf16[2,2,48,384]{3,2,0,1:T(8,128)(2,1)S(1)} %fusion.14), channel_id=1, source_target_pairs={{0,8},{4,12},{8,0},{12,4},{16,24},{20,28},{24,16},{28,20},{1,9},{5... | collective-permute-start | bytes 442376 | tf_op jit(solution)/shard_map/ppermute | solution.py:339
  194.4 6.0 %collective-permute-start.32 = (bf16[2,2,48,384]{3,2,0,1:T(8,128)(2,1)S(1)}, bf16[2,2,48,384]{3,2,0,1:T(8,128)(2,1)S(1)}, u32[]{:S(2)}, u32[]{:S(2)}) collective-permute-start(bf16[2,2,48,384]{3,2,0,1:T(8,128)(2,1)S(1)} %fusion.13), channel_id=1, source_target_pairs={{0,8},{4,12},{8,0},{12,4},{16,24},{20,28},{24,16},{28,20},{1,9},{5... | collective-permute-start | bytes 442376 | tf_op jit(solution)/shard_map/ppermute | solution.py:339
  196.1 9.3 %collective-permute-start.45 = (bf16[2,1,48,384]{3,2,0,1:T(8,128)(2,1)S(1)}, bf16[2,1,48,384]{3,2,0,1:T(8,128)(2,1)S(1)}, u32[]{:S(2)}, u32[]{:S(2)}) collective-permute-start(bf16[2,1,48,384]{3,2,0,1:T(8,128)(2,1)S(1)} %fusion.29), channel_id=1, source_target_pairs={{0,16},{4,20},{8,24},{12,28},{16,0},{20,4},{24,8},{28,12},{1,17},{... | collective-permute-start | bytes 221192 | tf_op jit(solution)/shard_map/ppermute | solution.py:339
  198.2 9.5 %collective-permute-start.39 = (bf16[2,1,48,384]{3,2,0,1:T(8,128)(2,1)S(1)}, bf16[2,1,48,384]{3,2,0,1:T(8,128)(2,1)S(1)}, u32[]{:S(2)}, u32[]{:S(2)}) collective-permute-start(bf16[2,1,48,384]{3,2,0,1:T(8,128)(2,1)S(1)} %fusion.27), channel_id=1, source_target_pairs={{0,16},{4,20},{8,24},{12,28},{16,0},{20,4},{24,8},{28,12},{1,17},{... | collective-permute-start | bytes 221192 | tf_op jit(solution)/shard_map/ppermute | solution.py:339
  200.4 8.9 %collective-permute-start.33 = (bf16[2,1,48,384]{3,2,0,1:T(8,128)(2,1)S(1)}, bf16[2,1,48,384]{3,2,0,1:T(8,128)(2,1)S(1)}, u32[]{:S(2)}, u32[]{:S(2)}) collective-permute-start(bf16[2,1,48,384]{3,2,0,1:T(8,128)(2,1)S(1)} %fusion.25), channel_id=1, source_target_pairs={{0,16},{4,20},{8,24},{12,28},{16,0},{20,4},{24,8},{28,12},{1,17},{... | collective-permute-start | bytes 221192 | tf_op jit(solution)/shard_map/ppermute | solution.py:339
  (55 other events, 356.7 us)
where the time goes:
time: 231 us; the launch traced here: 228 us
  Pallas kernels  62.6 us (27%)
  starting transfers between devices  62 us (27%)
  waiting for transfers between devices  43.7 us (19%)
  local copies, waits for them, and re-layouts  36.6 us (16%)
  other arithmetic  18.7 us (8%)
  matrix products  2.5 us (1%)
    ppermute x59, starting transfers between devices, swap(): return lax.ppermute(value, axis, [(i, i ^ bit) for i in range(size)])  62 us
    pallas_call x3, Pallas kernels, call(): pl.pallas_call(kernel, grid_spec=pltpu.PrefetchScalarGridSpec(num_scalar_...  55.7 us
    ppermute x59, waiting for transfers between devices, swap(): return lax.ppermute(value, axis, [(i, i ^ bit) for i in range(size)])  43.7 us
    unnamed x157, local copies, waits for them, and re-layouts  26.4 us
    pallas_call x1, Pallas kernels, body(): pl.pallas_call(adam_kernel, grid_spec=pltpu.PrefetchScalarGridSpec(num_sc...  6.87 us
    pallas_call x4, other arithmetic, body(): pl.pallas_call(adam_kernel, grid_spec=pltpu.PrefetchScalarGridSpec(num_sc...  5.13 us
  transfers between devices with their start and end apart: 59, of which 23 were waited for; matrix products, arithmetic and copies ran while one was open for 22% of the time, Pallas kernels for 24%

commit v1 on v0

--- a/solution.py
+++ b/solution.py
@@ -57,6 +57,10 @@
     return jnp.concatenate([jnp.cos(angles), jnp.sin(angles)], axis=1)
 
 
+def spot_of(relative, owners):
+    return (relative & 1) * (owners // 2) + (relative >> 1)
+
+
 def unpack_columns(place, pieces, whole):
     owners, rows, width = pieces[0].shape
     me, mine = place[0], place[1]
@@ -67,7 +71,7 @@
             def _():
                 for owner in range(owners):
                     whole[owner * rows : (owner + 1) * rows, block * width : (block + 1) * width] = (
-                        pieces[k][owner ^ me]
+                        pieces[k][spot_of(owner ^ me, owners)]
                     )
 
 
@@ -81,21 +85,21 @@
             def _():
                 for owner in range(owners):
                     start = (owner * GROUP + block) * rows
-                    whole[start : start + rows, :] = pieces[k][owner ^ me]
+                    whole[start : start + rows, :] = pieces[k][spot_of(owner ^ me, owners)]
 
 
 def pack_block(place, block, owner, value, keep, send):
     k = place[1] ^ block
-    spot = place[0] ^ owner
+    spot = spot_of(place[0] ^ owner, keep.shape[0])
     half = k >> 1
 
     @pl.when((k & 1) == 0)
     def _():
-        keep[half, spot] = value
+        keep[spot, half] = value
 
     @pl.when((k & 1) == 1)
     def _():
-        send[half, spot] = value.astype(bf16)
+        send[spot, half] = value.astype(bf16)
 
 
 def lane_masks():
@@ -206,7 +210,7 @@
 
     @pl.when(step == pl.num_programs(0) - 1)
     def _():
-        owners, rows = upk_o.shape[1], upk_o.shape[2]
+        owners, rows = upk_o.shape[0], upk_o.shape[2]
         for block in range(GROUP):
             for owner in range(owners):
                 value = acc_up[owner * rows : (owner + 1) * rows, block * width : (block + 1) * width]
@@ -218,19 +222,25 @@
                 pack_block(place, block, owner, whole_down[start : start + rows, :], dnk_o, dns_o)
 
 
-def attn_backward(
-    place, lat, dmid, qkv, lse, mod, gattn, p0, p1, p2, p3,
-    glat_o, dmod_o, gbias_o, keep_o, send_o,
-    whole, dq_t, dproj, acc,
-):
+def attn_backward(first, last, place, lat, dmid, qkv, lse, mod, p0, p1, p2, p3, *refs):
+    refs = list(refs)
+    if not first:
+        acc_i, gbias_i = refs.pop(0), refs.pop(0)
+    if last:
+        gattn = refs.pop(0)
+    glat_o, dmod_o, gbias_o = refs.pop(0), refs.pop(0), refs.pop(0)
+    if last:
+        keep_o, send_o, whole, dq_t, dproj, acc = refs
+    else:
+        acc, whole, dq_t, dproj = refs
     width = lat.shape[-1]
     step = pl.program_id(0)
 
     @pl.when(step == 0)
     def _():
         unpack_columns(place, (p0, p1, p2, p3), whole)
-        acc[...] = jnp.zeros_like(acc)
-        gbias_o[...] = jnp.zeros_like(gbias_o)
+        acc[...] = jnp.zeros_like(acc) if first else acc_i[...]
+        gbias_o[...] = jnp.zeros_like(gbias_o) if first else gbias_i[...]
 
     shift_a, scale_a, gate_a = mod[0, 0:1], mod[0, 1:2], mod[0, 2:3]
     normed, inv_std = layer_norm(lat[0].astype(f32))
@@ -276,17 +286,19 @@
     dmod_o[0, 0:1] = token_sum(d_input)
     glat_o[0] = d_middle + norm_back(d_input * (1.0 + scale_a), normed, inv_std)
 
-    @pl.when(step == pl.num_programs(0) - 1)
-    def _():
-        owners, rows = keep_o.shape[1], keep_o.shape[2]
-        for block in range(GROUP):
-            for owner in range(owners):
-                span = slice(owner * rows, (owner + 1) * rows)
-                if block < GROUP - 1:
-                    value = acc[span, block * width : (block + 1) * width]
-                else:
-                    value = gattn[span, :]
-                pack_block(place, block, owner, value, keep_o, send_o)
+    if last:
+
+        @pl.when(step == pl.num_programs(0) - 1)
+        def _():
+            owners, rows = keep_o.shape[0], keep_o.shape[2]
+            for block in range(GROUP):
+                for owner in range(owners):
+                    span = slice(owner * rows, (owner + 1) * rows)
+                    if block < GROUP - 1:
+                        value = acc[span, block * width : (block + 1) * width]
+                    else:
+                        value = gattn[span, :]
+                    pack_block(place, block, owner, value, keep_o, send_o)
 
 
 def adam_parts(weight, moment, second, gradient):
@@ -301,10 +313,10 @@
 
 
 def adam_kernel(place, *refs):
-    (att0, att1, up0, up1, dn0, dn1, gmod, gbias) = refs[:8]
-    weights, means, squares = refs[8:12], refs[12:16], refs[16:20]
-    grads, new_w, new_m, new_s = refs[20:24], refs[24:28], refs[28:32], refs[32:36]
-    width = att0.shape[-1]
+    att, up, down, gmod = refs[0:4], refs[4:8], refs[8:12], refs[12]
+    weights, means, squares = refs[13:16], refs[16:19], refs[19:22]
+    grads, new_w, new_m, new_s = refs[22:25], refs[25:28], refs[28:31], refs[31:34]
+    width = att[0].shape[-1]
 
     def write(which, where, gradient):
         grads[which][where] = gradient
@@ -313,25 +325,25 @@
         )
         new_w[which][where], new_m[which][where], new_s[which][where] = result
 
-    def block_of(same, other, block):
+    def block_of(parts, block):
         k = place[1] ^ block
-        mine = jnp.where((k & 2) == 0, same[0], same[1])
-        theirs = jnp.where((k & 2) == 0, other[0], other[1])
-        return jnp.where((k & 1) == 0, mine, theirs)
+        half = k >> 1
+        near = parts[0][half].astype(f32) + parts[1][1 - half].astype(f32)
+        far = parts[2][half].astype(f32) + parts[3][1 - half].astype(f32)
+        return jnp.where((k & 1) == 0, near, far)
 
     everything = slice(None)
     for block in range(GROUP):
-        g_att = block_of(att0, att1, block)
+        g_att = block_of(att, block)
         if block < GROUP - 1:
             write(0, (everything, slice(block * width, (block + 1) * width)), g_att)
         else:
             write(1, (everything, everything), g_att)
         at = (GROUP - 1 + block) * width
-        write(0, (everything, slice(at, at + width)), block_of(up0, up1, block))
-        write(2, (block,), block_of(dn0, dn1, block))
+        write(0, (everything, slice(at, at + width)), block_of(up, block))
+        write(2, (block,), block_of(down, block))
     at = (2 * GROUP - 1) * width
     write(0, (everything, slice(at, at + gmod.shape[1])), gmod[...])
-    write(3, (everything, everything), gbias[...])
 
 
 def swap(value, axis, bit):
@@ -339,24 +351,22 @@
     return lax.ppermute(value, axis, [(i, i ^ bit) for i in range(size)])
 
 
-def gather_bits(size):
-    bits = [1 << b for b in range(size.bit_length() - 1)]
-    return bits[1:][::-1] + bits[:1]
+def upper_stages(owners):
+    half = owners // 2
+    if half <= 4:
+        return [list(range(1, half))]
+    return [[1 << b] for b in range(half.bit_length() - 1)]
+
+
+def gather_upper(held):
+    for stage in upper_stages(lax.axis_size("dp")):
+        held = jnp.concatenate([held] + [swap(held, "dp", 2 * c) for c in stage], axis=0)
+    return held
 
 
 def dp_gather(value):
-    owners = lax.axis_size("dp")
-    bits = gather_bits(owners)
-    held, order = value[None], [0]
-    for bit in bits:
-        held = jnp.concatenate([held, swap(held, "dp", bit)], axis=0)
-        order = order + [o ^ bit for o in order]
-    spots = [order.index(i) for i in range(owners)]
-    return held, spots
-
-
-def reorder(held, spots):
-    return jnp.concatenate([held[s : s + 1] for s in spots], axis=0)
+    held = gather_upper(value[None])
+    return jnp.concatenate([held, swap(held, "dp", 1)], axis=0)
 
 
 def group_gather(value):
@@ -366,26 +376,27 @@
     return value, one, two, three
 
 
-def dp_scatter(keep, axis, compress):
-    owners = lax.axis_size("dp")
-    for bit in [1 << b for b in range(owners.bit_length() - 1)]:
-        shape = keep.shape
-        pairs = keep.reshape(shape[:axis] + (shape[axis] // 2, 2) + shape[axis + 1 :])
-        mine = lax.index_in_dim(pairs, 0, axis + 1, keepdims=False)
-        theirs = lax.index_in_dim(pairs, 1, axis + 1, keepdims=False)
-        if compress:
-            theirs = theirs.astype(bf16)
-        keep = mine + swap(theirs, "dp", bit).astype(f32)
-    return lax.index_in_dim(keep, 0, axis, keepdims=False)
-
-
-def reduce_blocks(keep, send):
-    keep = keep + swap(send, "group", 1).astype(f32)
-    keep = dp_scatter(keep, 1, True)
-    sent = keep.astype(bf16)
-    received = swap(sent[::-1], "group", 2)
-    own = sent.astype(f32) + received.astype(f32)
-    return own, swap(own, "group", 1)
+def scatter_near(keep, dtype):
+    half = keep.shape[0] // 2
+    return keep[:half] + swap(keep[half:].astype(dtype), "dp", 1).astype(f32)
+
+
+def scatter_upper(keep, dtype):
+    for stage in upper_stages(lax.axis_size("dp")):
+        if len(stage) == keep.shape[0] - 1:
+            total = keep[0]
+            for c in stage:
+                total = total + swap(keep[c].astype(dtype), "dp", 2 * c).astype(f32)
+            return total
+        bit = stage[0]
+        pairs = keep.reshape((keep.shape[0] // 2, 2) + keep.shape[1:])
+        keep = pairs[:, 0] + swap(pairs[:, 1].astype(dtype), "dp", 2 * bit).astype(f32)
+    return keep[0]
+
+
+def share_parts(total):
+    sent = total.astype(bf16)
+    return [sent] + [swap(sent, "group", k) for k in (2, 1, 3)]
 
 
 def sum_all(value):
@@ -413,9 +424,14 @@
     return pl.BlockSpec((1,) + tuple(array.shape[1:]), lambda l, *_: (l,) + zeros)
 
 
-def call(kernel, place, latent_args, whole_args, latent_outs, whole_outs, scratch, grid, flip=False):
-    ins = [latent_spec(a) for a in latent_args] + [whole_spec(a) for a in whole_args]
+def call(kernel, place, latent_args, whole_args, latent_outs, whole_outs, scratch, grid, start=0, us=15):
+    def shifted(array):
+        zeros = (0,) * (len(array.shape) - 1)
+        return pl.BlockSpec((1,) + tuple(array.shape[1:]), lambda l, *_: (l + start,) + zeros)
+
+    ins = [shifted(a) for a in latent_args] + [whole_spec(a) for a in whole_args]
     outs = [latent_spec(a) for a in latent_outs] + [whole_spec(a) for a in whole_outs]
+    func = kernel.func if isinstance(kernel, functools.partial) else kernel
     return pl.pallas_call(
         kernel,
         grid_spec=pltpu.PrefetchScalarGridSpec(
@@ -427,7 +443,10 @@
         ),
         out_shape=list(latent_outs) + list(whole_outs),
         compiler_params=compiler(),
-        name=kernel.__name__,
+        cost_estimate=pl.CostEstimate(
+            flops=int(us * 1e9), bytes_accessed=int(us * 1e6), transcendentals=0
+        ),
+        name=func.__name__,
     )(place, *latent_args, *whole_args)
 
 
@@ -450,42 +469,38 @@
     mine = lax.axis_index("group")
     place = jnp.stack([me, mine]).astype(jnp.int32)
 
+    bias_shard = biases.shape[0]
+    message = jnp.concatenate([timestep.astype(f32), labels.astype(f32), biases])
+    small = dp_gather(message)
+    times_rel = small[:, :count].reshape(-1)
+    labels_rel = small[:, count : 2 * count].reshape(-1).astype(jnp.int32)
+    absolute = spot_of(jnp.arange(owners, dtype=jnp.int32) ^ me, owners)
+    bias_all = (
+        jnp.take(small[:, 2 * count :], absolute, axis=0).reshape(1, -1).astype(bf16).astype(f32)
+    )
     class_count = class_table.shape[0]
-    one_hot = (labels[:, None] == jnp.arange(class_count, dtype=jnp.int32)[None, :]).astype(bf16)
-    condition = time_embed(timestep, width) + dot(one_hot, class_table)
-    sigmoid_c = jax.nn.sigmoid(condition)
-    cond_act = (condition * sigmoid_c).astype(bf16)
-    bias_shard = biases.shape[0]
-    bias_rows = -(-bias_shard // width)
-    bias_b = jnp.pad(biases.astype(bf16), (0, bias_rows * width - bias_shard)).reshape(-1, width)
-    small, spots = dp_gather(jnp.concatenate([cond_act, bias_b], axis=0))
-    small = reorder(small, spots)
-    cond_rel = small[:, :count]
-    bias_rel = small[:, count:].reshape(owners, -1)[:, :bias_shard]
-    absolute = jnp.arange(owners, dtype=jnp.int32) ^ me
-    bias_all = jnp.take(bias_rel, absolute, axis=0).reshape(1, -1).astype(f32)
+    one_hot = (labels_rel[:, None] == jnp.arange(class_count, dtype=jnp.int32)[None, :]).astype(bf16)
+    condition = time_embed(times_rel, width) + dot(one_hot, class_table)
+    cond_rel = (condition * jax.nn.sigmoid(condition)).astype(bf16)
     mod_at = 3 * width + hidden
     w_mod = input_proj[:, mod_at:].astype(bf16)
-    cond_cols = lax.dynamic_slice_in_dim(cond_rel.reshape(owners * count, width), me * rows, rows, 1)
+    cond_cols = lax.dynamic_slice_in_dim(cond_rel, me * rows, rows, 1)
     partial = dot(cond_cols, w_mod).reshape(owners, count, -1)
     bias_mod_at = 4 * width + hidden
-    modulation = dp_scatter(partial, 0, False) + bias_all[:, bias_mod_at:]
+    modulation = scatter_upper(scatter_near(partial, f32), f32) + bias_all[:, bias_mod_at:]
     mod = modulation.reshape(count, 6, width)
 
-    att_blocks = jnp.stack(
-        [input_proj[:, b * width : (b + 1) * width] for b in range(3)] + [attn_proj]
-    )
-    up_blocks = jnp.stack(
-        [input_proj[:, (3 + b) * width : (4 + b) * width] for b in range(hidden // width)]
-    )
-    down_blocks = mlp_down.reshape(GROUP, rows, width)
-
-    def pick(blocks):
-        return lax.dynamic_index_in_dim(blocks, mine, 0, keepdims=False).astype(bf16)
+    att_blocks = [input_proj[:, b * width : (b + 1) * width] for b in range(3)] + [attn_proj]
+    up_blocks = [input_proj[:, (3 + b) * width : (4 + b) * width] for b in range(GROUP)]
+    down_blocks = [mlp_down[b * rows : (b + 1) * rows] for b in range(GROUP)]
 
     def weights_of(blocks):
-        held, spots = dp_gather(pick(blocks))
-        return [reorder(part, spots) for part in group_gather(held)]
+        chosen = jnp.where(
+            mine < 2,
+            jnp.where(mine == 0, blocks[0], blocks[1]),
+            jnp.where(mine == 2, blocks[2], blocks[3]),
+        ).astype(bf16)
+        return list(group_gather(dp_gather(chosen)))
 
     att_parts = weights_of(att_blocks)
     up_parts = weights_of(up_blocks)
@@ -504,8 +519,8 @@
         [pltpu.VMEM((width, 4 * width), bf16), pltpu.VMEM((width, seq_len), f32)],
         count,
     )
-    kept = like((2, owners, rows, width), f32)
-    sent = like((2, owners, rows, width), bf16)
+    kept = like((owners, 2, rows, width), f32)
+    sent = like((owners, 2, rows, width), bf16)
     bias_like = like((1, bias_mod_at), f32)
     block_out, d_middle, d_mod_m, g_attn, g_bias_m, up_keep, up_send, dn_keep, dn_send = call(
         mlp_both, place,
@@ -526,21 +541,45 @@
             pltpu.VMEM((width, hidden), f32),
         ],
         count,
-    )
-    grad_latents, d_mod_a, g_bias_a, at_keep, at_send = call(
-        attn_backward, place,
-        [latents, d_middle, qkv, lse, mod], [g_attn] + att_parts,
-        [like((count, seq_len, width), f32), like((count, 2, width), f32)],
-        [like((1, 2 * width), f32), kept, sent],
-        [
-            pltpu.VMEM((width, 4 * width), bf16),
-            pltpu.VMEM((width, seq_len), f32),
-            pltpu.VMEM((seq_len, 3 * width), bf16),
-            pltpu.VMEM((width, 3 * width), f32),
-        ],
-        count,
-    )
-
+        us=20,
+    )
+    up_keep = up_keep + swap(up_send, "group", 1).astype(f32)
+    dn_keep = dn_keep + swap(dn_send, "group", 1).astype(f32)
+    d_middle, up_keep, dn_keep = lax.optimization_barrier((d_middle, up_keep, dn_keep))
+
+    half = count // 2
+    token_like = like((half, seq_len, width), f32)
+    mod_like = like((half, 2, width), f32)
+    gb_like = like((1, 2 * width), f32)
+    acc_like = like((width, 3 * width), f32)
+    scratch = [
+        pltpu.VMEM((width, 4 * width), bf16),
+        pltpu.VMEM((width, seq_len), f32),
+        pltpu.VMEM((seq_len, 3 * width), bf16),
+    ]
+    token_args = [latents, d_middle, qkv, lse, mod]
+    glat_0, d_mod_0, g_bias_a, acc = call(
+        functools.partial(attn_backward, True, False), place,
+        token_args, att_parts,
+        [token_like, mod_like], [gb_like, acc_like], scratch, half, 0, 10,
+    )
+    up_keep = scatter_near(up_keep, bf16)
+    dn_keep = scatter_near(dn_keep, bf16)
+    acc, up_keep, dn_keep = lax.optimization_barrier((acc, up_keep, dn_keep))
+    glat_1, d_mod_1, g_bias_a, at_keep, at_send = call(
+        functools.partial(attn_backward, False, True), place,
+        token_args, att_parts + [acc, g_bias_a, g_attn],
+        [token_like, mod_like], [gb_like, kept, sent],
+        scratch + [pltpu.VMEM((width, 3 * width), f32)], count - half, half, 10,
+    )
+    up_total = scatter_upper(up_keep, bf16)
+    dn_total = scatter_upper(dn_keep, bf16)
+    at_send, up_total, dn_total = lax.optimization_barrier((at_send, up_total, dn_total))
+    at_keep = at_keep + swap(at_send, "group", 1).astype(f32)
+    at_total = scatter_upper(scatter_near(at_keep, bf16), bf16)
+    grad_latents = jnp.concatenate([glat_0, glat_1], axis=0)
+
+    d_mod_a = jnp.concatenate([d_mod_0, d_mod_1], axis=0)
     d_modulation = jnp.concatenate([d_mod_a, d_mod_m[:, 2:]], axis=1).reshape(count, 6 * width)
     d_modulation_b = d_modulation.astype(bf16)
     bias_grad = jnp.concatenate(
@@ -550,48 +589,43 @@
             jnp.sum(d_modulation, axis=0),
         ]
     )
-    dm_rel = reorder(*dp_gather(d_modulation_b))
-    dm_parts = group_gather(dm_rel)
-    cond_parts = group_gather(cond_rel)
-    dm_all = jnp.concatenate(dm_parts, axis=0).reshape(-1, 6 * width)
-    cond_all = jnp.concatenate(cond_parts, axis=0).reshape(-1, width)
-    g_mod = dot(lax.dynamic_slice_in_dim(cond_all, me * rows, rows, 1), dm_all, TN)
-
-    back = dot(dm_rel.reshape(owners * count, 6 * width), w_mod, NT).reshape(owners, count, rows)
-    for bit in [1 << b for b in range(owners.bit_length() - 1)]:
-        shaped = back.reshape(owners // (2 * bit), 2, bit, count, rows)
-        received = swap(shaped[:, 1], "dp", bit)
-        back = jnp.stack([shaped[:, 0], received], axis=1).reshape(owners, count, rows)
+    dm_rel = dp_gather(d_modulation_b).reshape(owners * count, 6 * width)
+    dm_all = jnp.concatenate(group_gather(dm_rel), axis=0)
+    cond_all = jnp.concatenate(group_gather(cond_cols), axis=0)
+    g_mod = dot(cond_all, dm_all, TN)
+
+    back = dp_gather(dot(dm_rel, w_mod, NT))
+    back = back.reshape(owners, owners, count, rows)
+    back = jnp.stack([back[s, s] for s in range(owners)])
     back = jnp.take(back, absolute, axis=0)
     d_cond = back.transpose(1, 0, 2).reshape(count, width)
-    grad_cond = d_cond * (sigmoid_c * (1.0 + condition * (1.0 - sigmoid_c)))
-
-    up_own, up_other = reduce_blocks(up_keep, up_send)
-    dn_own, dn_other = reduce_blocks(dn_keep, dn_send)
-    at_own, at_other = reduce_blocks(at_keep, at_send)
-    bias_sum = lax.dynamic_slice_in_dim(sum_all(bias_grad), me * bias_shard, bias_shard, 0)
+    own_cond = condition[:count]
+    own_sig = jax.nn.sigmoid(own_cond)
+    grad_cond = d_cond * (own_sig * (1.0 + own_cond * (1.0 - own_sig)))
+
+    parts = share_parts(at_total) + share_parts(up_total) + share_parts(dn_total)
+    g_biases = lax.dynamic_slice_in_dim(sum_all(bias_grad), me * bias_shard, bias_shard, 0)
+    bias_out = (g_biases,) + adam_parts(biases, mean_biases, sq_biases, g_biases)
 
     steps = rows // 16 if rows % 16 == 0 else 1
     block_rows = rows // steps
 
     def spec_of(array):
-        if array.ndim == 3:
+        if len(array.shape) == 3:
             return pl.BlockSpec((array.shape[0], block_rows, width), lambda s, *_: (0, s, 0))
-        if array.shape[0] == 1:
-            return pl.BlockSpec(tuple(array.shape), lambda s, *_: (0, 0))
         return pl.BlockSpec((block_rows, array.shape[1]), lambda s, *_: (s, 0))
 
-    def shaped(four):
-        return [four[0], four[1], four[2].reshape(GROUP, rows, width), four[3].reshape(1, -1)]
-
-    state = (
-        shaped((input_proj, attn_proj, mlp_down, biases))
-        + shaped((mean_input, mean_attn, mean_down, mean_biases))
-        + shaped((sq_input, sq_attn, sq_down, sq_biases))
-    )
-    args = [at_own, at_other, up_own, up_other, dn_own, dn_other, g_mod, bias_sum.reshape(1, -1)]
-    args = args + state
-    results = [like(a.shape, f32) for a in state[:4]] * 4
+    state = [
+        entry
+        for three in (
+            (input_proj, attn_proj, mlp_down),
+            (mean_input, mean_attn, mean_down),
+            (sq_input, sq_attn, sq_down),
+        )
+        for entry in (three[0], three[1], three[2].reshape(GROUP, rows, width))
+    ]
+    args = parts + [g_mod] + state
+    results = [like(a.shape, f32) for a in state[:3]] * 4
     outs = pl.pallas_call(
         adam_kernel,
         grid_spec=pltpu.PrefetchScalarGridSpec(
@@ -605,13 +639,11 @@
         name="adam",
     )(place, *args)
 
-    def flat(four):
-        return (four[0], four[1], four[2].reshape(mlp_down.shape), four[3].reshape(-1))
-
-    return (
-        (block_out, grad_latents, grad_cond)
-        + flat(outs[:4]) + flat(outs[4:8]) + flat(outs[8:12]) + flat(outs[12:16])
-    )
+    def flat(index):
+        three = outs[3 * index : 3 * index + 3]
+        return (three[0], three[1], three[2].reshape(mlp_down.shape), bias_out[index])
+
+    return (block_out, grad_latents, grad_cond) + flat(0) + flat(1) + flat(2) + flat(3)
 
 
 def solution(mesh):

time: 231 us -> 219 us (0.948)
  local copies, waits for them, and re-layouts: 36.6 us -> 15.8 us
  starting transfers between devices: 62 us -> 70.3 us
  Pallas kernels: 62.6 us -> 67.1 us
  other arithmetic: 18.7 us -> 16 us
    unnamed x157 -> x90, local copies, waits for them, and re-layouts: 26.4 us -> 7.39 us
    ppermute x59 -> x72, starting transfers between devices: 62 us -> 70.3 us  [swap(): return lax.ppermute(value, axis, [(i, i ^ bit) for i in range(size)])]
    pallas_call x4 -> x0, other arithmetic: 5.13 us -> none  [body(): pl.pallas_call(adam_kernel, grid_spec=pltpu.PrefetchScalarGridSpec(num_sc...]
    pallas_call x3 -> x4, Pallas kernels: 55.7 us -> 60.2 us  [call(): pl.pallas_call(kernel, grid_spec=pltpu.PrefetchScalarGridSpec(num_scalar_...]
    unnamed x4 -> x2, other arithmetic: 0.12 us -> 3.42 us
    concatenate x14 -> x5, local copies, waits for them, and re-layouts: 3.29 us -> 0.81 us  [dp_gather(): return jnp.concatenate([held, swap(held, 'dp', 1)], axis=0)]
    add x12 -> x9, other arithmetic: 5.52 us -> 3.39 us  [the longest x1 1.52 us: body(): at_keep = at_keep + swap(at_send, 'group', 1).astype(f32)]
    ppermute x59 -> x72, waiting for transfers between devices: 43.7 us -> 44.3 us  [swap(): return lax.ppermute(value, axis, [(i, i ^ bit) for i in range(size)])]
  transfers between devices with their start and end apart: 59 -> 72, of which waited for: 23 -> 20; matrix products, arithmetic and copies ran while one was open for 22% -> 12% of each run, Pallas kernels for 24% -> 12%
where the time goes in v1:
time: 219 us; the launch traced here: 218 us
  starting transfers between devices  70.3 us (32%)
  Pallas kernels  67.1 us (31%)
  waiting for transfers between devices  44.3 us (20%)
  other arithmetic  16 us (7%)
  local copies, waits for them, and re-layouts  15.8 us (7%)
  matrix products  2.6 us (1%)
    ppermute x72, starting transfers between devices, swap(): return lax.ppermute(value, axis, [(i, i ^ bit) for i in range(size)])  70.3 us
    pallas_call x4, Pallas kernels, call(): pl.pallas_call(kernel, grid_spec=pltpu.PrefetchScalarGridSpec(num_scalar_...  60.2 us
    ppermute x72, waiting for transfers between devices, swap(): return lax.ppermute(value, axis, [(i, i ^ bit) for i in range(size)])  44.3 us
    unnamed x90, local copies, waits for them, and re-layouts  7.39 us
    pallas_call x1, Pallas kernels, body(): pl.pallas_call(adam_kernel, grid_spec=pltpu.PrefetchScalarGridSpec(num_sc...  6.89 us
  transfers between devices with their start and end apart: 72, of which 20 were waited for; matrix products, arithmetic and copies ran while one was open for 12% of the time, Pallas kernels for 12%

profile of v1, /device:TPU:0, one launch (start us, length us, event | category | flops | bytes accessed | tf_op | source)
XLA Modules:
  0.0 217.9 jit_solution(13908258070676927557)
XLA Ops:
  2.9 3.1 %collective-permute-start = (f32[1,680]{1,0:T(1,128)S(1)}, f32[1,680]{1,0:T(1,128)S(1)}, u32[]{:S(2)}, u32[]{:S(2)}) collective-permute-start(f32[1,680]{1,0:T(1,128)S(1)} %broadcast_in_dim.39), channel_id=1, source_target_pairs={{0,8},{4,12},{8,0},{12,4},{16,24},{20,28},{24,16},{28,20},{1,9},{5... | collective-permute-start | bytes 8168 | tf_op jit(solution)/shard_map/ppermute | solution.py:351
  5.9 2.6 %collective-permute-start.1 = (f32[1,680]{1,0:T(1,128)S(1)}, f32[1,680]{1,0:T(1,128)S(1)}, u32[]{:S(2)}, u32[]{:S(2)}) collective-permute-start(f32[1,680]{1,0:T(1,128)S(1)} %broadcast_in_dim.39), channel_id=1, source_target_pairs={{0,16},{4,20},{8,24},{12,28},{16,0},{20,4},{24,8},{28,12},{1,17},{... | collective-permute-start | bytes 8168 | tf_op jit(solution)/shard_map/ppermute | solution.py:351
  8.5 1.8 constant_dynamic-update-slice_fusion.9
  10.3 3.8 %collective-permute-start.10 = (bf16[1,48,384]{2,1,0:T(8,128)(2,1)S(1)}, bf16[1,48,384]{2,1,0:T(8,128)(2,1)S(1)}, u32[]{:S(2)}, u32[]{:S(2)}) collective-permute-start(bf16[1,48,384]{2,1,0:T(8,128)(2,1)S(1)} %get-tuple-element.118), channel_id=1, source_target_pairs={{0,24},{4,28},{8,16},{12,20},{16,8},{20,12},{24,0},{28,4},{1,25},{... | collective-permute-start | bytes 110600 | tf_op jit(solution)/shard_map/ppermute | solution.py:351
  21.8 2.8 %collective-permute-start.16 = (bf16[1,48,384]{2,1,0:T(8,128)(2,1)S(1)}, bf16[1,48,384]{2,1,0:T(8,128)(2,1)S(1)}, u32[]{:S(2)}, u32[]{:S(2)}) collective-permute-start(bf16[1,48,384]{2,1,0:T(8,128)(2,1)S(1)} %get-tuple-element.114), channel_id=1, source_target_pairs={{0,16},{4,20},{8,24},{12,28},{16,0},{20,4},{24,8},{28,12},{1,17},{... | collective-permute-start | bytes 110600 | tf_op jit(solution)/shard_map/ppermute | solution.py:351
  27.5 3.7 %collective-permute-start.23 = (bf16[1,48,384]{2,1,0:T(8,128)(2,1)S(1)}, bf16[1,48,384]{2,1,0:T(8,128)(2,1)S(1)}, u32[]{:S(2)}, u32[]{:S(2)}) collective-permute-start(bf16[1,48,384]{2,1,0:T(8,128)(2,1)S(1)} %get-tuple-element.112), channel_id=1, source_target_pairs={{0,16},{4,20},{8,24},{12,28},{16,0},{20,4},{24,8},{28,12},{1,17},{... | collective-permute-start | bytes 110600 | tf_op jit(solution)/shard_map/ppermute | solution.py:351
  35.2 1.9 collective-permute-done.24
  46.1 3.1 %collective-permute-start.7 = (f32[4,2304]{1,0:T(4,128)S(1)}, f32[4,2304]{1,0:T(4,128)S(1)}, u32[]{:S(2)}, u32[]{:S(2)}) collective-permute-start(f32[4,2304]{1,0:T(4,128)S(1)} %get-tuple-element.131), channel_id=1, source_target_pairs={{0,24},{4,28},{8,16},{12,20},{16,8},{20,12},{24,0},{28,4},{1,25},{... | collective-permute-start | bytes 110600 | tf_op jit(solution)/shard_map/ppermute | solution.py:351
  50.1 1.7 collective-permute-done.7
  53.5 5.8 %collective-permute-done.20.u2 = bf16[8,48,384]{2,1,0:T(8,128)(2,1)} collective-permute-done((bf16[8,48,384]{2,1,0:T(8,128)(2,1)S(1)}, bf16[8,48,384]{2,1,0:T(8,128)(2,1)}, u32[]{:S(2)}, u32[]{:S(2)}) %collective-permute-start.20) | collective-permute-done | bytes 294944 | tf_op jit(solution)/shard_map/ppermute | solution.py:351
  59.4 5.8 %collective-permute-done.27.w2 = bf16[8,48,384]{2,1,0:T(8,128)(2,1)} collective-permute-done((bf16[8,48,384]{2,1,0:T(8,128)(2,1)S(1)}, bf16[8,48,384]{2,1,0:T(8,128)(2,1)}, u32[]{:S(2)}, u32[]{:S(2)}) %collective-permute-start.27) | collective-permute-done | bytes 294944 | tf_op jit(solution)/shard_map/ppermute | solution.py:351
  65.2 14.9 %attn_forward.1 = (bf16[4,256,1152]{2,1,0:T(8,128)(2,1)}, bf16[4,256,384]{2,1,0:T(8,128)(2,1)}, f32[4,256,384]{2,1,0:T(8,128)}, f32[4,6,256]{2,1,0:T(8,128)}) custom-call(s32[2]{0:T(128)} %pad_add_fusion.place, bf16[4,256,384]{2,1,0:T(8,128)(2,1)} %lat.7, f32[4,6,384]{2,1,0:T(8,128)} %reshape.180.mod, f32[1,5376]{1,0:T(1,128)} %copy-done.17, ...), custom_call_target="tpu_custom_call" | custom-call | flops 15000000512 | bytes 15000000 | tf_op jit(solution)/shard_map/attn_forward/pallas_call | solution.py:435
  81.1 21.2 %mlp_both.1 = (bf16[4,256,384]{2,1,0:T(8,128)(2,1)}, f32[4,256,384]{2,1,0:T(8,128)}, f32[4,6,384]{2,1,0:T(8,128)}, f32[384,384]{1,0:T(8,128)}, f32[1,3072]{1,0:T...) custom-call(s32[2]{0:T(128)} %pad_add_fusion.place, ...), custom_call_target="tpu_custom_call" | custom-call | flops 20000000000 | bytes 20000000 | tf_op jit(solution)/shard_map/mlp_both/pallas_call | solution.py:435
  103.5 3.0 %collective-permute-done.62 = bf16[32,48]{1,0:T(8,128)(2,1)S(1)} collective-permute-done((bf16[32,48]{1,0:T(8,128)(2,1)S(1)}, bf16[32,48]{1,0:T(8,128)(2,1)S(1)}, u32[]{:S(2)}, u32[]{:S(2)}) %collective-permute-start.62) | collective-permute-done | bytes 3104 | tf_op jit(solution)/shard_map/ppermute | solution.py:351
  114.8 11.3 %attn_backward.2 = (f32[2,256,384]{2,1,0:T(8,128)}, f32[2,2,384]{2,1,0:T(2,128)}, f32[1,768]{1,0:T(1,128)}, f32[384,1152]{1,0:T(8,128)}) custom-call(s32[2]{0:T(128)} %pad_add_fusion.place, bf16[4,256,384]{2,1,0:T(8,128)(2,1)} %lat.7, f32[4,256,384]{2,1,0:T(8,128)} %get-tuple-element.70.dmid, bf16[4,256,1152]{2,1,0:T(8,128)(2,1)} %get-tuple-element.71.qkv, ...), custom_call_target="tpu_custom_call" | custom-call | flops 10000000000 | bytes 10000000 | tf_op jit(solution)/shard_map/attn_backward/pallas_call | solution.py:435
  126.1 2.3 %collective-permute-done.31 = bf16[4,2,48,384]{3,2,1,0:T(8,128)(2,1)S(1)} collective-permute-done((bf16[4,2,48,384]{3,2,1,0:T(8,128)(2,1)S(1)}, bf16[4,2,48,384]{3,2,1,0:T(8,128)(2,1)S(1)}, u32[]{:S(2)}, u32[]{:S(2)}) %collective-permute-start.31) | collective-permute-done | bytes 294944 | tf_op jit(solution)/shard_map/ppermute | solution.py:351
  128.5 12.8 %attn_backward.3 = (f32[2,256,384]{2,1,0:T(8,128)}, f32[2,2,384]{2,1,0:T(2,128)}, f32[1,768]{1,0:T(1,128)}, f32[8,2,48,384]{3,2,1,0:T(8,128)}, bf16[8,2,48,384]{3,2,1,0:T(8,128)(2,1)}) custom-call(s32[2]{0:T(128)} %pad_add_fusion.place, bf16[4,256,384]{2,1,0:T(8,128)(2,1)} %lat.7, f32[4,256,384]{2,1,0:T(8,128)} %get-tuple-element.70.dmid, ...), custom_call_target="tpu_custom_call" | custom-call | flops 10000000000 | bytes 10000000 | tf_op jit(solution)/shard_map/attn_backward/pallas_call | solution.py:435
  144.2 3.1 %collective-permute-start.35 = (bf16[1,4,2304]{2,1,0:T(4,128)(2,1)S(1)}, bf16[1,4,2304]{2,1,0:T(4,128)(2,1)S(1)}, u32[]{:S(2)}, u32[]{:S(2)}) collective-permute-start(bf16[1,4,2304]{2,1,0:T(4,128)(2,1)S(1)} %convert_element_type.169), channel_id=1, source_target_pairs={{0,24},{4,28},{8,16},{12,20},{16,8},{20,12},{24,0},{28,4},{1,25},{... | collective-permute-start | bytes 55304 | tf_op jit(solution)/shard_map/ppermute | solution.py:351
  150.9 3.1 %collective-permute-start.46 = (bf16[2,48,384]{2,1,0:T(8,128)(2,1)S(1)}, bf16[2,48,384]{2,1,0:T(8,128)(2,1)S(1)}, u32[]{:S(2)}, u32[]{:S(2)}) collective-permute-start(bf16[2,48,384]{2,1,0:T(8,128)(2,1)S(1)} %get-tuple-element.123), channel_id=1, source_target_pairs={{0,24},{4,28},{8,16},{12,20},{16,8},{20,12},{24,0},{28,4},{1,25},{... | collective-permute-start | bytes 221192 | tf_op jit(solution)/shard_map/ppermute | solution.py:351
  154.8 3.3 %collective-permute-done.68 = f32[5376]{0:T(1024)S(1)} collective-permute-done((f32[5376]{0:T(1024)S(1)}, f32[5376]{0:T(1024)S(1)}, u32[]{:S(2)}, u32[]{:S(2)}) %collective-permute-start.68) | collective-permute-done | bytes 21536 | tf_op jit(solution)/shard_map/ppermute | solution.py:351
  158.6 3.3 %collective-permute-done.69 = f32[5376]{0:T(1024)S(1)} collective-permute-done((f32[5376]{0:T(1024)S(1)}, f32[5376]{0:T(1024)S(1)}, u32[]{:S(2)}, u32[]{:S(2)}) %collective-permute-start.69) | collective-permute-done | bytes 21536 | tf_op jit(solution)/shard_map/ppermute | solution.py:351
  163.1 3.1 %collective-permute-start.43 = (bf16[2,48,384]{2,1,0:T(8,128)(2,1)S(1)}, bf16[2,48,384]{2,1,0:T(8,128)(2,1)S(1)}, u32[]{:S(2)}, u32[]{:S(2)}) collective-permute-start(bf16[2,48,384]{2,1,0:T(8,128)(2,1)S(1)} %get-tuple-element.126), channel_id=1, source_target_pairs={{0,24},{4,28},{8,16},{12,20},{16,8},{20,12},{24,0},{28,4},{1,25},{... | collective-permute-start | bytes 221192 | tf_op jit(solution)/shard_map/ppermute | solution.py:351
  167.2 2.2 %collective-permute-done.43 = bf16[2,48,384]{2,1,0:T(8,128)(2,1)S(1)} collective-permute-done((bf16[2,48,384]{2,1,0:T(8,128)(2,1)S(1)}, bf16[2,48,384]{2,1,0:T(8,128)(2,1)S(1)}, u32[]{:S(2)}, u32[]{:S(2)}) %collective-permute-start.43) | collective-permute-done | bytes 73760 | tf_op jit(solution)/shard_map/ppermute | solution.py:351
  171.2 2.8 %collective-permute-start.38 = (f32[1,32,48]{2,1,0:T(8,128)S(1)}, f32[1,32,48]{2,1,0:T(8,128)S(1)}, u32[]{:S(2)}, u32[]{:S(2)}) collective-permute-start(f32[1,32,48]{2,1,0:T(8,128)S(1)} %bitcast.123), channel_id=1, source_target_pairs={{0,16},{4,20},{8,24},{12,28},{16,0},{20,4},{24,8},{28,12},{1,17},{... | collective-permute-start | bytes 18440 | tf_op jit(solution)/shard_map/ppermute | solution.py:351
  177.3 2.2 %collective-permute-done.39 = f32[1,32,48]{2,1,0:T(8,128)S(1)} collective-permute-done((f32[1,32,48]{2,1,0:T(8,128)S(1)}, f32[1,32,48]{2,1,0:T(8,128)S(1)}, u32[]{:S(2)}, u32[]{:S(2)}) %collective-permute-start.39) | collective-permute-done | bytes 6176 | tf_op jit(solution)/shard_map/ppermute | solution.py:351
  181.6 2.3 %collective-permute-done.40 = f32[4,32,48]{2,1,0:T(8,128)S(1)} collective-permute-done((f32[4,32,48]{2,1,0:T(8,128)S(1)}, f32[4,32,48]{2,1,0:T(8,128)S(1)}, u32[]{:S(2)}, u32[]{:S(2)}) %collective-permute-start.40) | collective-permute-done | bytes 24608 | tf_op jit(solution)/shard_map/ppermute | solution.py:351
  188.4 4.7 %collective-permute-done.48 = bf16[4,2,48,384]{3,2,1,0:T(8,128)(2,1)S(1)} collective-permute-done((bf16[4,2,48,384]{3,2,1,0:T(8,128)(2,1)S(1)}, bf16[4,2,48,384]{3,2,1,0:T(8,128)(2,1)S(1)}, u32[]{:S(2)}, u32[]{:S(2)}) %collective-permute-start.48) | collective-permute-done | bytes 294944 | tf_op jit(solution)/shard_map/ppermute | solution.py:351
  195.2 2.4 %collective-permute-start.51 = (bf16[2,48,384]{2,1,0:T(8,128)(2,1)S(1)}, bf16[2,48,384]{2,1,0:T(8,128)(2,1)S(1)}, u32[]{:S(2)}, u32[]{:S(2)}) collective-permute-start(bf16[2,48,384]{2,1,0:T(8,128)(2,1)S(1)} %get-tuple-element.120), channel_id=1, source_target_pairs={{0,24},{4,28},{8,16},{12,20},{16,8},{20,12},{24,0},{28,4},{1,25},{... | collective-permute-start | bytes 221192 | tf_op jit(solution)/shard_map/ppermute | solution.py:351
  198.3 1.7 collective-permute-start.57
  202.7 1.9 collective-permute-start.60
  206.8 2.0 fusion.refs_12_
  210.8 6.9 %adam.1 = (f32[48,4992]{1,0:T(8,128)}, f32[48,384]{1,0:T(8,128)}, f32[4,48,384]{2,1,0:T(8,128)}, f32[48,4992]{1,0:T(8,128)}, f32[48,384]{1,0:T(8,128)}, /*index=...) custom-call(s32[2]{0:T(128)} %pad_add_fusion.place, ...), custom_call_target="tpu_custom_call" | custom-call | tf_op jit(solution)/shard_map/adam/pallas_call | solution.py:629
  (292 shorter events, 69.3 us)
Async XLA Ops:
  2.9 13.0 %collective-permute-start = (f32[1,680]{1,0:T(1,128)S(1)}, f32[1,680]{1,0:T(1,128)S(1)}, u32[]{:S(2)}, u32[]{:S(2)}) collective-permute-start(f32[1,680]{1,0:T(1,128)S(1)} %broadcast_in_dim.39), channel_id=1, source_target_pairs={{0,8},{4,12},{8,0},{12,4},{16,24},{20,28},{24,16},{28,20},{1,9},{5... | collective-permute-start | bytes 8168 | tf_op jit(solution)/shard_map/ppermute | solution.py:351
  5.9 10.5 %collective-permute-start.1 = (f32[1,680]{1,0:T(1,128)S(1)}, f32[1,680]{1,0:T(1,128)S(1)}, u32[]{:S(2)}, u32[]{:S(2)}) collective-permute-start(f32[1,680]{1,0:T(1,128)S(1)} %broadcast_in_dim.39), channel_id=1, source_target_pairs={{0,16},{4,20},{8,24},{12,28},{16,0},{20,4},{24,8},{28,12},{1,17},{... | collective-permute-start | bytes 8168 | tf_op jit(solution)/shard_map/ppermute | solution.py:351
  8.5 9.5 %collective-permute-start.2 = (f32[1,680]{1,0:T(1,128)S(1)}, f32[1,680]{1,0:T(1,128)S(1)}, u32[]{:S(2)}, u32[]{:S(2)}) collective-permute-start(f32[1,680]{1,0:T(1,128)S(1)} %broadcast_in_dim.39), channel_id=1, source_target_pairs={{0,24},{4,28},{8,16},{12,20},{16,8},{20,12},{24,0},{28,4},{1,25},{... | collective-permute-start | bytes 8168 | tf_op jit(solution)/shard_map/ppermute | solution.py:351
  10.3 16.4 %collective-permute-start.10 = (bf16[1,48,384]{2,1,0:T(8,128)(2,1)S(1)}, bf16[1,48,384]{2,1,0:T(8,128)(2,1)S(1)}, u32[]{:S(2)}, u32[]{:S(2)}) collective-permute-start(bf16[1,48,384]{2,1,0:T(8,128)(2,1)S(1)} %get-tuple-element.118), channel_id=1, source_target_pairs={{0,24},{4,28},{8,16},{12,20},{16,8},{20,12},{24,0},{28,4},{1,25},{... | collective-permute-start | bytes 110600 | tf_op jit(solution)/shard_map/ppermute | solution.py:351
  14.1 12.7 %collective-permute-start.8 = (bf16[1,48,384]{2,1,0:T(8,128)(2,1)S(1)}, bf16[1,48,384]{2,1,0:T(8,128)(2,1)S(1)}, u32[]{:S(2)}, u32[]{:S(2)}) collective-permute-start(bf16[1,48,384]{2,1,0:T(8,128)(2,1)S(1)} %get-tuple-element.118), channel_id=1, source_target_pairs={{0,8},{4,12},{8,0},{12,4},{16,24},{20,28},{24,16},{28,20},{1,9},{5... | collective-permute-start | bytes 110600 | tf_op jit(solution)/shard_map/ppermute | solution.py:351
  15.9 11.6 %collective-permute-start.9 = (bf16[1,48,384]{2,1,0:T(8,128)(2,1)S(1)}, bf16[1,48,384]{2,1,0:T(8,128)(2,1)S(1)}, u32[]{:S(2)}, u32[]{:S(2)}) collective-permute-start(bf16[1,48,384]{2,1,0:T(8,128)(2,1)S(1)} %get-tuple-element.118), channel_id=1, source_target_pairs={{0,16},{4,20},{8,24},{12,28},{16,0},{20,4},{24,8},{28,12},{1,17},{... | collective-permute-start | bytes 110600 | tf_op jit(solution)/shard_map/ppermute | solution.py:351
  16.5 14.8 %collective-permute-start.15 = (bf16[1,48,384]{2,1,0:T(8,128)(2,1)S(1)}, bf16[1,48,384]{2,1,0:T(8,128)(2,1)S(1)}, u32[]{:S(2)}, u32[]{:S(2)}) collective-permute-start(bf16[1,48,384]{2,1,0:T(8,128)(2,1)S(1)} %get-tuple-element.114), channel_id=1, source_target_pairs={{0,8},{4,12},{8,0},{12,4},{16,24},{20,28},{24,16},{28,20},{1,9},{5... | collective-permute-start | bytes 110600 | tf_op jit(solution)/shard_map/ppermute | solution.py:351
  21.8 9.6 %collective-permute-start.16 = (bf16[1,48,384]{2,1,0:T(8,128)(2,1)S(1)}, bf16[1,48,384]{2,1,0:T(8,128)(2,1)S(1)}, u32[]{:S(2)}, u32[]{:S(2)}) collective-permute-start(bf16[1,48,384]{2,1,0:T(8,128)(2,1)S(1)} %get-tuple-element.114), channel_id=1, source_target_pairs={{0,16},{4,20},{8,24},{12,28},{16,0},{20,4},{24,8},{28,12},{1,17},{... | collective-permute-start | bytes 110600 | tf_op jit(solution)/shard_map/ppermute | solution.py:351
  31.4 11.0 %collective-permute-start.4 = (f32[4,4,2304]{2,1,0:T(4,128)S(1)}, f32[4,4,2304]{2,1,0:T(4,128)S(1)}, u32[]{:S(2)}, u32[]{:S(2)}) collective-permute-start(f32[4,4,2304]{2,1,0:T(4,128)S(1)} %slice.186), channel_id=1, source_target_pairs={{0,4},{4,0},{8,12},{12,8},{16,20},{20,16},{24,28},{28,24},{1,5},{5... | collective-permute-start | bytes 442376 | tf_op jit(solution)/shard_map/ppermute | solution.py:351
  33.0 9.5 %collective-permute-start.11 = (bf16[4,48,384]{2,1,0:T(8,128)(2,1)S(1)}, bf16[4,48,384]{2,1,0:T(8,128)(2,1)S(1)}, u32[]{:S(2)}, u32[]{:S(2)}) collective-permute-start(bf16[4,48,384]{2,1,0:T(8,128)(2,1)S(1)} %pad_maximum_fusion.1), channel_id=1, source_target_pairs={{0,4},{4,0},{8,12},{12,8},{16,20},{20,16},{24,28},{28,24},{1,5},{5... | collective-permute-start | bytes 442376 | tf_op jit(solution)/shard_map/ppermute | solution.py:351
  34.1 12.0 %collective-permute-start.18 = (bf16[4,48,384]{2,1,0:T(8,128)(2,1)S(1)}, bf16[4,48,384]{2,1,0:T(8,128)(2,1)S(1)}, u32[]{:S(2)}, u32[]{:S(2)}) collective-permute-start(bf16[4,48,384]{2,1,0:T(8,128)(2,1)S(1)} %pad_maximum_fusion.2), channel_id=1, source_target_pairs={{0,4},{4,0},{8,12},{12,8},{16,20},{20,16},{24,28},{28,24},{1,5},{5... | collective-permute-start | bytes 442376 | tf_op jit(solution)/shard_map/ppermute | solution.py:351
  37.1 12.1 %collective-permute-start.25 = (bf16[4,48,384]{2,1,0:T(8,128)(2,1)S(1)}, bf16[4,48,384]{2,1,0:T(8,128)(2,1)S(1)}, u32[]{:S(2)}, u32[]{:S(2)}) collective-permute-start(bf16[4,48,384]{2,1,0:T(8,128)(2,1)S(1)} %pad_maximum_fusion.3), channel_id=1, source_target_pairs={{0,4},{4,0},{8,12},{12,8},{16,20},{20,16},{24,28},{28,24},{1,5},{5... | collective-permute-start | bytes 442376 | tf_op jit(solution)/shard_map/ppermute | solution.py:351
  43.2 9.2 %collective-permute-start.13 = (bf16[8,48,384]{2,1,0:T(8,128)(2,1)}, bf16[8,48,384]{2,1,0:T(8,128)(2,1)S(1)}, u32[]{:S(2)}, u32[]{:S(2)}) collective-permute-start(bf16[8,48,384]{2,1,0:T(8,128)(2,1)} %constant_dynamic-update-slice_fusion.p0), channel_id=1, source_target_pairs={{0,2},{1,3},{2,0},{3,1},{4,6},{5,7},{6,4},{7,5},{8,10},{9,11},{10,... | collective-permute-start | bytes 884744 | tf_op jit(solution)/shard_map/ppermute | solution.py:351
  49.3 10.0 %collective-permute-start.20 = (bf16[8,48,384]{2,1,0:T(8,128)(2,1)S(1)}, bf16[8,48,384]{2,1,0:T(8,128)(2,1)}, u32[]{:S(2)}, u32[]{:S(2)}) collective-permute-start(bf16[8,48,384]{2,1,0:T(8,128)(2,1)S(1)} %constant_dynamic-update-slice_fusion.5.u0), channel_id=1, source_target_pairs={{0,2},{1,3},{2,0},{3,1},{4,6},{5,7},{6,4},{7,5},{8,10},{9,11},{10,... | collective-permute-start | bytes 884744 | tf_op jit(solution)/shard_map/ppermute | solution.py:351
  49.9 30.2 %collective-permute-start.19 = (bf16[8,48,384]{2,1,0:T(8,128)(2,1)S(1)}, bf16[8,48,384]{2,1,0:T(8,128)(2,1)}, u32[]{:S(2)}, u32[]{:S(2)}) collective-permute-start(bf16[8,48,384]{2,1,0:T(8,128)(2,1)S(1)} %constant_dynamic-update-slice_fusion.5.u0), channel_id=1, source_target_pairs={{0,1},{1,0},{2,3},{3,2},{4,5},{5,4},{6,7},{7,6},{8,9},{9,8},{10,11... | collective-permute-start | bytes 884744 | tf_op jit(solution)/shard_map/ppermute | solution.py:351
  51.8 13.4 %collective-permute-start.27 = (bf16[8,48,384]{2,1,0:T(8,128)(2,1)S(1)}, bf16[8,48,384]{2,1,0:T(8,128)(2,1)}, u32[]{:S(2)}, u32[]{:S(2)}) collective-permute-start(bf16[8,48,384]{2,1,0:T(8,128)(2,1)S(1)} %constant_dynamic-update-slice_fusion.10.w0), channel_id=1, source_target_pairs={{0,2},{1,3},{2,0},{3,1},{4,6},{5,7},{6,4},{7,5},{8,10},{9,11},{10,... | collective-permute-start | bytes 884744 | tf_op jit(solution)/shard_map/ppermute | solution.py:351
  52.4 12.9 %collective-permute-start.14 = (bf16[8,48,384]{2,1,0:T(8,128)(2,1)S(1)}, bf16[8,48,384]{2,1,0:T(8,128)(2,1)}, u32[]{:S(2)}, u32[]{:S(2)}) collective-permute-start(bf16[8,48,384]{2,1,0:T(8,128)(2,1)S(1)} %collective-permute-done.13.p2), channel_id=1, source_target_pairs={{0,1},{1,0},{2,3},{3,2},{4,5},{5,4},{6,7},{7,6},{8,9},{9,8},{10,11... | collective-permute-start | bytes 884744 | tf_op jit(solution)/shard_map/ppermute | solution.py:351
  53.1 27.0 %collective-permute-start.26 = (bf16[8,48,384]{2,1,0:T(8,128)(2,1)S(1)}, bf16[8,48,384]{2,1,0:T(8,128)(2,1)S(1)}, u32[]{:S(2)}, u32[]{:S(2)}) collective-permute-start(bf16[8,48,384]{2,1,0:T(8,128)(2,1)S(1)} %constant_dynamic-update-slice_fusion.10.w0), channel_id=1, source_target_pairs={{0,1},{1,0},{2,3},{3,2},{4,5},{5,4},{6,7},{7,6},{8,9},{9,8},{10,11... | collective-permute-start | bytes 884744 | tf_op jit(solution)/shard_map/ppermute | solution.py:351
  59.4 20.8 %collective-permute-start.21 = (bf16[8,48,384]{2,1,0:T(8,128)(2,1)}, bf16[8,48,384]{2,1,0:T(8,128)(2,1)S(1)}, u32[]{:S(2)}, u32[]{:S(2)}) collective-permute-start(bf16[8,48,384]{2,1,0:T(8,128)(2,1)} %collective-permute-done.20.u2), channel_id=1, source_target_pairs={{0,1},{1,0},{2,3},{3,2},{4,5},{5,4},{6,7},{7,6},{8,9},{9,8},{10,11... | collective-permute-start | bytes 884744 | tf_op jit(solution)/shard_map/ppermute | solution.py:351
  65.2 15.0 %collective-permute-start.28 = (bf16[8,48,384]{2,1,0:T(8,128)(2,1)}, bf16[8,48,384]{2,1,0:T(8,128)(2,1)S(1)}, u32[]{:S(2)}, u32[]{:S(2)}) collective-permute-start(bf16[8,48,384]{2,1,0:T(8,128)(2,1)} %collective-permute-done.27.w2), channel_id=1, source_target_pairs={{0,1},{1,0},{2,3},{3,2},{4,5},{5,4},{6,7},{7,6},{8,9},{9,8},{10,11... | collective-permute-start | bytes 884744 | tf_op jit(solution)/shard_map/ppermute | solution.py:351
  102.3 8.5 %collective-permute-start.30 = (bf16[8,2,48,384]{3,2,1,0:T(8,128)(2,1)}, bf16[8,2,48,384]{3,2,1,0:T(8,128)(2,1)S(1)}, u32[]{:S(2)}, u32[]{:S(2)}) collective-permute-start(bf16[8,2,48,384]{3,2,1,0:T(8,128)(2,1)} %get-tuple-element.69), channel_id=1, source_target_pairs={{0,1},{1,0},{2,3},{3,2},{4,5},{5,4},{6,7},{7,6},{8,9},{9,8},{10,11... | collective-permute-start | bytes 1769480 | tf_op jit(solution)/shard_map/ppermute | solution.py:351
  102.8 9.5 %collective-permute-start.29 = (bf16[8,2,48,384]{3,2,1,0:T(8,128)(2,1)}, bf16[8,2,48,384]{3,2,1,0:T(8,128)(2,1)S(1)}, u32[]{:S(2)}, u32[]{:S(2)}) collective-permute-start(bf16[8,2,48,384]{3,2,1,0:T(8,128)(2,1)} %get-tuple-element.67), channel_id=1, source_target_pairs={{0,1},{1,0},{2,3},{3,2},{4,5},{5,4},{6,7},{7,6},{8,9},{9,8},{10,11... | collective-permute-start | bytes 1769480 | tf_op jit(solution)/shard_map/ppermute | solution.py:351
  112.6 13.5 %collective-permute-start.32 = (bf16[4,2,48,384]{3,2,1,0:T(8,128)(2,1)S(1)}, bf16[4,2,48,384]{3,2,1,0:T(8,128)(2,1)S(1)}, u32[]{:S(2)}, u32[]{:S(2)}) collective-permute-start(bf16[4,2,48,384]{3,2,1,0:T(8,128)(2,1)S(1)} %slice.374), channel_id=1, source_target_pairs={{0,4},{4,0},{8,12},{12,8},{16,20},{20,16},{24,28},{28,24},{1,5},{5... | collective-permute-start | bytes 884744 | tf_op jit(solution)/shard_map/ppermute | solution.py:351
  113.2 15.2 %collective-permute-start.31 = (bf16[4,2,48,384]{3,2,1,0:T(8,128)(2,1)S(1)}, bf16[4,2,48,384]{3,2,1,0:T(8,128)(2,1)S(1)}, u32[]{:S(2)}, u32[]{:S(2)}) collective-permute-start(bf16[4,2,48,384]{3,2,1,0:T(8,128)(2,1)S(1)} %slice.375), channel_id=1, source_target_pairs={{0,4},{4,0},{8,12},{12,8},{16,20},{20,16},{24,28},{28,24},{1,5},{5... | collective-permute-start | bytes 884744 | tf_op jit(solution)/shard_map/ppermute | solution.py:351
  144.2 9.8 %collective-permute-start.35 = (bf16[1,4,2304]{2,1,0:T(4,128)(2,1)S(1)}, bf16[1,4,2304]{2,1,0:T(4,128)(2,1)S(1)}, u32[]{:S(2)}, u32[]{:S(2)}) collective-permute-start(bf16[1,4,2304]{2,1,0:T(4,128)(2,1)S(1)} %convert_element_type.169), channel_id=1, source_target_pairs={{0,24},{4,28},{8,16},{12,20},{16,8},{20,12},{24,0},{28,4},{1,25},{... | collective-permute-start | bytes 55304 | tf_op jit(solution)/shard_map/ppermute | solution.py:351
  148.1 15.0 %collective-permute-start.44 = (bf16[2,48,384]{2,1,0:T(8,128)(2,1)S(1)}, bf16[2,48,384]{2,1,0:T(8,128)(2,1)S(1)}, u32[]{:S(2)}, u32[]{:S(2)}) collective-permute-start(bf16[2,48,384]{2,1,0:T(8,128)(2,1)S(1)} %get-tuple-element.122), channel_id=1, source_target_pairs={{0,8},{4,12},{8,0},{12,4},{16,24},{20,28},{24,16},{28,20},{1,9},{5... | collective-permute-start | bytes 221192 | tf_op jit(solution)/shard_map/ppermute | solution.py:351
  150.6 15.7 %collective-permute-start.45 = (bf16[2,48,384]{2,1,0:T(8,128)(2,1)S(1)}, bf16[2,48,384]{2,1,0:T(8,128)(2,1)S(1)}, u32[]{:S(2)}, u32[]{:S(2)}) collective-permute-start(bf16[2,48,384]{2,1,0:T(8,128)(2,1)S(1)} %get-tuple-element.124), channel_id=1, source_target_pairs={{0,16},{4,20},{8,24},{12,28},{16,0},{20,4},{24,8},{28,12},{1,17},{... | collective-permute-start | bytes 221192 | tf_op jit(solution)/shard_map/ppermute | solution.py:351
  150.9 15.9 %collective-permute-start.46 = (bf16[2,48,384]{2,1,0:T(8,128)(2,1)S(1)}, bf16[2,48,384]{2,1,0:T(8,128)(2,1)S(1)}, u32[]{:S(2)}, u32[]{:S(2)}) collective-permute-start(bf16[2,48,384]{2,1,0:T(8,128)(2,1)S(1)} %get-tuple-element.123), channel_id=1, source_target_pairs={{0,24},{4,28},{8,16},{12,20},{16,8},{20,12},{24,0},{28,4},{1,25},{... | collective-permute-start | bytes 221192 | tf_op jit(solution)/shard_map/ppermute | solution.py:351
  153.9 12.9 %collective-permute-start.41 = (bf16[2,48,384]{2,1,0:T(8,128)(2,1)S(1)}, bf16[2,48,384]{2,1,0:T(8,128)(2,1)S(1)}, u32[]{:S(2)}, u32[]{:S(2)}) collective-permute-start(bf16[2,48,384]{2,1,0:T(8,128)(2,1)S(1)} %get-tuple-element.125), channel_id=1, source_target_pairs={{0,8},{4,12},{8,0},{12,4},{16,24},{20,28},{24,16},{28,20},{1,9},{5... | collective-permute-start | bytes 221192 | tf_op jit(solution)/shard_map/ppermute | solution.py:351
  169.4 14.5 %collective-permute-start.47 = (bf16[8,2,48,384]{3,2,1,0:T(8,128)(2,1)}, bf16[8,2,48,384]{3,2,1,0:T(8,128)(2,1)S(1)}, u32[]{:S(2)}, u32[]{:S(2)}) collective-permute-start(bf16[8,2,48,384]{3,2,1,0:T(8,128)(2,1)} %get-tuple-element.88), channel_id=1, source_target_pairs={{0,1},{1,0},{2,3},{3,2},{4,5},{5,4},{6,7},{7,6},{8,9},{9,8},{10,11... | collective-permute-start | bytes 1769480 | tf_op jit(solution)/shard_map/ppermute | solution.py:351
  169.5 28.7 %collective-permute-start.55 = (bf16[2,48,384]{2,1,0:T(8,128)(2,1)S(1)}, bf16[2,48,384]{2,1,0:T(8,128)(2,1)}, u32[]{:S(2)}, u32[]{:S(2)}) collective-permute-start(bf16[2,48,384]{2,1,0:T(8,128)(2,1)S(1)} %fusion.15.refs_4_), channel_id=1, source_target_pairs={{0,2},{1,3},{2,0},{3,1},{4,6},{5,7},{6,4},{7,5},{8,10},{9,11},{10,... | collective-permute-start | bytes 221192 | tf_op jit(solution)/shard_map/ppermute | solution.py:351
  175.8 22.5 %collective-permute-start.65 = (bf16[32,2304]{1,0:T(8,128)(2,1)S(1)}, bf16[32,2304]{1,0:T(8,128)(2,1)}, u32[]{:S(2)}, u32[]{:S(2)}) collective-permute-start(bf16[32,2304]{1,0:T(8,128)(2,1)S(1)} %reshape.181), channel_id=1, source_target_pairs={{0,2},{1,3},{2,0},{3,1},{4,6},{5,7},{6,4},{7,5},{8,10},{9,11},{10,... | collective-permute-start | bytes 442376 | tf_op jit(solution)/shard_map/ppermute | solution.py:351
  (75 other events, 608.8 us)

commit v2 on v1

--- a/solution.py
+++ b/solution.py
@@ -61,37 +61,52 @@
     return (relative & 1) * (owners // 2) + (relative >> 1)
 
 
-def unpack_columns(place, pieces, whole):
-    owners, rows, width = pieces[0].shape
-    me, mine = place[0], place[1]
-    for block in range(GROUP):
-        for k in range(GROUP):
-
-            @pl.when((mine ^ k) == block)
+def unpack_attn(place, own, other, whole):
+    owners, width = own.shape[0], own.shape[-1]
+    rows = whole.shape[0] // owners
+    for core in range(2):
+        for source, near in ((own, True), (other, False)):
+
+            @pl.when(((place[1] & 1) == core) == near)
             def _():
-                for owner in range(owners):
-                    whole[owner * rows : (owner + 1) * rows, block * width : (block + 1) * width] = (
-                        pieces[k][spot_of(owner ^ me, owners)]
-                    )
-
-
-def unpack_rows(place, pieces, whole):
-    owners, rows, width = pieces[0].shape
-    me, mine = place[0], place[1]
-    for block in range(GROUP):
-        for k in range(GROUP):
-
-            @pl.when((mine ^ k) == block)
-            def _():
-                for owner in range(owners):
-                    start = (owner * GROUP + block) * rows
-                    whole[start : start + rows, :] = pieces[k][spot_of(owner ^ me, owners)]
-
-
-def pack_block(place, block, owner, value, keep, send):
+                for part in range(2):
+                    block = 2 * core + part
+                    for owner in range(owners):
+                        whole[
+                            owner * rows : (owner + 1) * rows, block * width : (block + 1) * width
+                        ] = source[owner, part * rows : (part + 1) * rows, :]
+
+
+def unpack_mlp(place, own, other, w_up, w_down):
+    width = w_up.shape[0]
+    upper = own[0].shape[0]
+    owners = 2 * upper
+    rows = width // owners
+    for core in range(2):
+        for source, near in ((own, True), (other, False)):
+            for side in range(2):
+
+                @pl.when((((place[1] & 1) == core) == near))
+                def _():
+                    for owner in range(owners):
+
+                        @pl.when(((place[0] ^ owner) & 1) == side)
+                        def _():
+                            spot = (place[0] ^ owner) >> 1
+                            piece = source[side]
+                            for part in range(2):
+                                block = 2 * core + part
+                                w_up[
+                                    owner * rows : (owner + 1) * rows,
+                                    block * width : (block + 1) * width,
+                                ] = piece[spot, part * rows : (part + 1) * rows, :]
+                            start = (owner * GROUP + 2 * core) * rows
+                            w_down[start : start + 2 * rows, :] = piece[spot, 2 * rows : 4 * rows, :]
+
+
+def pack_block(place, block, spot, value, keep, send, offset=0):
     k = place[1] ^ block
-    spot = spot_of(place[0] ^ owner, keep.shape[0])
-    half = k >> 1
+    half = (k >> 1) + offset
 
     @pl.when((k & 1) == 0)
     def _():
@@ -108,12 +123,12 @@
     return low.astype(bf16), (1.0 - low).astype(bf16)
 
 
-def attn_forward(place, lat, mod, bias, p0, p1, p2, p3, qkv_o, att_o, branch_o, lse_o, whole, att_t):
+def attn_forward(place, lat, mod, bias, own, other, qkv_o, att_o, branch_o, lse_o, whole, att_t):
     width = lat.shape[-1]
 
     @pl.when(pl.program_id(0) == 0)
     def _():
-        unpack_columns(place, (p0, p1, p2, p3), whole)
+        unpack_attn(place, own, other, whole)
 
     normed, _ = layer_norm(lat[0].astype(f32))
     input_a = (normed * (1.0 + mod[0, 1:2]) + mod[0, 0:1]).astype(bf16)
@@ -147,8 +162,8 @@
 
 def mlp_both(
     place, lat, cot, branch, att, mod, bias,
-    u0, u1, u2, u3, w0, w1, w2, w3,
-    out_o, dmid_o, dmod_o, gattn_o, gbias_o, upk_o, ups_o, dnk_o, dns_o,
+    own_near, own_far, other_near, other_far,
+    out_o, dmid_o, dmod_o, gattn_o, gbias_o, keep_o, send_o,
     w_up, w_down, gelu_s, slope_s, dpre_s, acc_up, acc_down,
 ):
     width = lat.shape[-1]
@@ -158,8 +173,7 @@
 
     @pl.when(first)
     def _():
-        unpack_columns(place, (u0, u1, u2, u3), w_up)
-        unpack_rows(place, (w0, w1, w2, w3), w_down)
+        unpack_mlp(place, (own_near, own_far), (other_near, other_far), w_up, w_down)
         acc_up[...] = jnp.zeros_like(acc_up)
         acc_down[...] = jnp.zeros_like(acc_down)
         gattn_o[...] = jnp.zeros_like(gattn_o)
@@ -210,19 +224,19 @@
 
     @pl.when(step == pl.num_programs(0) - 1)
     def _():
-        owners, rows = upk_o.shape[0], upk_o.shape[2]
-        for block in range(GROUP):
-            for owner in range(owners):
+        owners, rows = keep_o.shape[0], keep_o.shape[2]
+        whole_down = acc_down[...].T
+        for owner in range(owners):
+            spot = spot_of(place[0] ^ owner, owners)
+            for block in range(GROUP):
                 value = acc_up[owner * rows : (owner + 1) * rows, block * width : (block + 1) * width]
-                pack_block(place, block, owner, value, upk_o, ups_o)
-        whole_down = acc_down[...].T
-        for block in range(GROUP):
-            for owner in range(owners):
+                pack_block(place, block, spot, value, keep_o, send_o)
                 start = (owner * GROUP + block) * rows
-                pack_block(place, block, owner, whole_down[start : start + rows, :], dnk_o, dns_o)
-
-
-def attn_backward(first, last, place, lat, dmid, qkv, lse, mod, p0, p1, p2, p3, *refs):
+                value = whole_down[start : start + rows, :]
+                pack_block(place, block, spot, value, keep_o, send_o, 2)
+
+
+def attn_backward(first, last, place, lat, dmid, qkv, lse, mod, own, other, *refs):
     refs = list(refs)
     if not first:
         acc_i, gbias_i = refs.pop(0), refs.pop(0)
@@ -238,7 +252,7 @@
 
     @pl.when(step == 0)
     def _():
-        unpack_columns(place, (p0, p1, p2, p3), whole)
+        unpack_attn(place, own, other, whole)
         acc[...] = jnp.zeros_like(acc) if first else acc_i[...]
         gbias_o[...] = jnp.zeros_like(gbias_o) if first else gbias_i[...]
 
@@ -313,9 +327,9 @@
 
 
 def adam_kernel(place, *refs):
-    att, up, down, gmod = refs[0:4], refs[4:8], refs[8:12], refs[12]
-    weights, means, squares = refs[13:16], refs[16:19], refs[19:22]
-    grads, new_w, new_m, new_s = refs[22:25], refs[25:28], refs[28:31], refs[31:34]
+    att, mlp = refs[0:4], refs[4:8]
+    weights, means, squares = refs[8:11], refs[11:14], refs[14:17]
+    grads, new_w, new_m, new_s = refs[17:20], refs[20:23], refs[23:26], refs[26:29]
     width = att[0].shape[-1]
 
     def write(which, where, gradient):
@@ -325,11 +339,11 @@
         )
         new_w[which][where], new_m[which][where], new_s[which][where] = result
 
-    def block_of(parts, block):
+    def block_of(parts, block, offset=0):
         k = place[1] ^ block
-        half = k >> 1
-        near = parts[0][half].astype(f32) + parts[1][1 - half].astype(f32)
-        far = parts[2][half].astype(f32) + parts[3][1 - half].astype(f32)
+        here, there = offset + (k >> 1), offset + 1 - (k >> 1)
+        near = parts[0][here].astype(f32) + parts[1][there].astype(f32)
+        far = parts[2][here].astype(f32) + parts[3][there].astype(f32)
         return jnp.where((k & 1) == 0, near, far)
 
     everything = slice(None)
@@ -340,10 +354,17 @@
         else:
             write(1, (everything, everything), g_att)
         at = (GROUP - 1 + block) * width
-        write(0, (everything, slice(at, at + width)), block_of(up, block))
-        write(2, (block,), block_of(down, block))
-    at = (2 * GROUP - 1) * width
-    write(0, (everything, slice(at, at + gmod.shape[1])), gmod[...])
+        write(0, (everything, slice(at, at + width)), block_of(mlp, block))
+        write(2, (block,), block_of(mlp, block, 2))
+
+
+def adam_mod(grad, weight, mean, square, *refs):
+    grad_o, weight_o, mean_o, square_o = refs[4:]
+    gradient = grad[...]
+    grad_o[...] = gradient
+    weight_o[...], mean_o[...], square_o[...] = adam_parts(
+        weight[...], mean[...], square[...], gradient
+    )
 
 
 def swap(value, axis, bit):
@@ -364,16 +385,25 @@
     return held
 
 
-def dp_gather(value):
-    held = gather_upper(value[None])
-    return jnp.concatenate([held, swap(held, "dp", 1)], axis=0)
-
-
 def group_gather(value):
     two = swap(value, "group", 2)
-    one = swap(value, "group", 1)
-    three = swap(two, "group", 1)
-    return value, one, two, three
+    return value, two, swap(value, "group", 1), swap(two, "group", 1)
+
+
+def in_order(parts, mine):
+    low = mine < 2
+    even = (mine & 1) == 0
+    near, far = jnp.where(low, parts[0], parts[1]), jnp.where(low, parts[1], parts[0])
+    other, wide = jnp.where(low, parts[2], parts[3]), jnp.where(low, parts[3], parts[2])
+    return jnp.concatenate(
+        [
+            jnp.where(even, near, other),
+            jnp.where(even, other, near),
+            jnp.where(even, far, wide),
+            jnp.where(even, wide, far),
+        ],
+        axis=0,
+    )
 
 
 def scatter_near(keep, dtype):
@@ -399,13 +429,18 @@
     return [sent] + [swap(sent, "group", k) for k in (2, 1, 3)]
 
 
-def sum_all(value):
-    value = value + swap(value, "group", 1)
-    value = value + swap(value, "group", 2)
-    owners = lax.axis_size("dp")
-    for bit in [1 << b for b in range(owners.bit_length() - 1)]:
-        value = value + swap(value, "dp", bit)
-    return value
+def to_owners(value):
+    return lax.all_to_all(value, "dp", 0, 0, tiled=True)
+
+
+def pad_rows(value, width, rows):
+    flat = value.reshape(value.shape[0], -1)
+    return jnp.pad(flat, ((0, 0), (0, rows * width - flat.shape[1]))).reshape(-1, rows, width)
+
+
+def halves(value):
+    high = lax.reduce_precision(value, 8, 7)
+    return jnp.concatenate([high.astype(bf16), (value - high).astype(bf16)], axis=-1)
 
 
 def compiler(limit=56):
@@ -469,46 +504,62 @@
     mine = lax.axis_index("group")
     place = jnp.stack([me, mine]).astype(jnp.int32)
 
+    core = mine & 1
     bias_shard = biases.shape[0]
-    message = jnp.concatenate([timestep.astype(f32), labels.astype(f32), biases])
-    small = dp_gather(message)
-    times_rel = small[:, :count].reshape(-1)
-    labels_rel = small[:, count : 2 * count].reshape(-1).astype(jnp.int32)
-    absolute = spot_of(jnp.arange(owners, dtype=jnp.int32) ^ me, owners)
-    bias_all = (
-        jnp.take(small[:, 2 * count :], absolute, axis=0).reshape(1, -1).astype(bf16).astype(f32)
-    )
+    mod_at = 3 * width + hidden
+    bias_mod_at = 4 * width + hidden
+
+    def blocks_of(first, second):
+        return jnp.where(core == 0, first, second)
+
+    q_rows, k_rows, v_rows = [input_proj[:, b * width : (b + 1) * width] for b in range(3)]
+    ids = jnp.concatenate([timestep, labels]).astype(jnp.int32)
+    note = jnp.concatenate([biases, (ids // 32).astype(f32), (ids % 32).astype(f32)])
+    note_size = note.shape[0]
+    note_rows = 8 * -(-note_size // (8 * width))
+    note = pad_rows(note[None].astype(bf16), width, note_rows)[0]
+    message = jnp.concatenate(
+        [
+            blocks_of(q_rows, v_rows).astype(bf16),
+            blocks_of(k_rows, attn_proj).astype(bf16),
+            note,
+        ],
+        axis=0,
+    )
+    att_own = to_owners(jnp.broadcast_to(message[None], (owners,) + message.shape))
+    up_rows = [input_proj[:, (3 + b) * width : (4 + b) * width] for b in range(GROUP)]
+    mlp_piece = jnp.concatenate(
+        [
+            blocks_of(up_rows[0], up_rows[2]),
+            blocks_of(up_rows[1], up_rows[3]),
+            blocks_of(mlp_down[: 2 * rows], mlp_down[2 * rows :]),
+        ],
+        axis=0,
+    ).astype(bf16)
+    att_own, mlp_piece = lax.optimization_barrier((att_own, mlp_piece))
+    att_other = swap(att_own, "group", 1)
+    mlp_near = gather_upper(mlp_piece[None])
+
+    notes = att_own[:, 2 * rows :].reshape(owners, -1)[:, :note_size].astype(f32)
+    bias_all = notes[:, :bias_shard].reshape(1, -1)
+    ids = 32.0 * notes[:, bias_shard : bias_shard + 2 * count] + notes[:, bias_shard + 2 * count :]
+    times_all = ids[:, :count].reshape(-1)
+    labels_all = ids[:, count:].reshape(-1).astype(jnp.int32)
     class_count = class_table.shape[0]
-    one_hot = (labels_rel[:, None] == jnp.arange(class_count, dtype=jnp.int32)[None, :]).astype(bf16)
-    condition = time_embed(times_rel, width) + dot(one_hot, class_table)
-    cond_rel = (condition * jax.nn.sigmoid(condition)).astype(bf16)
-    mod_at = 3 * width + hidden
+    one_hot = (labels_all[:, None] == jnp.arange(class_count, dtype=jnp.int32)[None, :]).astype(bf16)
+    condition = time_embed(times_all, width) + dot(one_hot, class_table)
+    cond_b = (condition * jax.nn.sigmoid(condition)).astype(bf16)
     w_mod = input_proj[:, mod_at:].astype(bf16)
-    cond_cols = lax.dynamic_slice_in_dim(cond_rel, me * rows, rows, 1)
+    cond_cols = lax.dynamic_slice_in_dim(cond_b, me * rows, rows, 1)
     partial = dot(cond_cols, w_mod).reshape(owners, count, -1)
-    bias_mod_at = 4 * width + hidden
-    modulation = scatter_upper(scatter_near(partial, f32), f32) + bias_all[:, bias_mod_at:]
+    modulation = jnp.sum(to_owners(partial), axis=0) + bias_all[:, bias_mod_at:]
     mod = modulation.reshape(count, 6, width)
-
-    att_blocks = [input_proj[:, b * width : (b + 1) * width] for b in range(3)] + [attn_proj]
-    up_blocks = [input_proj[:, (3 + b) * width : (4 + b) * width] for b in range(GROUP)]
-    down_blocks = [mlp_down[b * rows : (b + 1) * rows] for b in range(GROUP)]
-
-    def weights_of(blocks):
-        chosen = jnp.where(
-            mine < 2,
-            jnp.where(mine == 0, blocks[0], blocks[1]),
-            jnp.where(mine == 2, blocks[2], blocks[3]),
-        ).astype(bf16)
-        return list(group_gather(dp_gather(chosen)))
-
-    att_parts = weights_of(att_blocks)
-    up_parts = weights_of(up_blocks)
-    down_parts = weights_of(down_blocks)
+    mod, mlp_near = lax.optimization_barrier((mod, mlp_near))
+    mlp_far = swap(mlp_near, "dp", 1)
 
     qkv, attended, branch_a, lse = call(
         attn_forward, place,
-        [latents, mod], [bias_all] + att_parts,
+        [latents, mod], [bias_all, att_own, att_other],
         [
             like((count, seq_len, 3 * width), bf16),
             like((count, seq_len, width), bf16),
@@ -519,18 +570,24 @@
         [pltpu.VMEM((width, 4 * width), bf16), pltpu.VMEM((width, seq_len), f32)],
         count,
     )
-    kept = like((owners, 2, rows, width), f32)
-    sent = like((owners, 2, rows, width), bf16)
+    branch_a, mlp_near, mlp_far = lax.optimization_barrier((branch_a, mlp_near, mlp_far))
+    mlp_parts = [mlp_near, mlp_far, swap(mlp_near, "group", 1), swap(mlp_far, "group", 1)]
+    cond_group = [cond_cols] + [swap(cond_cols, "group", k) for k in (2, 1, 3)]
     bias_like = like((1, bias_mod_at), f32)
-    block_out, d_middle, d_mod_m, g_attn, g_bias_m, up_keep, up_send, dn_keep, dn_send = call(
+    block_out, d_middle, d_mod_m, g_attn, g_bias_m, mlp_keep, mlp_send = call(
         mlp_both, place,
-        [latents, cotangent, branch_a, attended, mod], [bias_all] + up_parts + down_parts,
+        [latents, cotangent, branch_a, attended, mod], [bias_all] + mlp_parts,
         [
             like((count, seq_len, width), bf16),
             like((count, seq_len, width), f32),
             like((count, 6, width), f32),
         ],
-        [like((width, width), f32), bias_like, kept, sent, kept, sent],
+        [
+            like((width, width), f32),
+            bias_like,
+            like((owners, 4, rows, width), f32),
+            like((owners, 4, rows, width), bf16),
+        ],
         [
             pltpu.VMEM((width, hidden), bf16),
             pltpu.VMEM((hidden, width), bf16),
@@ -543,15 +600,13 @@
         count,
         us=20,
     )
-    up_keep = up_keep + swap(up_send, "group", 1).astype(f32)
-    dn_keep = dn_keep + swap(dn_send, "group", 1).astype(f32)
-    d_middle, up_keep, dn_keep = lax.optimization_barrier((d_middle, up_keep, dn_keep))
+    mlp_keep = mlp_keep + swap(mlp_send, "group", 1).astype(f32)
+    d_middle, mlp_keep = lax.optimization_barrier((d_middle, mlp_keep))
 
     half = count // 2
     token_like = like((half, seq_len, width), f32)
     mod_like = like((half, 2, width), f32)
     gb_like = like((1, 2 * width), f32)
-    acc_like = like((width, 3 * width), f32)
     scratch = [
         pltpu.VMEM((width, 4 * width), bf16),
         pltpu.VMEM((width, seq_len), f32),
@@ -560,52 +615,64 @@
     token_args = [latents, d_middle, qkv, lse, mod]
     glat_0, d_mod_0, g_bias_a, acc = call(
         functools.partial(attn_backward, True, False), place,
-        token_args, att_parts,
-        [token_like, mod_like], [gb_like, acc_like], scratch, half, 0, 10,
-    )
-    up_keep = scatter_near(up_keep, bf16)
-    dn_keep = scatter_near(dn_keep, bf16)
-    acc, up_keep, dn_keep = lax.optimization_barrier((acc, up_keep, dn_keep))
+        token_args, [att_own, att_other],
+        [token_like, mod_like], [gb_like, like((width, 3 * width), f32)], scratch, half, 0, 10,
+    )
+    mlp_keep = scatter_near(mlp_keep, bf16)
+    acc, mlp_keep = lax.optimization_barrier((acc, mlp_keep))
     glat_1, d_mod_1, g_bias_a, at_keep, at_send = call(
         functools.partial(attn_backward, False, True), place,
-        token_args, att_parts + [acc, g_bias_a, g_attn],
-        [token_like, mod_like], [gb_like, kept, sent],
+        token_args, [att_own, att_other, acc, g_bias_a, g_attn],
+        [token_like, mod_like],
+        [gb_like, like((owners, 2, rows, width), f32), like((owners, 2, rows, width), bf16)],
         scratch + [pltpu.VMEM((width, 3 * width), f32)], count - half, half, 10,
     )
-    up_total = scatter_upper(up_keep, bf16)
-    dn_total = scatter_upper(dn_keep, bf16)
-    at_send, up_total, dn_total = lax.optimization_barrier((at_send, up_total, dn_total))
-    at_keep = at_keep + swap(at_send, "group", 1).astype(f32)
-    at_total = scatter_upper(scatter_near(at_keep, bf16), bf16)
+    mlp_total = scatter_upper(mlp_keep, bf16)
     grad_latents = jnp.concatenate([glat_0, glat_1], axis=0)
 
     d_mod_a = jnp.concatenate([d_mod_0, d_mod_1], axis=0)
     d_modulation = jnp.concatenate([d_mod_a, d_mod_m[:, 2:]], axis=1).reshape(count, 6 * width)
-    d_modulation_b = d_modulation.astype(bf16)
     bias_grad = jnp.concatenate(
+        [g_bias_a[0], g_bias_m[0, 2 * width :], jnp.sum(d_modulation, axis=0)]
+    )
+    at_keep = at_keep + swap(at_send, "group", 1).astype(f32)
+    bias_grad = (bias_grad + swap(bias_grad, "group", 2)) + (
+        swap(bias_grad, "group", 1) + swap(bias_grad, "group", 3)
+    )
+
+    dm_rows = count * 6
+    bias_halves = halves(bias_grad.reshape(owners, bias_shard))
+    tail_rows = -(-2 * bias_shard // width)
+    tail_rows += -(2 * rows + dm_rows + tail_rows) % 8
+    message = jnp.concatenate(
         [
-            g_bias_a[0],
-            g_bias_m[0, 2 * width :],
-            jnp.sum(d_modulation, axis=0),
-        ]
-    )
-    dm_rel = dp_gather(d_modulation_b).reshape(owners * count, 6 * width)
-    dm_all = jnp.concatenate(group_gather(dm_rel), axis=0)
-    cond_all = jnp.concatenate(group_gather(cond_cols), axis=0)
-    g_mod = dot(cond_all, dm_all, TN)
-
-    back = dp_gather(dot(dm_rel, w_mod, NT))
-    back = back.reshape(owners, owners, count, rows)
-    back = jnp.stack([back[s, s] for s in range(owners)])
-    back = jnp.take(back, absolute, axis=0)
+            at_keep.astype(bf16).reshape(owners, 2 * rows, width),
+            jnp.broadcast_to(
+                d_modulation.astype(bf16).reshape(1, dm_rows, width), (owners, dm_rows, width)
+            ),
+            pad_rows(bias_halves, width, tail_rows),
+        ],
+        axis=1,
+    )
+    message, mlp_total = lax.optimization_barrier((message, mlp_total))
+    mlp_shared = share_parts(mlp_total)
+    arrived = to_owners(message)
+    at_total = jnp.sum(arrived[:, : 2 * rows].astype(f32), axis=0).reshape(2, rows, width)
+    at_shared = share_parts(at_total)
+    dm_all = arrived[:, 2 * rows : 2 * rows + dm_rows].reshape(owners * count, 6 * width)
+    dm_group = group_gather(dm_all)
+    g_halves = jnp.sum(
+        arrived[:, 2 * rows + dm_rows :].reshape(owners, -1)[:, : 2 * bias_shard].astype(f32), axis=0
+    )
+    g_biases = g_halves[:bias_shard] + g_halves[bias_shard:]
+    bias_out = (g_biases,) + adam_parts(biases, mean_biases, sq_biases, g_biases)
+
+    back = dot(dm_all, w_mod, NT).reshape(owners, count, rows)
+    back = to_owners(back)
     d_cond = back.transpose(1, 0, 2).reshape(count, width)
-    own_cond = condition[:count]
+    own_cond = lax.dynamic_slice_in_dim(condition, me * count, count, 0)
     own_sig = jax.nn.sigmoid(own_cond)
     grad_cond = d_cond * (own_sig * (1.0 + own_cond * (1.0 - own_sig)))
-
-    parts = share_parts(at_total) + share_parts(up_total) + share_parts(dn_total)
-    g_biases = lax.dynamic_slice_in_dim(sum_all(bias_grad), me * bias_shard, bias_shard, 0)
-    bias_out = (g_biases,) + adam_parts(biases, mean_biases, sq_biases, g_biases)
 
     steps = rows // 16 if rows % 16 == 0 else 1
     block_rows = rows // steps
@@ -613,7 +680,7 @@
     def spec_of(array):
         if len(array.shape) == 3:
             return pl.BlockSpec((array.shape[0], block_rows, width), lambda s, *_: (0, s, 0))
-        return pl.BlockSpec((block_rows, array.shape[1]), lambda s, *_: (s, 0))
+        return pl.BlockSpec((block_rows, min(array.shape[1], mod_at)), lambda s, *_: (s, 0))
 
     state = [
         entry
@@ -624,7 +691,7 @@
         )
         for entry in (three[0], three[1], three[2].reshape(GROUP, rows, width))
     ]
-    args = parts + [g_mod] + state
+    args = at_shared + mlp_shared + state
     results = [like(a.shape, f32) for a in state[:3]] * 4
     outs = pl.pallas_call(
         adam_kernel,
@@ -639,9 +706,25 @@
         name="adam",
     )(place, *args)
 
+    g_mod = dot(in_order(cond_group, mine), in_order(dm_group, mine), TN)
+    first = mod_at // width
+    local = pl.BlockSpec((rows, width), lambda s: (0, s))
+    placed = pl.BlockSpec((rows, width), lambda s: (0, s + first))
+    anywhere = pl.BlockSpec(memory_space=pl.ANY)
+    wide = pl.pallas_call(
+        adam_mod,
+        grid=(6,),
+        in_specs=[local] + [placed] * 3 + [anywhere] * 4,
+        out_specs=[placed] * 4,
+        out_shape=[like(input_proj.shape, f32)] * 4,
+        input_output_aliases={4 + i: i for i in range(4)},
+        compiler_params=compiler(),
+        name="adam_mod",
+    )(g_mod, input_proj, mean_input, sq_input, outs[0], outs[3], outs[6], outs[9])
+
     def flat(index):
         three = outs[3 * index : 3 * index + 3]
-        return (three[0], three[1], three[2].reshape(mlp_down.shape), bias_out[index])
+        return (wide[index], three[1], three[2].reshape(mlp_down.shape), bias_out[index])
 
     return (block_out, grad_latents, grad_cond) + flat(0) + flat(1) + flat(2) + flat(3)
 

time: 219 us -> 214 us (0.977)
  starting transfers between devices: 70.3 us -> 42.1 us
  waiting for transfers between devices: 44.3 us -> 65 us
  local copies, waits for them, and re-layouts: 15.8 us -> 9.12 us
  other arithmetic: 16 us -> 22.3 us
  Pallas kernels: 67.1 us -> 70.5 us
    ppermute x72 -> x28, starting transfers between devices: 70.3 us -> 23.5 us  [swap(): return lax.ppermute(value, axis, [(i, i ^ bit) for i in range(size)])]
    all_to_all x0 -> x4, waiting for transfers between devices: none -> 29.8 us  [to_owners(): return lax.all_to_all(value, 'dp', 0, 0, tiled=True)]
    all_to_all x0 -> x4, starting transfers between devices: none -> 18.5 us  [to_owners(): return lax.all_to_all(value, 'dp', 0, 0, tiled=True)]
    ppermute x72 -> x28, waiting for transfers between devices: 44.3 us -> 35.2 us  [swap(): return lax.ppermute(value, axis, [(i, i ^ bit) for i in range(size)])]
    unnamed x90 -> x57, local copies, waits for them, and re-layouts: 7.39 us -> 2.37 us
    pallas_call x0 -> x1, Pallas kernels: none -> 4.73 us  [body(): pl.pallas_call(adam_mod, grid=(6,), in_specs=[local] + [placed] * 3 + [an...]
    unnamed x2 -> x0, other arithmetic: 3.42 us -> none
  transfers between devices with their start and end apart: 72 -> 32, of which waited for: 20 -> 14; matrix products, arithmetic and copies ran while one was open for 12% -> 8% of each run, Pallas kernels for 12% -> 15%
where the time goes in v2:
time: 214 us; the launch traced here: 212 us
  Pallas kernels  70.5 us (33%)
  waiting for transfers between devices  65 us (30%)
  starting transfers between devices  42.1 us (20%)
  other arithmetic  22.3 us (10%)
  local copies, waits for them, and re-layouts  9.12 us (4%)
    pallas_call x4, Pallas kernels, call(): pl.pallas_call(kernel, grid_spec=pltpu.PrefetchScalarGridSpec(num_scalar_...  59.9 us
    ppermute x28, waiting for transfers between devices, swap(): return lax.ppermute(value, axis, [(i, i ^ bit) for i in range(size)])  35.2 us
    all_to_all x4, waiting for transfers between devices, to_owners(): return lax.all_to_all(value, 'dp', 0, 0, tiled=True)  29.8 us
    ppermute x28, starting transfers between devices, swap(): return lax.ppermute(value, axis, [(i, i ^ bit) for i in range(size)])  23.5 us
    all_to_all x4, starting transfers between devices, to_owners(): return lax.all_to_all(value, 'dp', 0, 0, tiled=True)  18.5 us
    pallas_call x1, Pallas kernels, body(): pl.pallas_call(adam_kernel, grid_spec=pltpu.PrefetchScalarGridSpec(num_sc...  5.91 us
    pallas_call x1, Pallas kernels, body(): pl.pallas_call(adam_mod, grid=(6,), in_specs=[local] + [placed] * 3 + [an...  4.73 us
  transfers between devices with their start and end apart: 32, of which 14 were waited for; matrix products, arithmetic and copies ran while one was open for 8% of the time, Pallas kernels for 15%

profile of v2, /device:TPU:0, one launch (start us, length us, event | category | flops | bytes accessed | tf_op | source)
XLA Modules:
  0.0 212.1 jit_solution(6193664884628569763)
XLA Ops:
  4.4 7.4 %all-to-all-start = ((bf16[8,104,384]{2,1,0:T(8,128)(2,1)}), bf16[8,104,384]{2,1,0:T(8,128)(2,1)S(1)}, u32[]{:S(2)}, u32[]{:S(2)}) async-start(bf16[8,104,384]{2,1,0:T(8,128)(2,1)} %broadcast_in_dim.6), calls=%async_computation | async-start | bytes 1277952 | tf_op jit(solution)/shard_map/all_to_all | solution.py:433
  11.9 16.9 %all-to-all-done.own = bf16[8,104,384]{2,1,0:T(8,128)(2,1)S(1)} async-done(((bf16[8,104,384]{2,1,0:T(8,128)(2,1)}), bf16[8,104,384]{2,1,0:T(8,128)(2,1)S(1)}, u32[]{:S(2)}, u32[]{:S(2)}) %all-to-all-start) | async-done | bytes 639008 | tf_op jit(solution)/shard_map/all_to_all | solution.py:433
  30.8 3.6 %all-to-all-start.1 = ((f32[8,4,2304]{2,1,0:T(4,128)}), f32[8,4,2304]{2,1,0:T(4,128)S(1)}, u32[]{:S(2)}, u32[]{:S(2)}) async-start(f32[8,4,2304]{2,1,0:T(4,128)} %reshape.195), calls=%async_computation.1 | async-start | bytes 589824 | tf_op jit(solution)/shard_map/all_to_all | solution.py:433
  34.5 2.0 collective-permute-start
  36.5 2.4 %collective-permute-start.1 = (bf16[1,192,384]{2,1,0:T(8,128)(2,1)S(1)}, bf16[1,192,384]{2,1,0:T(8,128)(2,1)}, u32[]{:S(2)}, u32[]{:S(2)}) collective-permute-start(bf16[1,192,384]{2,1,0:T(8,128)(2,1)S(1)} %bitcast.49), channel_id=1, source_target_pairs={{0,16},{4,20},{8,24},{12,28},{16,0},{20,4},{24,8},{28,12},{1,17},{... | collective-permute-start | bytes 442376 | tf_op jit(solution)/shard_map/ppermute | solution.py:372
  40.3 6.5 %collective-permute-done = bf16[1,192,384]{2,1,0:T(8,128)(2,1)S(1)} collective-permute-done((bf16[1,192,384]{2,1,0:T(8,128)(2,1)S(1)}, bf16[1,192,384]{2,1,0:T(8,128)(2,1)S(1)}, u32[]{:S(2)}, u32[]{:S(2)}) %collective-permute-start) | collective-permute-done | bytes 147488 | tf_op jit(solution)/shard_map/ppermute | solution.py:372
  46.8 8.1 %collective-permute-done.1 = bf16[1,192,384]{2,1,0:T(8,128)(2,1)} collective-permute-done((bf16[1,192,384]{2,1,0:T(8,128)(2,1)S(1)}, bf16[1,192,384]{2,1,0:T(8,128)(2,1)}, u32[]{:S(2)}, u32[]{:S(2)}) %collective-permute-start.1) | collective-permute-done | bytes 147488 | tf_op jit(solution)/shard_map/ppermute | solution.py:372
  58.8 14.7 %attn_forward.1 = (bf16[4,256,1152]{2,1,0:T(8,128)(2,1)}, bf16[4,256,384]{2,1,0:T(8,128)(2,1)}, f32[4,256,384]{2,1,0:T(8,128)}, f32[4,6,256]{2,1,0:T(8,128)}) custom-call(s32[2]{0:T(128)} %pad_add_fusion.place, bf16[4,256,384]{2,1,0:T(8,128)(2,1)} %lat.7, f32[4,6,384]{2,1,0:T(8,128)} %broadcast_add_fusion.mod, f32[1,5376]{1,0:T(1,128)} %copy-done.14, ...), custom_call_target="tpu_custom_call" | custom-call | flops 15000000512 | bytes 15000000 | tf_op jit(solution)/shard_map/attn_forward/pallas_call | solution.py:470
  74.1 1.5 collective-permute-done.5.other_near
  77.2 21.3 %mlp_both.1 = (bf16[4,256,384]{2,1,0:T(8,128)(2,1)}, f32[4,256,384]{2,1,0:T(8,128)}, f32[4,6,384]{2,1,0:T(8,128)}, f32[384,384]{1,0:T(8,128)}, f32[1,3072]{1,0:T...) custom-call(s32[2]{0:T(128)} %pad_add_fusion.place, bf16[4,256,384]{2,1,0:T(8,128)(2,1)} %lat.7, ...), custom_call_target="tpu_custom_call" | custom-call | flops 20000000000 | bytes 20000000 | tf_op jit(solution)/shard_map/mlp_both/pallas_call | solution.py:470
  101.7 1.9 convert_add_fusion
  104.6 11.2 %attn_backward.2 = (f32[2,256,384]{2,1,0:T(8,128)}, f32[2,2,384]{2,1,0:T(2,128)}, f32[1,768]{1,0:T(1,128)}, f32[384,1152]{1,0:T(8,128)}) custom-call(s32[2]{0:T(128)} %pad_add_fusion.place, bf16[4,256,384]{2,1,0:T(8,128)(2,1)} %lat.7, f32[4,256,384]{2,1,0:T(8,128)} %get-tuple-element.81.dmid, bf16[4,256,1152]{2,1,0:T(8,128)(2,1)} %get-tuple-element.82.qkv, ...), custom_call_target="tpu_custom_call" | custom-call | flops 10000000000 | bytes 10000000 | tf_op jit(solution)/shard_map/attn_backward/pallas_call | solution.py:470
  115.7 3.4 %collective-permute-done.8 = bf16[4,4,48,384]{3,2,1,0:T(8,128)(2,1)S(1)} collective-permute-done((bf16[4,4,48,384]{3,2,1,0:T(8,128)(2,1)S(1)}, bf16[4,4,48,384]{3,2,1,0:T(8,128)(2,1)S(1)}, u32[]{:S(2)}, u32[]{:S(2)}) %collective-permute-start.8) | collective-permute-done | bytes 589856 | tf_op jit(solution)/shard_map/ppermute | solution.py:372
  119.3 12.7 %attn_backward.3 = (f32[2,256,384]{2,1,0:T(8,128)}, f32[2,2,384]{2,1,0:T(2,128)}, f32[1,768]{1,0:T(1,128)}, f32[8,2,48,384]{3,2,1,0:T(8,128)}, bf16[8,2,48,384]{3,2,1,0:T(8,128)(2,1)}) custom-call(s32[2]{0:T(128)} %pad_add_fusion.place, bf16[4,256,384]{2,1,0:T(8,128)(2,1)} %lat.7, f32[4,256,384]{2,1,0:T(8,128)} %get-tuple-element.81.dmid, ...), custom_call_target="tpu_custom_call" | custom-call | flops 10000000000 | bytes 10000000 | tf_op jit(solution)/shard_map/attn_backward/pallas_call | solution.py:470
  133.5 1.6 collective-permute-start.10
  135.8 2.8 %collective-permute-start.13 = (bf16[4,48,384]{2,1,0:T(8,128)(2,1)S(1)}, bf16[4,48,384]{2,1,0:T(8,128)(2,1)}, u32[]{:S(2)}, u32[]{:S(2)}) collective-permute-start(bf16[4,48,384]{2,1,0:T(8,128)(2,1)S(1)} %get-tuple-element.131), channel_id=1, source_target_pairs={{0,8},{4,12},{8,0},{12,4},{16,24},{20,28},{24,16},{28,20},{1,9},{5... | collective-permute-start | bytes 442376 | tf_op jit(solution)/shard_map/ppermute | solution.py:372
  138.7 2.4 %collective-permute-start.15 = (bf16[4,48,384]{2,1,0:T(8,128)(2,1)S(1)}, bf16[4,48,384]{2,1,0:T(8,128)(2,1)}, u32[]{:S(2)}, u32[]{:S(2)}) collective-permute-start(bf16[4,48,384]{2,1,0:T(8,128)(2,1)S(1)} %get-tuple-element.132), channel_id=1, source_target_pairs={{0,24},{4,28},{8,16},{12,20},{16,8},{20,12},{24,0},{28,4},{1,25},{... | collective-permute-start | bytes 442376 | tf_op jit(solution)/shard_map/ppermute | solution.py:372
  142.1 2.4 %collective-permute-done.13 = bf16[4,48,384]{2,1,0:T(8,128)(2,1)} collective-permute-done((bf16[4,48,384]{2,1,0:T(8,128)(2,1)S(1)}, bf16[4,48,384]{2,1,0:T(8,128)(2,1)}, u32[]{:S(2)}, u32[]{:S(2)}) %collective-permute-start.13) | collective-permute-done | bytes 147488 | tf_op jit(solution)/shard_map/ppermute | solution.py:372
  144.5 8.1 %collective-permute-done.14 = bf16[4,48,384]{2,1,0:T(8,128)(2,1)} collective-permute-done((bf16[4,48,384]{2,1,0:T(8,128)(2,1)S(1)}, bf16[4,48,384]{2,1,0:T(8,128)(2,1)}, u32[]{:S(2)}, u32[]{:S(2)}) %collective-permute-start.14) | collective-permute-done | bytes 147488 | tf_op jit(solution)/shard_map/ppermute | solution.py:372
  153.7 1.6 add_convert_fusion
  156.3 3.9 %all-to-all-start.2 = ((bf16[8,128,384]{2,1,0:T(8,128)(2,1)}), bf16[8,128,384]{2,1,0:T(8,128)(2,1)S(1)}, u32[]{:S(2)}, u32[]{:S(2)}) async-start(bf16[8,128,384]{2,1,0:T(8,128)(2,1)} %pad_maximum_fusion.1), calls=%async_computation.2 | async-start | bytes 1572864 | tf_op jit(solution)/shard_map/all_to_all | solution.py:433
  160.2 1.6 collective-permute-start.16
  162.4 1.5 collective-permute-done.16
  167.3 2.5 %pad_maximum_fusion = f32[4,256,384]{2,1,0:T(8,128)} fusion(f32[2,256,384]{2,1,0:T(8,128)} %get-tuple-element.90, f32[2,256,384]{2,1,0:T(8,128)S(1)} %copy-done.2), kind=kLoop, calls=%fused_computation.1 | loop fusion | flops 393216 | bytes 3145728 | tf_op jit(solution)/shard_map/concatenate | solution.py:631
  171.9 7.8 %all-to-all-done.2 = bf16[8,128,384]{2,1,0:T(8,128)(2,1)S(1)} async-done(((bf16[8,128,384]{2,1,0:T(8,128)(2,1)}), bf16[8,128,384]{2,1,0:T(8,128)(2,1)S(1)}, u32[]{:S(2)}, u32[]{:S(2)}) %all-to-all-start.2) | async-done | bytes 786464 | tf_op jit(solution)/shard_map/all_to_all | solution.py:433
  180.1 1.6 collective-permute-start.22
  183.1 3.5 %all-to-all-start.3 = ((f32[8,1,192]{2,1,0:T(1,128)}), f32[8,1,192]{2,1,0:T(1,128)S(1)}, u32[]{:S(2)}, u32[]{:S(2)}) async-start(f32[8,1,192]{2,1,0:T(1,128)} %reshape.215), calls=%async_computation.3 | async-start | bytes 16384 | tf_op jit(solution)/shard_map/all_to_all | solution.py:433
  186.7 1.4 divide_subtract_fusion
  188.1 5.1 %all-to-all-done.3 = f32[8,1,192]{2,1,0:T(1,128)S(1)} async-done(((f32[8,1,192]{2,1,0:T(1,128)}), f32[8,1,192]{2,1,0:T(1,128)S(1)}, u32[]{:S(2)}, u32[]{:S(2)}) %all-to-all-start.3) | async-done | bytes 6176 | tf_op jit(solution)/shard_map/all_to_all | solution.py:433
  194.6 1.6 collective-permute-start.24
  199.3 5.9 %adam.1 = (f32[48,4992]{1,0:T(8,128)}, f32[48,384]{1,0:T(8,128)}, f32[4,48,384]{2,1,0:T(8,128)}, f32[48,4992]{1,0:T(8,128)}, f32[48,384]{1,0:T(8,128)}, /*index=...) custom-call(s32[2]{0:T(128)} %pad_add_fusion.place, ...), custom_call_target="tpu_custom_call" | custom-call | tf_op jit(solution)/shard_map/adam/pallas_call | solution.py:696
  207.3 4.7 %adam_mod.1 = (f32[48,4992]{1,0:T(8,128)}, f32[48,4992]{1,0:T(8,128)}, f32[48,4992]{1,0:T(8,128)}, f32[48,4992]{1,0:T(8,128)}) custom-call(f32[48,2304]{1,0:T(8,128)} %fusion.grad, f32[48,4992]{1,0:T(8,128)} %weight.1, f32[48,4992]{1,0:T(8,128)} %mean.1, f32[48,4992]{1,0:T(8,128)} %square.1, ...), custom_call_target="tpu_custom_call", output_to_operand_aliasing={{0}: (4, {}), {1}: (5, {}), {2}: (6, {}), {3}: (7, {})} | custom-call | tf_op jit(solution)/shard_map/adam_mod/pallas_call | solution.py:714
  (166 shorter events, 37.1 us)
Async XLA Ops:
  4.4 24.4 %all-to-all-start = ((bf16[8,104,384]{2,1,0:T(8,128)(2,1)}), bf16[8,104,384]{2,1,0:T(8,128)(2,1)S(1)}, u32[]{:S(2)}, u32[]{:S(2)}) async-start(bf16[8,104,384]{2,1,0:T(8,128)(2,1)} %broadcast_in_dim.6), calls=%async_computation | async-start | bytes 1277952 | tf_op jit(solution)/shard_map/all_to_all | solution.py:433
  30.8 25.3 %all-to-all-start.1 = ((f32[8,4,2304]{2,1,0:T(4,128)}), f32[8,4,2304]{2,1,0:T(4,128)S(1)}, u32[]{:S(2)}, u32[]{:S(2)}) async-start(f32[8,4,2304]{2,1,0:T(4,128)} %reshape.195), calls=%async_computation.1 | async-start | bytes 589824 | tf_op jit(solution)/shard_map/all_to_all | solution.py:433
  34.4 24.4 %collective-permute-start.3 = (bf16[8,104,384]{2,1,0:T(8,128)(2,1)S(1)}, bf16[8,104,384]{2,1,0:T(8,128)(2,1)}, u32[]{:S(2)}, u32[]{:S(2)}) collective-permute-start(bf16[8,104,384]{2,1,0:T(8,128)(2,1)S(1)} %all-to-all-done.own), channel_id=1, source_target_pairs={{0,1},{1,0},{2,3},{3,2},{4,5},{5,4},{6,7},{7,6},{8,9},{9,8},{10,11... | collective-permute-start | bytes 1916936 | tf_op jit(solution)/shard_map/ppermute | solution.py:372
  34.5 12.4 %collective-permute-start = (bf16[1,192,384]{2,1,0:T(8,128)(2,1)S(1)}, bf16[1,192,384]{2,1,0:T(8,128)(2,1)S(1)}, u32[]{:S(2)}, u32[]{:S(2)}) collective-permute-start(bf16[1,192,384]{2,1,0:T(8,128)(2,1)S(1)} %bitcast.48), channel_id=1, source_target_pairs={{0,8},{4,12},{8,0},{12,4},{16,24},{20,28},{24,16},{28,20},{1,9},{5... | collective-permute-start | bytes 442376 | tf_op jit(solution)/shard_map/ppermute | solution.py:372
  36.5 18.5 %collective-permute-start.1 = (bf16[1,192,384]{2,1,0:T(8,128)(2,1)S(1)}, bf16[1,192,384]{2,1,0:T(8,128)(2,1)}, u32[]{:S(2)}, u32[]{:S(2)}) collective-permute-start(bf16[1,192,384]{2,1,0:T(8,128)(2,1)S(1)} %bitcast.49), channel_id=1, source_target_pairs={{0,16},{4,20},{8,24},{12,28},{16,0},{20,4},{24,8},{28,12},{1,17},{... | collective-permute-start | bytes 442376 | tf_op jit(solution)/shard_map/ppermute | solution.py:372
  38.9 16.1 %collective-permute-start.2 = (bf16[1,192,384]{2,1,0:T(8,128)(2,1)S(1)}, bf16[1,192,384]{2,1,0:T(8,128)(2,1)}, u32[]{:S(2)}, u32[]{:S(2)}) collective-permute-start(bf16[1,192,384]{2,1,0:T(8,128)(2,1)S(1)} %bitcast.50), channel_id=1, source_target_pairs={{0,24},{4,28},{8,16},{12,20},{16,8},{20,12},{24,0},{28,4},{1,25},{... | collective-permute-start | bytes 442376 | tf_op jit(solution)/shard_map/ppermute | solution.py:372
  57.5 15.9 %collective-permute-start.4 = (bf16[4,192,384]{2,1,0:T(8,128)(2,1)S(1)}, bf16[4,192,384]{2,1,0:T(8,128)(2,1)S(1)}, u32[]{:S(2)}, u32[]{:S(2)}) collective-permute-start(bf16[4,192,384]{2,1,0:T(8,128)(2,1)S(1)} %pad_maximum_fusion.2.own_near), channel_id=1, source_target_pairs={{0,4},{4,0},{8,12},{12,8},{16,20},{20,16},{24,28},{28,24},{1,5},{5... | collective-permute-start | bytes 1769480 | tf_op jit(solution)/shard_map/ppermute | solution.py:372
  73.5 2.1 collective-permute-start.5
  73.6 2.8 %collective-permute-start.6 = (bf16[4,192,384]{2,1,0:T(8,128)(2,1)S(1)}, bf16[4,192,384]{2,1,0:T(8,128)(2,1)S(1)}, u32[]{:S(2)}, u32[]{:S(2)}) collective-permute-start(bf16[4,192,384]{2,1,0:T(8,128)(2,1)S(1)} %collective-permute-done.4.own_far), channel_id=1, source_target_pairs={{0,1},{1,0},{2,3},{3,2},{4,5},{5,4},{6,7},{7,6},{8,9},{9,8},{10,11... | collective-permute-start | bytes 1769480 | tf_op jit(solution)/shard_map/ppermute | solution.py:372
  98.5 3.1 %collective-permute-start.7 = (bf16[8,4,48,384]{3,2,1,0:T(8,128)(2,1)}, bf16[8,4,48,384]{3,2,1,0:T(8,128)(2,1)S(1)}, u32[]{:S(2)}, u32[]{:S(2)}) collective-permute-start(bf16[8,4,48,384]{3,2,1,0:T(8,128)(2,1)} %get-tuple-element.80), channel_id=1, source_target_pairs={{0,1},{1,0},{2,3},{3,2},{4,5},{5,4},{6,7},{7,6},{8,9},{9,8},{10,11... | collective-permute-start | bytes 3538952 | tf_op jit(solution)/shard_map/ppermute | solution.py:372
  103.7 15.4 %collective-permute-start.8 = (bf16[4,4,48,384]{3,2,1,0:T(8,128)(2,1)S(1)}, bf16[4,4,48,384]{3,2,1,0:T(8,128)(2,1)S(1)}, u32[]{:S(2)}, u32[]{:S(2)}) collective-permute-start(bf16[4,4,48,384]{3,2,1,0:T(8,128)(2,1)S(1)} %slice.183), channel_id=1, source_target_pairs={{0,4},{4,0},{8,12},{12,8},{16,20},{20,16},{24,28},{28,24},{1,5},{5... | collective-permute-start | bytes 1769480 | tf_op jit(solution)/shard_map/ppermute | solution.py:372
  133.5 5.2 %collective-permute-start.10 = (f32[5376]{0:T(1024)S(1)}, f32[5376]{0:T(1024)S(1)}, u32[]{:S(2)}, u32[]{:S(2)}) collective-permute-start(f32[5376]{0:T(1024)S(1)} %pad_maximum_fusion.6), channel_id=1, source_target_pairs={{0,2},{1,3},{2,0},{3,1},{4,6},{5,7},{6,4},{7,5},{8,10},{9,11},{10,... | collective-permute-start | bytes 64520 | tf_op jit(solution)/shard_map/ppermute | solution.py:372
  135.0 6.1 %collective-permute-start.11 = (f32[5376]{0:T(1024)S(1)}, f32[5376]{0:T(1024)S(1)}, u32[]{:S(2)}, u32[]{:S(2)}) collective-permute-start(f32[5376]{0:T(1024)S(1)} %pad_maximum_fusion.6), channel_id=1, source_target_pairs={{0,1},{1,0},{2,3},{3,2},{4,5},{5,4},{6,7},{7,6},{8,9},{9,8},{10,11... | collective-permute-start | bytes 64520 | tf_op jit(solution)/shard_map/ppermute | solution.py:372
  135.0 6.1 %collective-permute-start.12 = (f32[5376]{0:T(1024)S(1)}, f32[5376]{0:T(1024)}, u32[]{:S(2)}, u32[]{:S(2)}) collective-permute-start(f32[5376]{0:T(1024)S(1)} %pad_maximum_fusion.6), channel_id=1, source_target_pairs={{0,3},{1,2},{2,1},{3,0},{4,7},{5,6},{6,5},{7,4},{8,11},{9,10},{10,... | collective-permute-start | bytes 64520 | tf_op jit(solution)/shard_map/ppermute | solution.py:372
  135.8 8.6 %collective-permute-start.13 = (bf16[4,48,384]{2,1,0:T(8,128)(2,1)S(1)}, bf16[4,48,384]{2,1,0:T(8,128)(2,1)}, u32[]{:S(2)}, u32[]{:S(2)}) collective-permute-start(bf16[4,48,384]{2,1,0:T(8,128)(2,1)S(1)} %get-tuple-element.131), channel_id=1, source_target_pairs={{0,8},{4,12},{8,0},{12,4},{16,24},{20,28},{24,16},{28,20},{1,9},{5... | collective-permute-start | bytes 442376 | tf_op jit(solution)/shard_map/ppermute | solution.py:372
  138.6 13.9 %collective-permute-start.14 = (bf16[4,48,384]{2,1,0:T(8,128)(2,1)S(1)}, bf16[4,48,384]{2,1,0:T(8,128)(2,1)}, u32[]{:S(2)}, u32[]{:S(2)}) collective-permute-start(bf16[4,48,384]{2,1,0:T(8,128)(2,1)S(1)} %get-tuple-element.133), channel_id=1, source_target_pairs={{0,16},{4,20},{8,24},{12,28},{16,0},{20,4},{24,8},{28,12},{1,17},{... | collective-permute-start | bytes 442376 | tf_op jit(solution)/shard_map/ppermute | solution.py:372
  138.7 13.8 %collective-permute-start.15 = (bf16[4,48,384]{2,1,0:T(8,128)(2,1)S(1)}, bf16[4,48,384]{2,1,0:T(8,128)(2,1)}, u32[]{:S(2)}, u32[]{:S(2)}) collective-permute-start(bf16[4,48,384]{2,1,0:T(8,128)(2,1)S(1)} %get-tuple-element.132), channel_id=1, source_target_pairs={{0,24},{4,28},{8,16},{12,20},{16,8},{20,12},{24,0},{28,4},{1,25},{... | collective-permute-start | bytes 442376 | tf_op jit(solution)/shard_map/ppermute | solution.py:372
  141.2 12.5 %collective-permute-start.9 = (bf16[8,2,48,384]{3,2,1,0:T(8,128)(2,1)}, bf16[8,2,48,384]{3,2,1,0:T(8,128)(2,1)}, u32[]{:S(2)}, u32[]{:S(2)}) collective-permute-start(bf16[8,2,48,384]{3,2,1,0:T(8,128)(2,1)} %get-tuple-element.92), channel_id=1, source_target_pairs={{0,1},{1,0},{2,3},{3,2},{4,5},{5,4},{6,7},{7,6},{8,9},{9,8},{10,11... | collective-permute-start | bytes 1769480 | tf_op jit(solution)/shard_map/ppermute | solution.py:372
  156.3 23.4 %all-to-all-start.2 = ((bf16[8,128,384]{2,1,0:T(8,128)(2,1)}), bf16[8,128,384]{2,1,0:T(8,128)(2,1)S(1)}, u32[]{:S(2)}, u32[]{:S(2)}) async-start(bf16[8,128,384]{2,1,0:T(8,128)(2,1)} %pad_maximum_fusion.1), calls=%async_computation.2 | async-start | bytes 1572864 | tf_op jit(solution)/shard_map/all_to_all | solution.py:433
  160.2 3.7 %collective-permute-start.16 = (bf16[32,48]{1,0:T(8,128)(2,1)S(1)}, bf16[32,48]{1,0:T(8,128)(2,1)S(1)}, u32[]{:S(2)}, u32[]{:S(2)}) collective-permute-start(bf16[32,48]{1,0:T(8,128)(2,1)S(1)} %copy-done.16), channel_id=1, source_target_pairs={{0,2},{1,3},{2,0},{3,1},{4,6},{5,7},{6,4},{7,5},{8,10},{9,11},{10,... | collective-permute-start | bytes 9224 | tf_op jit(solution)/shard_map/ppermute | solution.py:372
  161.8 2.1 %collective-permute-start.17 = (bf16[32,48]{1,0:T(8,128)(2,1)S(1)}, bf16[32,48]{1,0:T(8,128)(2,1)S(1)}, u32[]{:S(2)}, u32[]{:S(2)}) collective-permute-start(bf16[32,48]{1,0:T(8,128)(2,1)S(1)} %copy-done.16), channel_id=1, source_target_pairs={{0,1},{1,0},{2,3},{3,2},{4,5},{5,4},{6,7},{7,6},{8,9},{9,8},{10,11... | collective-permute-start | bytes 9224 | tf_op jit(solution)/shard_map/ppermute | solution.py:372
  161.8 3.1 %collective-permute-start.18 = (bf16[32,48]{1,0:T(8,128)(2,1)S(1)}, bf16[32,48]{1,0:T(8,128)(2,1)S(1)}, u32[]{:S(2)}, u32[]{:S(2)}) collective-permute-start(bf16[32,48]{1,0:T(8,128)(2,1)S(1)} %copy-done.16), channel_id=1, source_target_pairs={{0,3},{1,2},{2,1},{3,0},{4,7},{5,6},{6,5},{7,4},{8,11},{9,10},{10,... | collective-permute-start | bytes 9224 | tf_op jit(solution)/shard_map/ppermute | solution.py:372
  169.8 24.7 %collective-permute-start.25 = (bf16[4,48,384]{2,1,0:T(8,128)(2,1)S(1)}, bf16[4,48,384]{2,1,0:T(8,128)(2,1)S(1)}, u32[]{:S(2)}, u32[]{:S(2)}) collective-permute-start(bf16[4,48,384]{2,1,0:T(8,128)(2,1)S(1)} %fusion.9.refs_4_), channel_id=1, source_target_pairs={{0,2},{1,3},{2,0},{3,1},{4,6},{5,7},{6,4},{7,5},{8,10},{9,11},{10,... | collective-permute-start | bytes 442376 | tf_op jit(solution)/shard_map/ppermute | solution.py:372
  170.4 24.2 %collective-permute-start.26 = (bf16[4,48,384]{2,1,0:T(8,128)(2,1)S(1)}, bf16[4,48,384]{2,1,0:T(8,128)(2,1)S(1)}, u32[]{:S(2)}, u32[]{:S(2)}) collective-permute-start(bf16[4,48,384]{2,1,0:T(8,128)(2,1)S(1)} %fusion.9.refs_4_), channel_id=1, source_target_pairs={{0,1},{1,0},{2,3},{3,2},{4,5},{5,4},{6,7},{7,6},{8,9},{9,8},{10,11... | collective-permute-start | bytes 442376 | tf_op jit(solution)/shard_map/ppermute | solution.py:372
  170.8 25.4 %collective-permute-start.27 = (bf16[4,48,384]{2,1,0:T(8,128)(2,1)S(1)}, bf16[4,48,384]{2,1,0:T(8,128)(2,1)}, u32[]{:S(2)}, u32[]{:S(2)}) collective-permute-start(bf16[4,48,384]{2,1,0:T(8,128)(2,1)S(1)} %fusion.9.refs_4_), channel_id=1, source_target_pairs={{0,3},{1,2},{2,1},{3,0},{4,7},{5,6},{6,5},{7,4},{8,11},{9,10},{10,... | collective-permute-start | bytes 442376 | tf_op jit(solution)/shard_map/ppermute | solution.py:372
  180.1 18.0 %collective-permute-start.22 = (bf16[2,48,384]{2,1,0:T(8,128)(2,1)S(1)}, bf16[2,48,384]{2,1,0:T(8,128)(2,1)S(1)}, u32[]{:S(2)}, u32[]{:S(2)}) collective-permute-start(bf16[2,48,384]{2,1,0:T(8,128)(2,1)S(1)} %bitcast.54), channel_id=1, source_target_pairs={{0,2},{1,3},{2,0},{3,1},{4,6},{5,7},{6,4},{7,5},{8,10},{9,11},{10,... | collective-permute-start | bytes 221192 | tf_op jit(solution)/shard_map/ppermute | solution.py:372
  181.6 14.7 %collective-permute-start.19 = (bf16[32,2304]{1,0:T(8,128)(2,1)S(1)}, bf16[32,2304]{1,0:T(8,128)(2,1)}, u32[]{:S(2)}, u32[]{:S(2)}) collective-permute-start(bf16[32,2304]{1,0:T(8,128)(2,1)S(1)} %reshape.201), channel_id=1, source_target_pairs={{0,2},{1,3},{2,0},{3,1},{4,6},{5,7},{6,4},{7,5},{8,10},{9,11},{10,... | collective-permute-start | bytes 442376 | tf_op jit(solution)/shard_map/ppermute | solution.py:372
  183.1 10.1 %all-to-all-start.3 = ((f32[8,1,192]{2,1,0:T(1,128)}), f32[8,1,192]{2,1,0:T(1,128)S(1)}, u32[]{:S(2)}, u32[]{:S(2)}) async-start(f32[8,1,192]{2,1,0:T(1,128)} %reshape.215), calls=%async_computation.3 | async-start | bytes 16384 | tf_op jit(solution)/shard_map/all_to_all | solution.py:433
  194.5 3.6 %collective-permute-start.23 = (bf16[2,48,384]{2,1,0:T(8,128)(2,1)S(1)}, bf16[2,48,384]{2,1,0:T(8,128)(2,1)S(1)}, u32[]{:S(2)}, u32[]{:S(2)}) collective-permute-start(bf16[2,48,384]{2,1,0:T(8,128)(2,1)S(1)} %bitcast.55), channel_id=1, source_target_pairs={{0,1},{1,0},{2,3},{3,2},{4,5},{5,4},{6,7},{7,6},{8,9},{9,8},{10,11... | collective-permute-start | bytes 221192 | tf_op jit(solution)/shard_map/ppermute | solution.py:372
  194.6 4.0 %collective-permute-start.24 = (bf16[2,48,384]{2,1,0:T(8,128)(2,1)S(1)}, bf16[2,48,384]{2,1,0:T(8,128)(2,1)S(1)}, u32[]{:S(2)}, u32[]{:S(2)}) collective-permute-start(bf16[2,48,384]{2,1,0:T(8,128)(2,1)S(1)} %bitcast.56), channel_id=1, source_target_pairs={{0,3},{1,2},{2,1},{3,0},{4,7},{5,6},{6,5},{7,4},{8,11},{9,10},{10,... | collective-permute-start | bytes 221192 | tf_op jit(solution)/shard_map/ppermute | solution.py:372
  196.2 9.0 %collective-permute-start.20 = (bf16[32,2304]{1,0:T(8,128)(2,1)S(1)}, bf16[32,2304]{1,0:T(8,128)(2,1)S(1)}, u32[]{:S(2)}, u32[]{:S(2)}) collective-permute-start(bf16[32,2304]{1,0:T(8,128)(2,1)S(1)} %reshape.201), channel_id=1, source_target_pairs={{0,1},{1,0},{2,3},{3,2},{4,5},{5,4},{6,7},{7,6},{8,9},{9,8},{10,11... | collective-permute-start | bytes 442376 | tf_op jit(solution)/shard_map/ppermute | solution.py:372
  196.3 8.9 %collective-permute-start.21 = (bf16[32,2304]{1,0:T(8,128)(2,1)}, bf16[32,2304]{1,0:T(8,128)(2,1)S(1)}, u32[]{:S(2)}, u32[]{:S(2)}) collective-permute-start(bf16[32,2304]{1,0:T(8,128)(2,1)} %collective-permute-done.19), channel_id=1, source_target_pairs={{0,1},{1,0},{2,3},{3,2},{4,5},{5,4},{6,7},{7,6},{8,9},{9,8},{10,11... | collective-permute-start | bytes 442376 | tf_op jit(solution)/shard_map/ppermute | solution.py:372
  (25 other events, 253.3 us)

commit v3 on v2

--- a/solution.py
+++ b/solution.py
@@ -7,6 +7,7 @@
 from jax.experimental import pallas as pl
 from jax.experimental.pallas import tpu as pltpu
 from jax.sharding import PartitionSpec as P
+
 
 HEAD = 64
 STEP = 2
@@ -61,47 +62,73 @@
     return (relative & 1) * (owners // 2) + (relative >> 1)
 
 
-def unpack_attn(place, own, other, whole):
-    owners, width = own.shape[0], own.shape[-1]
-    rows = whole.shape[0] // owners
-    for core in range(2):
-        for source, near in ((own, True), (other, False)):
-
-            @pl.when(((place[1] & 1) == core) == near)
+def each_piece(place, pieces, store):
+    for block in range(GROUP):
+        for k, piece in zip((0, 2, 1, 3), pieces):
+
+            @pl.when((place[1] ^ k) == block)
             def _():
-                for part in range(2):
-                    block = 2 * core + part
-                    for owner in range(owners):
-                        whole[
-                            owner * rows : (owner + 1) * rows, block * width : (block + 1) * width
-                        ] = source[owner, part * rows : (part + 1) * rows, :]
-
-
-def unpack_mlp(place, own, other, w_up, w_down):
+                for owner in range(piece.shape[0]):
+                    store(block, owner, piece)
+
+
+def unpack_attn(place, pieces, whole, base):
+    width = pieces[0].shape[-1]
+    rows = whole.shape[0] // pieces[0].shape[0]
+
+    def store(block, owner, piece):
+        whole[owner * rows : (owner + 1) * rows, block * width : (block + 1) * width] = piece[
+            owner, base : base + rows, :
+        ]
+
+    each_piece(place, pieces, store)
+
+
+def unpack_mlp(place, pieces, w_up, w_down):
     width = w_up.shape[0]
-    upper = own[0].shape[0]
-    owners = 2 * upper
+    owners = 2 * pieces[0].shape[0]
     rows = width // owners
     for core in range(2):
-        for source, near in ((own, True), (other, False)):
+        for far in range(2):
             for side in range(2):
-
-                @pl.when((((place[1] & 1) == core) == near))
+                piece = pieces[2 * far + side]
+
+                @pl.when((place[1] & 1) == (core ^ far))
                 def _():
-                    for owner in range(owners):
-
-                        @pl.when(((place[0] ^ owner) & 1) == side)
-                        def _():
-                            spot = (place[0] ^ owner) >> 1
-                            piece = source[side]
-                            for part in range(2):
-                                block = 2 * core + part
-                                w_up[
-                                    owner * rows : (owner + 1) * rows,
-                                    block * width : (block + 1) * width,
-                                ] = piece[spot, part * rows : (part + 1) * rows, :]
-                            start = (owner * GROUP + 2 * core) * rows
-                            w_down[start : start + 2 * rows, :] = piece[spot, 2 * rows : 4 * rows, :]
+                    for upper in range(owners // 2):
+                        owner = place[0] ^ (2 * upper + side)
+                        at = pl.multiple_of(owner * rows, rows)
+                        for part in range(2):
+                            cols = slice((2 * core + part) * width, (2 * core + part + 1) * width)
+                            w_up[pl.ds(at, rows), cols] = piece[
+                                upper, part * rows : (part + 1) * rows, :
+                            ]
+                        start = pl.multiple_of(owner * (GROUP * rows) + 2 * core * rows, rows)
+                        w_down[pl.ds(start, 2 * rows), :] = piece[upper, 2 * rows : 4 * rows, :]
+
+
+def unpack_mlp_rows(place, pieces, w_up, w_down):
+    width = w_up.shape[0]
+    owners = 2 * pieces[0].shape[0]
+    rows = width // owners
+    for core in range(2):
+        for far in range(2):
+            near_side, far_side = pieces[2 * far], pieces[2 * far + 1]
+
+            @pl.when((place[1] & 1) == (core ^ far))
+            def _():
+                for owner in range(owners):
+                    relative = place[0] ^ owner
+                    piece = jnp.where(
+                        (relative & 1) == 0, near_side[relative >> 1], far_side[relative >> 1]
+                    )
+                    for part in range(2):
+                        block = 2 * core + part
+                        w_up[
+                            owner * rows : (owner + 1) * rows, block * width : (block + 1) * width
+                        ] = piece[part * rows : (part + 1) * rows]
+                    start = (owner * GROUP + 2 * core) * rows
+                    w_down[start : start + 2 * rows, :] = piece[2 * rows : 4 * rows]
 
 
 def pack_block(place, block, spot, value, keep, send, offset=0):
@@ -123,12 +150,12 @@
     return low.astype(bf16), (1.0 - low).astype(bf16)
 
 
-def attn_forward(place, lat, mod, bias, own, other, qkv_o, att_o, branch_o, lse_o, whole, att_t):
+def attn_forward(base, place, lat, mod, bias, p0, p1, p2, p3, qkv_o, att_o, branch_o, lse_o, whole, att_t):
     width = lat.shape[-1]
 
     @pl.when(pl.program_id(0) == 0)
     def _():
-        unpack_attn(place, own, other, whole)
+        unpack_attn(place, (p0, p1, p2, p3), whole, base)
 
     normed, _ = layer_norm(lat[0].astype(f32))
     input_a = (normed * (1.0 + mod[0, 1:2]) + mod[0, 0:1]).astype(bf16)
@@ -161,8 +188,8 @@
 
 
 def mlp_both(
-    place, lat, cot, branch, att, mod, bias,
-    own_near, own_far, other_near, other_far,
+    base, place, lat, cot, branch, att, mod, bias,
+    p0, p1, p2, p3,
     out_o, dmid_o, dmod_o, gattn_o, gbias_o, keep_o, send_o,
     w_up, w_down, gelu_s, slope_s, dpre_s, acc_up, acc_down,
 ):
@@ -173,7 +200,9 @@
 
     @pl.when(first)
     def _():
-        unpack_mlp(place, (own_near, own_far), (other_near, other_far), w_up, w_down)
+        whole_tiles = p0.shape[1] % 64 == 0
+        unpack = unpack_mlp if whole_tiles else unpack_mlp_rows
+        unpack(place, (p0, p1, p2, p3), w_up, w_down)
         acc_up[...] = jnp.zeros_like(acc_up)
         acc_down[...] = jnp.zeros_like(acc_down)
         gattn_o[...] = jnp.zeros_like(gattn_o)
@@ -236,7 +265,7 @@
                 pack_block(place, block, spot, value, keep_o, send_o, 2)
 
 
-def attn_backward(first, last, place, lat, dmid, qkv, lse, mod, own, other, *refs):
+def attn_backward(first, last, base, place, lat, dmid, qkv, lse, mod, p0, p1, p2, p3, *refs):
     refs = list(refs)
     if not first:
         acc_i, gbias_i = refs.pop(0), refs.pop(0)
@@ -252,7 +281,7 @@
 
     @pl.when(step == 0)
     def _():
-        unpack_attn(place, own, other, whole)
+        unpack_attn(place, (p0, p1, p2, p3), whole, base)
         acc[...] = jnp.zeros_like(acc) if first else acc_i[...]
         gbias_o[...] = jnp.zeros_like(gbias_o) if first else gbias_i[...]
 
@@ -326,45 +355,119 @@
     return weight, moment, second
 
 
+def adam_write(refs, gradient, where):
+    weight, mean, square, grad_o, weight_o, mean_o, square_o = refs
+    grad_o[where] = gradient
+    weight_o[where], mean_o[where], square_o[where] = adam_parts(
+        weight[where], mean[where], square[where], gradient
+    )
+
+
+def block_of(place, parts, block, rows, offset=0):
+    k = place[1] ^ block
+    here, there = offset + (k >> 1), offset + 1 - (k >> 1)
+    near = parts[0][here].astype(f32) + parts[1][there].astype(f32)
+    far = parts[2][here].astype(f32) + parts[3][there].astype(f32)
+    return jnp.where((k & 1) == 0, near, far)[:rows]
+
+
 def adam_kernel(place, *refs):
-    att, mlp = refs[0:4], refs[4:8]
-    weights, means, squares = refs[8:11], refs[11:14], refs[14:17]
-    grads, new_w, new_m, new_s = refs[17:20], refs[20:23], refs[23:26], refs[26:29]
+    att, mlp, mods, conds = refs[0:4], refs[4:8], refs[8:12], refs[12:16]
+    wide, square, down = refs[16:-1:3], refs[17:-1:3], refs[18:-1:3]
+    gmod = refs[-1]
     width = att[0].shape[-1]
-
-    def write(which, where, gradient):
-        grads[which][where] = gradient
-        result = adam_parts(
-            weights[which][where], means[which][where], squares[which][where], gradient
-        )
-        new_w[which][where], new_m[which][where], new_s[which][where] = result
-
-    def block_of(parts, block, offset=0):
-        k = place[1] ^ block
-        here, there = offset + (k >> 1), offset + 1 - (k >> 1)
-        near = parts[0][here].astype(f32) + parts[1][there].astype(f32)
-        far = parts[2][here].astype(f32) + parts[3][there].astype(f32)
-        return jnp.where((k & 1) == 0, near, far)
-
+    rows = square[0].shape[0]
     everything = slice(None)
+
+    @pl.when(pl.program_id(0) == 0)
+    def _():
+        near, across, other, far = [
+            dot(cond[...], mod[...], TN) for cond, mod in zip(conds, mods)
+        ]
+        gmod[...] = (near + across) + (other + far)
+
+    def columns(block):
+        return (everything, slice(block * width, (block + 1) * width))
+
     for block in range(GROUP):
-        g_att = block_of(att, block)
+        g_att = block_of(place, att, block, rows)
         if block < GROUP - 1:
-            write(0, (everything, slice(block * width, (block + 1) * width)), g_att)
+            adam_write(wide, g_att, columns(block))
         else:
-            write(1, (everything, everything), g_att)
-        at = (GROUP - 1 + block) * width
-        write(0, (everything, slice(at, at + width)), block_of(mlp, block))
-        write(2, (block,), block_of(mlp, block, 2))
-
-
-def adam_mod(grad, weight, mean, square, *refs):
-    grad_o, weight_o, mean_o, square_o = refs[4:]
-    gradient = grad[...]
-    grad_o[...] = gradient
-    weight_o[...], mean_o[...], square_o[...] = adam_parts(
-        weight[...], mean[...], square[...], gradient
-    )
+            adam_write(square, g_att, (everything, everything))
+        adam_write(wide, block_of(place, mlp, block, rows), columns(GROUP - 1 + block))
+        adam_write(down, block_of(place, mlp, block, rows, 2), (block,))
+    start = 0 if gmod.shape[0] == rows else pl.multiple_of(pl.program_id(0) * rows, rows)
+    for block in range(6):
+        gradient = gmod[pl.ds(start, rows), block * width : (block + 1) * width]
+        adam_write(wide, gradient, columns(2 * GROUP - 1 + block))
+
+
+def pack_message(keep, received, mods_m, mods_0, mods_1, bias_a, bias_m, out, dms, bias):
+    owners, _, rows, width = keep.shape
+    count = mods_m.shape[0]
+    half = mods_0.shape[0]
+    for latent in range(count):
+        early = mods_0 if latent < half else mods_1
+        for part in range(6):
+            if part < 2:
+                value = early[latent % half, part : part + 1, :]
+            else:
+                value = mods_m[latent, part : part + 1, :]
+            dms[part * count + latent : part * count + latent + 1, :] = value
+    edge = bias_a.shape[1]
+    bias[0:1, :edge] = bias_a[...]
+    bias[0:1, edge : bias_m.shape[1]] = bias_m[0:1, edge:]
+    for part in range(6):
+        at = bias_m.shape[1] + part * width
+        bias[0:1, at : at + width] = token_sum(dms[part * count : (part + 1) * count, :])
+    dm_rows = 6 * count
+    dm_b = dms[...].astype(bf16)
+    shard = bias.shape[1] // owners
+    spans = [(lo, min(lo + width, shard)) for lo in range(0, shard, width)]
+    tail = 2 * rows + dm_rows
+    for owner in range(owners):
+        for k in range(2):
+            out[owner, k * rows : (k + 1) * rows, :] = (
+                keep[owner, k] + received[owner, k].astype(f32)
+            ).astype(bf16)
+        out[owner, 2 * rows : tail, :] = dm_b
+        out[owner, tail:, :] = jnp.zeros((out.shape[1] - tail, width), bf16)
+        for index, (lo, hi) in enumerate(spans):
+            value = bias[0:1, owner * shard + lo : owner * shard + hi]
+            high = value.astype(bf16)
+            low = (value - high.astype(f32)).astype(bf16)
+            out[owner, tail + index : tail + index + 1, : hi - lo] = high
+            at = tail + len(spans) + index
+            out[owner, at : at + 1, : hi - lo] = low
+
+
+def open_message(spans, arrived, share, dm_all, dms):
+    owners, _, width = arrived.shape
+    count = dm_all.shape[0] // owners
+    dm_rows = 6 * count
+    rows = (share.shape[1] - 8 * -(-spans // 8))
+    share[...] = jnp.zeros(share.shape, bf16)
+    for k in range(2):
+        total = arrived[0, k * rows : (k + 1) * rows, :].astype(f32)
+        for owner in range(1, owners):
+            total = total + arrived[owner, k * rows : (k + 1) * rows, :].astype(f32)
+        share[k, :rows, :] = total.astype(bf16)
+    tail = 2 * rows + dm_rows
+    total = jnp.zeros((spans, width), f32)
+    for owner in range(owners):
+        ends = arrived[owner, tail:, :].astype(f32)
+        total = total + (ends[:spans] + ends[spans : 2 * spans])
+    high = total.astype(bf16)
+    share[0, rows : rows + spans, :] = high
+    share[1, rows : rows + spans, :] = (total - high.astype(f32)).astype(bf16)
+    for owner in range(owners):
+        block = arrived[owner, 2 * rows : tail, :].astype(f32)
+        for part in range(6):
+            dms[owner * count : (owner + 1) * count, part * width : (part + 1) * width] = block[
+                part * count : (part + 1) * count
+            ]
+    dm_all[...] = dms[...].astype(bf16)
 
 
 def swap(value, axis, bit):
@@ -383,27 +486,6 @@
     for stage in upper_stages(lax.axis_size("dp")):
         held = jnp.concatenate([held] + [swap(held, "dp", 2 * c) for c in stage], axis=0)
     return held
-
-
-def group_gather(value):
-    two = swap(value, "group", 2)
-    return value, two, swap(value, "group", 1), swap(two, "group", 1)
-
-
-def in_order(parts, mine):
-    low = mine < 2
-    even = (mine & 1) == 0
-    near, far = jnp.where(low, parts[0], parts[1]), jnp.where(low, parts[1], parts[0])
-    other, wide = jnp.where(low, parts[2], parts[3]), jnp.where(low, parts[3], parts[2])
-    return jnp.concatenate(
-        [
-            jnp.where(even, near, other),
-            jnp.where(even, other, near),
-            jnp.where(even, far, wide),
-            jnp.where(even, wide, far),
-        ],
-        axis=0,
-    )
 
 
 def scatter_near(keep, dtype):
@@ -438,11 +520,6 @@
     return jnp.pad(flat, ((0, 0), (0, rows * width - flat.shape[1]))).reshape(-1, rows, width)
 
 
-def halves(value):
-    high = lax.reduce_precision(value, 8, 7)
-    return jnp.concatenate([high.astype(bf16), (value - high).astype(bf16)], axis=-1)
-
-
 def compiler(limit=56):
     return pltpu.CompilerParams(
         dimension_semantics=("arbitrary",), vmem_limit_bytes=limit * 1024 * 1024
@@ -459,16 +536,25 @@
     return pl.BlockSpec((1,) + tuple(array.shape[1:]), lambda l, *_: (l,) + zeros)
 
 
-def call(kernel, place, latent_args, whole_args, latent_outs, whole_outs, scratch, grid, start=0, us=15):
+def piece_spec(array, start, size):
+    owners, _, width = array.shape
+    if size % 16 == 0 and start % size == 0:
+        return pl.BlockSpec((owners, size, width), lambda l, *_: (0, start // size, 0)), 0
+    return whole_spec(array), start
+
+
+def call(kernel, place, latent_args, whole_args, pieces, extra_args, latent_outs, whole_outs, scratch,
+         grid, part, start=0, us=15, options=()):
     def shifted(array):
         zeros = (0,) * (len(array.shape) - 1)
         return pl.BlockSpec((1,) + tuple(array.shape[1:]), lambda l, *_: (l + start,) + zeros)
 
+    spec, base = piece_spec(pieces[0], *part) if part else (whole_spec(pieces[0]), 0)
     ins = [shifted(a) for a in latent_args] + [whole_spec(a) for a in whole_args]
+    ins = ins + [spec] * len(pieces) + [whole_spec(a) for a in extra_args]
     outs = [latent_spec(a) for a in latent_outs] + [whole_spec(a) for a in whole_outs]
-    func = kernel.func if isinstance(kernel, functools.partial) else kernel
     return pl.pallas_call(
-        kernel,
+        functools.partial(kernel, *options, base),
         grid_spec=pltpu.PrefetchScalarGridSpec(
             num_scalar_prefetch=1,
             grid=(grid,),
@@ -481,8 +567,7 @@
         cost_estimate=pl.CostEstimate(
             flops=int(us * 1e9), bytes_accessed=int(us * 1e6), transcendentals=0
         ),
-        name=func.__name__,
-    )(place, *latent_args, *whole_args)
+    )(place, *latent_args, *whole_args, *pieces, *extra_args)
 
 
 def like(shape, dtype):
@@ -504,43 +589,46 @@
     mine = lax.axis_index("group")
     place = jnp.stack([me, mine]).astype(jnp.int32)
 
-    core = mine & 1
     bias_shard = biases.shape[0]
     mod_at = 3 * width + hidden
     bias_mod_at = 4 * width + hidden
 
-    def blocks_of(first, second):
-        return jnp.where(core == 0, first, second)
-
-    q_rows, k_rows, v_rows = [input_proj[:, b * width : (b + 1) * width] for b in range(3)]
+    def block_here(blocks):
+        return jnp.where(
+            mine < 2,
+            jnp.where(mine == 0, blocks[0], blocks[1]),
+            jnp.where(mine == 2, blocks[2], blocks[3]),
+        ).astype(bf16)
+
+    columns = [input_proj[:, b * width : (b + 1) * width] for b in range(3 + GROUP)]
     ids = jnp.concatenate([timestep, labels]).astype(jnp.int32)
     note = jnp.concatenate([biases, (ids // 32).astype(f32), (ids % 32).astype(f32)])
     note_size = note.shape[0]
     note_rows = 8 * -(-note_size // (8 * width))
-    note = pad_rows(note[None].astype(bf16), width, note_rows)[0]
     message = jnp.concatenate(
         [
-            blocks_of(q_rows, v_rows).astype(bf16),
-            blocks_of(k_rows, attn_proj).astype(bf16),
-            note,
+            block_here(columns[:3] + [attn_proj]),
+            pad_rows(note[None].astype(bf16), width, note_rows)[0],
         ],
         axis=0,
     )
-    att_own = to_owners(jnp.broadcast_to(message[None], (owners,) + message.shape))
-    up_rows = [input_proj[:, (3 + b) * width : (4 + b) * width] for b in range(GROUP)]
+    att_part = (0, rows)
+    pieces = to_owners(jnp.broadcast_to(message[None], (owners,) + message.shape))
+    pieces_y = swap(pieces, "group", 2)
+
+    even = (mine & 1) == 0
     mlp_piece = jnp.concatenate(
         [
-            blocks_of(up_rows[0], up_rows[2]),
-            blocks_of(up_rows[1], up_rows[3]),
-            blocks_of(mlp_down[: 2 * rows], mlp_down[2 * rows :]),
+            jnp.where(even, columns[3], columns[5]),
+            jnp.where(even, columns[4], columns[6]),
+            jnp.where(even, mlp_down[: 2 * rows], mlp_down[2 * rows :]),
         ],
         axis=0,
     ).astype(bf16)
-    att_own, mlp_piece = lax.optimization_barrier((att_own, mlp_piece))
-    att_other = swap(att_own, "group", 1)
     mlp_near = gather_upper(mlp_piece[None])
-
-    notes = att_own[:, 2 * rows :].reshape(owners, -1)[:, :note_size].astype(f32)
+    mlp_far = swap(mlp_near, "dp", 1)
+
+    notes = pieces[:, rows :].reshape(owners, -1)[:, :note_size].astype(f32)
     bias_all = notes[:, :bias_shard].reshape(1, -1)
     ids = 32.0 * notes[:, bias_shard : bias_shard + 2 * count] + notes[:, bias_shard + 2 * count :]
     times_all = ids[:, :count].reshape(-1)
@@ -552,14 +640,13 @@
     w_mod = input_proj[:, mod_at:].astype(bf16)
     cond_cols = lax.dynamic_slice_in_dim(cond_b, me * rows, rows, 1)
     partial = dot(cond_cols, w_mod).reshape(owners, count, -1)
-    modulation = jnp.sum(to_owners(partial), axis=0) + bias_all[:, bias_mod_at:]
-    mod = modulation.reshape(count, 6, width)
-    mod, mlp_near = lax.optimization_barrier((mod, mlp_near))
-    mlp_far = swap(mlp_near, "dp", 1)
+    partial = to_owners(partial)
+    mod = (jnp.sum(partial, axis=0) + bias_all[:, bias_mod_at:]).reshape(count, 6, width)
+    pieces = [pieces, pieces_y, swap(pieces, "group", 1), swap(pieces_y, "group", 1)]
 
     qkv, attended, branch_a, lse = call(
         attn_forward, place,
-        [latents, mod], [bias_all, att_own, att_other],
+        [latents, mod], [bias_all], pieces, [],
         [
             like((count, seq_len, 3 * width), bf16),
             like((count, seq_len, width), bf16),
@@ -568,15 +655,14 @@
         ],
         [],
         [pltpu.VMEM((width, 4 * width), bf16), pltpu.VMEM((width, seq_len), f32)],
-        count,
+        count, att_part,
     )
-    branch_a, mlp_near, mlp_far = lax.optimization_barrier((branch_a, mlp_near, mlp_far))
+    cond_group = [cond_cols] + [swap(cond_cols, "group", k) for k in (2, 1, 3)]
     mlp_parts = [mlp_near, mlp_far, swap(mlp_near, "group", 1), swap(mlp_far, "group", 1)]
-    cond_group = [cond_cols] + [swap(cond_cols, "group", k) for k in (2, 1, 3)]
     bias_like = like((1, bias_mod_at), f32)
     block_out, d_middle, d_mod_m, g_attn, g_bias_m, mlp_keep, mlp_send = call(
         mlp_both, place,
-        [latents, cotangent, branch_a, attended, mod], [bias_all] + mlp_parts,
+        [latents, cotangent, branch_a, attended, mod], [bias_all], mlp_parts, [],
         [
             like((count, seq_len, width), bf16),
             like((count, seq_len, width), f32),
@@ -597,11 +683,11 @@
             pltpu.VMEM((width, hidden), f32),
             pltpu.VMEM((width, hidden), f32),
         ],
-        count,
+        count, None,
         us=20,
     )
     mlp_keep = mlp_keep + swap(mlp_send, "group", 1).astype(f32)
-    d_middle, mlp_keep = lax.optimization_barrier((d_middle, mlp_keep))
+    d_middle, mlp_keep, g_bias_m = lax.optimization_barrier((d_middle, mlp_keep, g_bias_m))
 
     half = count // 2
     token_like = like((half, seq_len, width), f32)
@@ -614,57 +700,55 @@
     ]
     token_args = [latents, d_middle, qkv, lse, mod]
     glat_0, d_mod_0, g_bias_a, acc = call(
-        functools.partial(attn_backward, True, False), place,
-        token_args, [att_own, att_other],
-        [token_like, mod_like], [gb_like, like((width, 3 * width), f32)], scratch, half, 0, 10,
+        attn_backward, place,
+        token_args, [], pieces, [],
+        [token_like, mod_like], [gb_like, like((width, 3 * width), f32)],
+        scratch, half, att_part, 0, 10, (True, False),
     )
     mlp_keep = scatter_near(mlp_keep, bf16)
     acc, mlp_keep = lax.optimization_barrier((acc, mlp_keep))
     glat_1, d_mod_1, g_bias_a, at_keep, at_send = call(
-        functools.partial(attn_backward, False, True), place,
-        token_args, [att_own, att_other, acc, g_bias_a, g_attn],
+        attn_backward, place,
+        token_args, [], pieces, [acc, g_bias_a, g_attn],
         [token_like, mod_like],
         [gb_like, like((owners, 2, rows, width), f32), like((owners, 2, rows, width), bf16)],
-        scratch + [pltpu.VMEM((width, 3 * width), f32)], count - half, half, 10,
+        scratch + [pltpu.VMEM((width, 3 * width), f32)],
+        count - half, att_part, half, 10, (False, True),
     )
     mlp_total = scatter_upper(mlp_keep, bf16)
     grad_latents = jnp.concatenate([glat_0, glat_1], axis=0)
 
-    d_mod_a = jnp.concatenate([d_mod_0, d_mod_1], axis=0)
-    d_modulation = jnp.concatenate([d_mod_a, d_mod_m[:, 2:]], axis=1).reshape(count, 6 * width)
-    bias_grad = jnp.concatenate(
-        [g_bias_a[0], g_bias_m[0, 2 * width :], jnp.sum(d_modulation, axis=0)]
-    )
-    at_keep = at_keep + swap(at_send, "group", 1).astype(f32)
-    bias_grad = (bias_grad + swap(bias_grad, "group", 2)) + (
-        swap(bias_grad, "group", 1) + swap(bias_grad, "group", 3)
-    )
-
     dm_rows = count * 6
-    bias_halves = halves(bias_grad.reshape(owners, bias_shard))
-    tail_rows = -(-2 * bias_shard // width)
+    spans = -(-bias_shard // width)
+    tail_rows = 2 * spans
     tail_rows += -(2 * rows + dm_rows + tail_rows) % 8
-    message = jnp.concatenate(
-        [
-            at_keep.astype(bf16).reshape(owners, 2 * rows, width),
-            jnp.broadcast_to(
-                d_modulation.astype(bf16).reshape(1, dm_rows, width), (owners, dm_rows, width)
-            ),
-            pad_rows(bias_halves, width, tail_rows),
+    at_received = swap(at_send, "group", 1)
+    message = pl.pallas_call(
+        pack_message,
+        out_shape=like((owners, 2 * rows + dm_rows + tail_rows, width), bf16),
+        scratch_shapes=[pltpu.VMEM((dm_rows, width), f32), pltpu.VMEM((1, bias_shard * owners), f32)],
+        compiler_params=pltpu.CompilerParams(vmem_limit_bytes=56 * 1024 * 1024),
+        name="pack_message",
+    )(at_keep, at_received, d_mod_m, d_mod_0, d_mod_1, g_bias_a, g_bias_m)
+    arrived = to_owners(message)
+    mlp_shared = share_parts(mlp_total)
+    at_total, dm_all = pl.pallas_call(
+        functools.partial(open_message, spans),
+        out_shape=[
+            like((2, rows + 8 * -(-spans // 8), width), bf16),
+            like((owners * count, 6 * width), bf16),
         ],
-        axis=1,
-    )
-    message, mlp_total = lax.optimization_barrier((message, mlp_total))
-    mlp_shared = share_parts(mlp_total)
-    arrived = to_owners(message)
-    at_total = jnp.sum(arrived[:, : 2 * rows].astype(f32), axis=0).reshape(2, rows, width)
+        scratch_shapes=[pltpu.VMEM((owners * count, 6 * width), f32)],
+        compiler_params=pltpu.CompilerParams(vmem_limit_bytes=56 * 1024 * 1024),
+        name="open_message",
+    )(arrived)
     at_shared = share_parts(at_total)
-    dm_all = arrived[:, 2 * rows : 2 * rows + dm_rows].reshape(owners * count, 6 * width)
-    dm_group = group_gather(dm_all)
-    g_halves = jnp.sum(
-        arrived[:, 2 * rows + dm_rows :].reshape(owners, -1)[:, : 2 * bias_shard].astype(f32), axis=0
-    )
-    g_biases = g_halves[:bias_shard] + g_halves[bias_shard:]
+    dm_group = [dm_all] + [swap(dm_all, "group", k) for k in (2, 1, 3)]
+    near, across, other, wide = [
+        jnp.sum(part[:, rows : rows + spans].astype(f32).reshape(2, -1)[:, :bias_shard], axis=0)
+        for part in at_shared
+    ]
+    g_biases = (near + across) + (other + wide)
     bias_out = (g_biases,) + adam_parts(biases, mean_biases, sq_biases, g_biases)
 
     back = dot(dm_all, w_mod, NT).reshape(owners, count, rows)
@@ -675,56 +759,43 @@
     grad_cond = d_cond * (own_sig * (1.0 + own_cond * (1.0 - own_sig)))
 
     steps = rows // 16 if rows % 16 == 0 else 1
-    block_rows = rows // steps
 
     def spec_of(array):
         if len(array.shape) == 3:
-            return pl.BlockSpec((array.shape[0], block_rows, width), lambda s, *_: (0, s, 0))
-        return pl.BlockSpec((block_rows, min(array.shape[1], mod_at)), lambda s, *_: (s, 0))
-
-    state = [
-        entry
-        for three in (
-            (input_proj, attn_proj, mlp_down),
-            (mean_input, mean_attn, mean_down),
-            (sq_input, sq_attn, sq_down),
-        )
-        for entry in (three[0], three[1], three[2].reshape(GROUP, rows, width))
-    ]
-    args = at_shared + mlp_shared + state
+            size = rows // steps
+            if steps == 1:
+                size = array.shape[1]
+            return pl.BlockSpec((array.shape[0], size, width), lambda s, *_: (0, s, 0))
+        return pl.BlockSpec((rows // steps, array.shape[1]), lambda s, *_: (s, 0))
+
+    state = []
+    for three in (
+        (input_proj, attn_proj, mlp_down),
+        (mean_input, mean_attn, mean_down),
+        (sq_input, sq_attn, sq_down),
+    ):
+        state += [three[0], three[1], three[2].reshape(GROUP, rows, width)]
+    args = at_shared + mlp_shared + dm_group + cond_group + state
+    in_specs = [spec_of(a) for a in at_shared + mlp_shared]
+    in_specs += [whole_spec(a) for a in dm_group + cond_group] + [spec_of(a) for a in state]
     results = [like(a.shape, f32) for a in state[:3]] * 4
     outs = pl.pallas_call(
         adam_kernel,
         grid_spec=pltpu.PrefetchScalarGridSpec(
             num_scalar_prefetch=1,
             grid=(steps,),
-            in_specs=[spec_of(a) for a in args],
+            in_specs=in_specs,
             out_specs=[spec_of(a) for a in results],
+            scratch_shapes=[pltpu.VMEM((rows, 6 * width), f32)],
         ),
         out_shape=results,
         compiler_params=compiler(),
         name="adam",
     )(place, *args)
-
-    g_mod = dot(in_order(cond_group, mine), in_order(dm_group, mine), TN)
-    first = mod_at // width
-    local = pl.BlockSpec((rows, width), lambda s: (0, s))
-    placed = pl.BlockSpec((rows, width), lambda s: (0, s + first))
-    anywhere = pl.BlockSpec(memory_space=pl.ANY)
-    wide = pl.pallas_call(
-        adam_mod,
-        grid=(6,),
-        in_specs=[local] + [placed] * 3 + [anywhere] * 4,
-        out_specs=[placed] * 4,
-        out_shape=[like(input_proj.shape, f32)] * 4,
-        input_output_aliases={4 + i: i for i in range(4)},
-        compiler_params=compiler(),
-        name="adam_mod",
-    )(g_mod, input_proj, mean_input, sq_input, outs[0], outs[3], outs[6], outs[9])
+    wide, square, down = outs[0::3], outs[1::3], outs[2::3]
 
     def flat(index):
-        three = outs[3 * index : 3 * index + 3]
-        return (wide[index], three[1], three[2].reshape(mlp_down.shape), bias_out[index])
+        return (wide[index], square[index], down[index].reshape(mlp_down.shape), bias_out[index])
 
     return (block_out, grad_latents, grad_cond) + flat(0) + flat(1) + flat(2) + flat(3)
 
@@ -734,4 +805,5 @@
     four = (P("dp", None), P("dp", None), P("dp", None), P("dp"))
     in_specs = (tokens, tokens, P(("dp", "group")), P(("dp", "group")), P()) + four * 3
     out_specs = (tokens, tokens, P(("dp", "group"), None)) + four * 4
+
     return jax.shard_map(body, mesh=mesh, in_specs=in_specs, out_specs=out_specs, check_vma=False)

time: 214 us -> 209 us (0.977)
  other arithmetic: 22.3 us -> 10.1 us
  waiting for transfers between devices: 65 us -> 74.6 us
  local copies, waits for them, and re-layouts: 9.12 us -> 5.66 us
    ppermute x28 -> x27, waiting for transfers between devices: 35.2 us -> 64.1 us  [swap(): return lax.ppermute(value, axis, [(i, i ^ bit) for i in range(size)])]
    all_to_all x4, waiting for transfers between devices: 29.8 us -> 10.5 us  [to_owners(): return lax.all_to_all(value, 'dp', 0, 0, tiled=True)]
    all_to_all x4, starting transfers between devices: 18.5 us -> 21.2 us  [to_owners(): return lax.all_to_all(value, 'dp', 0, 0, tiled=True)]
    add x3 -> x1, other arithmetic: 3.24 us -> 0.63 us  [body(): jnp.sum(partial, axis=0) + bias_all[:, bias_mod_at:]]
    ppermute x28 -> x27, starting transfers between devices: 23.5 us -> 22.5 us  [swap(): return lax.ppermute(value, axis, [(i, i ^ bit) for i in range(size)])]
    pallas_call x5 -> x6, Pallas kernels: 64.6 us -> 64.1 us  [the longest x4 59.5 us: call(): pl.pallas_call(functools.partial(kernel, *options, base), grid_spec=pltpu...]
  transfers between devices with their start and end apart: 32 -> 31, of which waited for: 14 -> 16; matrix products, arithmetic and copies ran while one was open for 8% -> 5% of each run, Pallas kernels for 15% -> 13%
where the time goes in v3:
time: 209 us; the launch traced here: 208 us
  waiting for transfers between devices  74.6 us (36%)
  Pallas kernels  71.5 us (34%)
  starting transfers between devices  43.7 us (21%)
  other arithmetic  10.1 us (5%)
  local copies, waits for them, and re-layouts  5.66 us (3%)
    ppermute x27, waiting for transfers between devices, swap(): return lax.ppermute(value, axis, [(i, i ^ bit) for i in range(size)])  64.1 us
    pallas_call x4, Pallas kernels, call(): pl.pallas_call(functools.partial(kernel, *options, base), grid_spec=pltpu...  59.5 us
    ppermute x27, starting transfers between devices, swap(): return lax.ppermute(value, axis, [(i, i ^ bit) for i in range(size)])  22.5 us
    all_to_all x4, starting transfers between devices, to_owners(): return lax.all_to_all(value, 'dp', 0, 0, tiled=True)  21.2 us
    all_to_all x4, waiting for transfers between devices, to_owners(): return lax.all_to_all(value, 'dp', 0, 0, tiled=True)  10.5 us
    pallas_call x1, Pallas kernels, body(): pl.pallas_call(adam_kernel, grid_spec=pltpu.PrefetchScalarGridSpec(num_sc...  7.38 us
  transfers between devices with their start and end apart: 31, of which 16 were waited for; matrix products, arithmetic and copies ran while one was open for 5% of the time, Pallas kernels for 13%

profile of v3, /device:TPU:0, one launch (start us, length us, event | category | flops | bytes accessed | tf_op | source)
XLA Modules:
  0.0 208.3 jit_solution(8093482474050758227)
XLA Ops:
  4.3 7.3 %all-to-all-start = ((bf16[8,56,384]{2,1,0:T(8,128)(2,1)}), bf16[8,56,384]{2,1,0:T(8,128)(2,1)S(1)}, u32[]{:S(2)}, u32[]{:S(2)}) async-start(bf16[8,56,384]{2,1,0:T(8,128)(2,1)} %broadcast_in_dim.2), calls=%async_computation | async-start | bytes 688128 | tf_op jit(solution)/shard_map/all_to_all | solution.py:515
  11.7 2.1 collective-permute-start.3
  13.7 2.4 %collective-permute-start.4 = (bf16[1,192,384]{2,1,0:T(8,128)(2,1)S(1)}, bf16[1,192,384]{2,1,0:T(8,128)(2,1)S(1)}, u32[]{:S(2)}, u32[]{:S(2)}) collective-permute-start(bf16[1,192,384]{2,1,0:T(8,128)(2,1)S(1)} %pad_maximum_fusion.2), channel_id=1, source_target_pairs={{0,16},{4,20},{8,24},{12,28},{16,0},{20,4},{24,8},{28,12},{1,17},{... | collective-permute-start | bytes 442376 | tf_op jit(solution)/shard_map/ppermute | solution.py:475
  16.2 7.6 %collective-permute-done.3 = bf16[1,192,384]{2,1,0:T(8,128)(2,1)S(1)} collective-permute-done((bf16[1,192,384]{2,1,0:T(8,128)(2,1)S(1)}, bf16[1,192,384]{2,1,0:T(8,128)(2,1)S(1)}, u32[]{:S(2)}, u32[]{:S(2)}) %collective-permute-start.3) | collective-permute-done | bytes 147488 | tf_op jit(solution)/shard_map/ppermute | solution.py:475
  23.8 9.3 %collective-permute-done.4 = bf16[1,192,384]{2,1,0:T(8,128)(2,1)S(1)} collective-permute-done((bf16[1,192,384]{2,1,0:T(8,128)(2,1)S(1)}, bf16[1,192,384]{2,1,0:T(8,128)(2,1)S(1)}, u32[]{:S(2)}, u32[]{:S(2)}) %collective-permute-start.4) | collective-permute-done | bytes 147488 | tf_op jit(solution)/shard_map/ppermute | solution.py:475
  35.3 1.6 collective-permute-start
  37.8 4.0 %all-to-all-start.1 = ((f32[8,4,2304]{2,1,0:T(4,128)}), f32[8,4,2304]{2,1,0:T(4,128)S(1)}, u32[]{:S(2)}, u32[]{:S(2)}) async-start(f32[8,4,2304]{2,1,0:T(4,128)} %reshape.230), calls=%async_computation.1 | async-start | bytes 589824 | tf_op jit(solution)/shard_map/all_to_all | solution.py:515
  43.9 2.3 %collective-permute-done.6.p1 = bf16[4,192,384]{2,1,0:T(8,128)(2,1)} collective-permute-done((bf16[4,192,384]{2,1,0:T(8,128)(2,1)S(1)}, bf16[4,192,384]{2,1,0:T(8,128)(2,1)}, u32[]{:S(2)}, u32[]{:S(2)}) %collective-permute-start.6) | collective-permute-done | bytes 589856 | tf_op jit(solution)/shard_map/ppermute | solution.py:475
  46.1 4.6 %all-to-all-done.1 = f32[8,4,2304]{2,1,0:T(4,128)S(1)} async-done(((f32[8,4,2304]{2,1,0:T(4,128)}), f32[8,4,2304]{2,1,0:T(4,128)S(1)}, u32[]{:S(2)}, u32[]{:S(2)}) %all-to-all-start.1) | async-done | bytes 294944 | tf_op jit(solution)/shard_map/all_to_all | solution.py:515
  51.5 14.7 %shard_map.312 = (bf16[4,256,1152]{2,1,0:T(8,128)(2,1)}, bf16[4,256,384]{2,1,0:T(8,128)(2,1)}, f32[4,256,384]{2,1,0:T(8,128)}, f32[4,6,256]{2,1,0:T(8,128)}) custom-call(s32[2]{0:T(128)} %pad_add_fusion.place, bf16[4,256,384]{2,1,0:T(8,128)(2,1)} %lat.7, f32[4,6,384]{2,1,0:T(8,128)} %broadcast_add_fusion.mod, f32[1,5376]{1,0:T(1,128)} %copy-done.19, ...), custom_call_target="tpu_custom_call" | custom-call | flops 15000000512 | bytes 15000000 | tf_op jit(solution)/shard_map/pallas_call | solution.py:556
  66.2 21.0 %shard_map.313 = (bf16[4,256,384]{2,1,0:T(8,128)(2,1)}, f32[4,256,384]{2,1,0:T(8,128)}, f32[4,6,384]{2,1,0:T(8,128)}, f32[384,384]{1,0:T(8,128)}, f32[1,3072]{1,...) custom-call(s32[2]{0:T(128)} %pad_add_fusion.place, bf16[4,256,384]{2,1,0:T(8,128)(2,1)} %lat.7, ...), custom_call_target="tpu_custom_call" | custom-call | flops 20000000000 | bytes 20000000 | tf_op jit(solution)/shard_map/pallas_call | solution.py:556
  87.4 3.0 %collective-permute-done.9 = bf16[8,4,48,384]{3,2,1,0:T(8,128)(2,1)S(1)} collective-permute-done((bf16[8,4,48,384]{3,2,1,0:T(8,128)(2,1)}, bf16[8,4,48,384]{3,2,1,0:T(8,128)(2,1)S(1)}, u32[]{:S(2)}, u32[]{:S(2)}) %collective-permute-start.9) | collective-permute-done | bytes 1179680 | tf_op jit(solution)/shard_map/ppermute | solution.py:475
  90.4 1.9 convert_add_fusion
  93.9 11.1 %shard_map.314 = (f32[2,256,384]{2,1,0:T(8,128)}, f32[2,2,384]{2,1,0:T(2,128)}, f32[1,768]{1,0:T(1,128)}, f32[384,1152]{1,0:T(8,128)}) custom-call(s32[2]{0:T(128)} %pad_add_fusion.place, bf16[4,256,384]{2,1,0:T(8,128)(2,1)} %lat.7, f32[4,256,384]{2,1,0:T(8,128)} %get-tuple-element.65.dmid, bf16[4,256,1152]{2,1,0:T(8,128)(2,1)} %get-tuple-element.66.qkv, ...), custom_call_target="tpu_custom_call" | custom-call | flops 10000000000 | bytes 10000000 | tf_op jit(solution)/shard_map/pallas_call | solution.py:556
  105.0 2.8 %collective-permute-done.10 = bf16[4,4,48,384]{3,2,1,0:T(8,128)(2,1)S(1)} collective-permute-done((bf16[4,4,48,384]{3,2,1,0:T(8,128)(2,1)S(1)}, bf16[4,4,48,384]{3,2,1,0:T(8,128)(2,1)S(1)}, u32[]{:S(2)}, u32[]{:S(2)}) %collective-permute-start.10) | collective-permute-done | bytes 589856 | tf_op jit(solution)/shard_map/ppermute | solution.py:475
  108.0 12.7 %shard_map.315 = (f32[2,256,384]{2,1,0:T(8,128)}, f32[2,2,384]{2,1,0:T(2,128)}, f32[1,768]{1,0:T(1,128)}, f32[8,2,48,384]{3,2,1,0:T(8,128)}, bf16[8,2,48,384]{3,2,1,0:T(8,128)(2,1)}) custom-call(s32[2]{0:T(128)} %pad_add_fusion.place, bf16[4,256,384]{2,1,0:T(8,128)(2,1)} %lat.7, f32[4,256,384]{2,1,0:T(8,128)} %get-tuple-element.65.dmid, ...), custom_call_target="tpu_custom_call" | custom-call | flops 10000000000 | bytes 10000000 | tf_op jit(solution)/shard_map/pallas_call | solution.py:556
  120.7 2.2 %collective-permute-done.11.received = bf16[8,2,48,384]{3,2,1,0:T(8,128)(2,1)S(1)} collective-permute-done((bf16[8,2,48,384]{3,2,1,0:T(8,128)(2,1)}, bf16[8,2,48,384]{3,2,1,0:T(8,128)(2,1)S(1)}, u32[]{:S(2)}, u32[]{:S(2)}) %collective-permute-start.11) | collective-permute-done | bytes 589856 | tf_op jit(solution)/shard_map/ppermute | solution.py:475
  123.7 2.6 %pack_message.1 = bf16[8,128,384]{2,1,0:T(8,128)(2,1)} custom-call(f32[8,2,48,384]{3,2,1,0:T(8,128)} %get-tuple-element.75.keep, bf16[8,2,48,384]{3,2,1,0:T(8,128)(2,1)} %copy-done.7, f32[4,6,384]{2,1,0:T(8,128)} %get-tuple-element.77.mods_m, f32[2,2,384]{2,1,0:T(2,128)} %get-tuple-element.78.mods_0, f32[2,2,384]{2,1,0:T(2,128)} %get-tuple-element.79.mods_1, ...), custom_call_target="tpu_custom_call" | custom-call | tf_op jit(solution)/shard_map/pack_message/pallas_call | solution.py:726
  126.3 5.1 %all-to-all-start.2 = ((bf16[8,128,384]{2,1,0:T(8,128)(2,1)}), bf16[8,128,384]{2,1,0:T(8,128)(2,1)}, u32[]{:S(2)}, u32[]{:S(2)}) async-start(bf16[8,128,384]{2,1,0:T(8,128)(2,1)} %pack_message.1), calls=%async_computation.2 | async-start | bytes 1572864 | tf_op jit(solution)/shard_map/all_to_all | solution.py:515
  131.5 1.6 collective-permute-start.24
  133.1 2.0 collective-permute-start.15
  135.2 2.4 %collective-permute-start.16 = (bf16[4,48,384]{2,1,0:T(8,128)(2,1)S(1)}, bf16[4,48,384]{2,1,0:T(8,128)(2,1)S(1)}, u32[]{:S(2)}, u32[]{:S(2)}) collective-permute-start(bf16[4,48,384]{2,1,0:T(8,128)(2,1)S(1)} %get-tuple-element.108), channel_id=1, source_target_pairs={{0,16},{4,20},{8,24},{12,28},{16,0},{20,4},{24,8},{28,12},{1,17},{... | collective-permute-start | bytes 442376 | tf_op jit(solution)/shard_map/ppermute | solution.py:475
  138.9 9.7 %collective-permute-done.15 = bf16[4,48,384]{2,1,0:T(8,128)(2,1)S(1)} collective-permute-done((bf16[4,48,384]{2,1,0:T(8,128)(2,1)S(1)}, bf16[4,48,384]{2,1,0:T(8,128)(2,1)S(1)}, u32[]{:S(2)}, u32[]{:S(2)}) %collective-permute-start.15) | collective-permute-done | bytes 147488 | tf_op jit(solution)/shard_map/ppermute | solution.py:475
  148.6 13.9 %collective-permute-done.16 = bf16[4,48,384]{2,1,0:T(8,128)(2,1)S(1)} collective-permute-done((bf16[4,48,384]{2,1,0:T(8,128)(2,1)S(1)}, bf16[4,48,384]{2,1,0:T(8,128)(2,1)S(1)}, u32[]{:S(2)}, u32[]{:S(2)}) %collective-permute-start.16) | collective-permute-done | bytes 147488 | tf_op jit(solution)/shard_map/ppermute | solution.py:475
  164.1 1.9 open_message.1
  168.4 4.8 %all-to-all-start.3 = ((f32[8,1,192]{2,1,0:T(1,128)}), f32[8,1,192]{2,1,0:T(1,128)S(1)}, u32[]{:S(2)}, u32[]{:S(2)}) async-start(f32[8,1,192]{2,1,0:T(1,128)} %reshape.247), calls=%async_computation.3 | async-start | bytes 16384 | tf_op jit(solution)/shard_map/all_to_all | solution.py:515
  173.9 5.8 %all-to-all-done.3 = f32[8,1,192]{2,1,0:T(1,128)S(1)} async-done(((f32[8,1,192]{2,1,0:T(1,128)}), f32[8,1,192]{2,1,0:T(1,128)S(1)}, u32[]{:S(2)}, u32[]{:S(2)}) %all-to-all-start.3) | async-done | bytes 6176 | tf_op jit(solution)/shard_map/all_to_all | solution.py:515
  184.4 3.4 %collective-permute-done.14.refs_3_ = bf16[2,56,384]{2,1,0:T(8,128)(2,1)S(1)} collective-permute-done((bf16[2,56,384]{2,1,0:T(8,128)(2,1)}, bf16[2,56,384]{2,1,0:T(8,128)(2,1)S(1)}, u32[]{:S(2)}, u32[]{:S(2)}) %collective-permute-start.14) | collective-permute-done | bytes 86048 | tf_op jit(solution)/shard_map/ppermute | solution.py:475
  190.2 1.6 collective-permute-start.23
  193.9 4.1 %collective-permute-done.21.refs_9_ = bf16[32,2304]{1,0:T(8,128)(2,1)S(1)} collective-permute-done((bf16[32,2304]{1,0:T(8,128)(2,1)}, bf16[32,2304]{1,0:T(8,128)(2,1)S(1)}, u32[]{:S(2)}, u32[]{:S(2)}) %collective-permute-start.21) | collective-permute-done | bytes 147488 | tf_op jit(solution)/shard_map/ppermute | solution.py:475
  198.0 2.1 %collective-permute-done.23.refs_11_ = bf16[32,2304]{1,0:T(8,128)(2,1)S(1)} collective-permute-done((bf16[32,2304]{1,0:T(8,128)(2,1)}, bf16[32,2304]{1,0:T(8,128)(2,1)S(1)}, u32[]{:S(2)}, u32[]{:S(2)}) %collective-permute-start.23) | collective-permute-done | bytes 147488 | tf_op jit(solution)/shard_map/ppermute | solution.py:475
  200.8 7.4 %adam.1 = (f32[48,4992]{1,0:T(8,128)}, f32[48,384]{1,0:T(8,128)}, f32[4,48,384]{2,1,0:T(8,128)}, f32[48,4992]{1,0:T(8,128)}, f32[48,384]{1,0:T(8,128)}, /*index=...) custom-call(s32[2]{0:T(128)} %pad_add_fusion.place, ...), custom_call_target="tpu_custom_call" | custom-call | tf_op jit(solution)/shard_map/adam/pallas_call | solution.py:782
  (149 shorter events, 28.0 us)
Async XLA Ops:
  4.3 30.0 %all-to-all-start = ((bf16[8,56,384]{2,1,0:T(8,128)(2,1)}), bf16[8,56,384]{2,1,0:T(8,128)(2,1)S(1)}, u32[]{:S(2)}, u32[]{:S(2)}) async-start(bf16[8,56,384]{2,1,0:T(8,128)(2,1)} %broadcast_in_dim.2), calls=%async_computation | async-start | bytes 688128 | tf_op jit(solution)/shard_map/all_to_all | solution.py:515
  11.7 12.2 %collective-permute-start.3 = (bf16[1,192,384]{2,1,0:T(8,128)(2,1)S(1)}, bf16[1,192,384]{2,1,0:T(8,128)(2,1)S(1)}, u32[]{:S(2)}, u32[]{:S(2)}) collective-permute-start(bf16[1,192,384]{2,1,0:T(8,128)(2,1)S(1)} %pad_maximum_fusion.2), channel_id=1, source_target_pairs={{0,8},{4,12},{8,0},{12,4},{16,24},{20,28},{24,16},{28,20},{1,9},{5... | collective-permute-start | bytes 442376 | tf_op jit(solution)/shard_map/ppermute | solution.py:475
  13.7 19.4 %collective-permute-start.4 = (bf16[1,192,384]{2,1,0:T(8,128)(2,1)S(1)}, bf16[1,192,384]{2,1,0:T(8,128)(2,1)S(1)}, u32[]{:S(2)}, u32[]{:S(2)}) collective-permute-start(bf16[1,192,384]{2,1,0:T(8,128)(2,1)S(1)} %pad_maximum_fusion.2), channel_id=1, source_target_pairs={{0,16},{4,20},{8,24},{12,28},{16,0},{20,4},{24,8},{28,12},{1,17},{... | collective-permute-start | bytes 442376 | tf_op jit(solution)/shard_map/ppermute | solution.py:475
  16.1 17.0 %collective-permute-start.5 = (bf16[1,192,384]{2,1,0:T(8,128)(2,1)S(1)}, bf16[1,192,384]{2,1,0:T(8,128)(2,1)S(1)}, u32[]{:S(2)}, u32[]{:S(2)}) collective-permute-start(bf16[1,192,384]{2,1,0:T(8,128)(2,1)S(1)} %pad_maximum_fusion.2), channel_id=1, source_target_pairs={{0,24},{4,28},{8,16},{12,20},{16,8},{20,12},{24,0},{28,4},{1,25},{... | collective-permute-start | bytes 442376 | tf_op jit(solution)/shard_map/ppermute | solution.py:475
  33.2 12.9 %collective-permute-start.6 = (bf16[4,192,384]{2,1,0:T(8,128)(2,1)S(1)}, bf16[4,192,384]{2,1,0:T(8,128)(2,1)}, u32[]{:S(2)}, u32[]{:S(2)}) collective-permute-start(bf16[4,192,384]{2,1,0:T(8,128)(2,1)S(1)} %pad_maximum_fusion.1.p0), channel_id=1, source_target_pairs={{0,4},{4,0},{8,12},{12,8},{16,20},{20,16},{24,28},{28,24},{1,5},{5... | collective-permute-start | bytes 1769480 | tf_op jit(solution)/shard_map/ppermute | solution.py:475
  35.3 113.3 %copy-start.18 = (bf16[32,48]{1,0:T(8,128)(2,1)}, bf16[32,48]{1,0:T(8,128)(2,1)S(1)}, u32[]{:S(2)}) copy-start(bf16[32,48]{1,0:T(8,128)(2,1)S(1)} %multiply_convert_fusion.refs_12_) | copy-start | bytes 9220
  35.3 7.3 %collective-permute-start = (bf16[8,56,384]{2,1,0:T(8,128)(2,1)S(1)}, bf16[8,56,384]{2,1,0:T(8,128)(2,1)S(1)}, u32[]{:S(2)}, u32[]{:S(2)}) collective-permute-start(bf16[8,56,384]{2,1,0:T(8,128)(2,1)S(1)} %all-to-all-done.p0), channel_id=1, source_target_pairs={{0,2},{1,3},{2,0},{3,1},{4,6},{5,7},{6,4},{7,5},{8,10},{9,11},{10,... | collective-permute-start | bytes 1032200 | tf_op jit(solution)/shard_map/ppermute | solution.py:475
  37.8 12.9 %all-to-all-start.1 = ((f32[8,4,2304]{2,1,0:T(4,128)}), f32[8,4,2304]{2,1,0:T(4,128)S(1)}, u32[]{:S(2)}, u32[]{:S(2)}) async-start(f32[8,4,2304]{2,1,0:T(4,128)} %reshape.230), calls=%async_computation.1 | async-start | bytes 589824 | tf_op jit(solution)/shard_map/all_to_all | solution.py:515
  41.8 9.6 %collective-permute-start.1 = (bf16[8,56,384]{2,1,0:T(8,128)(2,1)S(1)}, bf16[8,56,384]{2,1,0:T(8,128)(2,1)}, u32[]{:S(2)}, u32[]{:S(2)}) collective-permute-start(bf16[8,56,384]{2,1,0:T(8,128)(2,1)S(1)} %all-to-all-done.p0), channel_id=1, source_target_pairs={{0,1},{1,0},{2,3},{3,2},{4,5},{5,4},{6,7},{7,6},{8,9},{9,8},{10,11... | collective-permute-start | bytes 1032200 | tf_op jit(solution)/shard_map/ppermute | solution.py:475
  42.6 8.9 %collective-permute-start.2 = (bf16[8,56,384]{2,1,0:T(8,128)(2,1)S(1)}, bf16[8,56,384]{2,1,0:T(8,128)(2,1)}, u32[]{:S(2)}, u32[]{:S(2)}) collective-permute-start(bf16[8,56,384]{2,1,0:T(8,128)(2,1)S(1)} %collective-permute-done.p1), channel_id=1, source_target_pairs={{0,1},{1,0},{2,3},{3,2},{4,5},{5,4},{6,7},{7,6},{8,9},{9,8},{10,11... | collective-permute-start | bytes 1032200 | tf_op jit(solution)/shard_map/ppermute | solution.py:475
  43.3 23.0 %collective-permute-start.7 = (bf16[4,192,384]{2,1,0:T(8,128)(2,1)S(1)}, bf16[4,192,384]{2,1,0:T(8,128)(2,1)}, u32[]{:S(2)}, u32[]{:S(2)}) collective-permute-start(bf16[4,192,384]{2,1,0:T(8,128)(2,1)S(1)} %pad_maximum_fusion.1.p0), channel_id=1, source_target_pairs={{0,1},{1,0},{2,3},{3,2},{4,5},{5,4},{6,7},{7,6},{8,9},{9,8},{10,11... | collective-permute-start | bytes 1769480 | tf_op jit(solution)/shard_map/ppermute | solution.py:475
  46.1 20.1 %collective-permute-start.8 = (bf16[4,192,384]{2,1,0:T(8,128)(2,1)}, bf16[4,192,384]{2,1,0:T(8,128)(2,1)}, u32[]{:S(2)}, u32[]{:S(2)}) collective-permute-start(bf16[4,192,384]{2,1,0:T(8,128)(2,1)} %collective-permute-done.6.p1), channel_id=1, source_target_pairs={{0,1},{1,0},{2,3},{3,2},{4,5},{5,4},{6,7},{7,6},{8,9},{9,8},{10,11... | collective-permute-start | bytes 1769480 | tf_op jit(solution)/shard_map/ppermute | solution.py:475
  87.3 3.1 %collective-permute-start.9 = (bf16[8,4,48,384]{3,2,1,0:T(8,128)(2,1)}, bf16[8,4,48,384]{3,2,1,0:T(8,128)(2,1)S(1)}, u32[]{:S(2)}, u32[]{:S(2)}) collective-permute-start(bf16[8,4,48,384]{3,2,1,0:T(8,128)(2,1)} %get-tuple-element.63), channel_id=1, source_target_pairs={{0,1},{1,0},{2,3},{3,2},{4,5},{5,4},{6,7},{7,6},{8,9},{9,8},{10,11... | collective-permute-start | bytes 3538952 | tf_op jit(solution)/shard_map/ppermute | solution.py:475
  92.4 15.4 %collective-permute-start.10 = (bf16[4,4,48,384]{3,2,1,0:T(8,128)(2,1)S(1)}, bf16[4,4,48,384]{3,2,1,0:T(8,128)(2,1)S(1)}, u32[]{:S(2)}, u32[]{:S(2)}) collective-permute-start(bf16[4,4,48,384]{3,2,1,0:T(8,128)(2,1)S(1)} %slice.217), channel_id=1, source_target_pairs={{0,4},{4,0},{8,12},{12,8},{16,20},{20,16},{24,28},{28,24},{1,5},{5... | collective-permute-start | bytes 1769480 | tf_op jit(solution)/shard_map/ppermute | solution.py:475
  120.6 2.3 %collective-permute-start.11 = (bf16[8,2,48,384]{3,2,1,0:T(8,128)(2,1)}, bf16[8,2,48,384]{3,2,1,0:T(8,128)(2,1)S(1)}, u32[]{:S(2)}, u32[]{:S(2)}) collective-permute-start(bf16[8,2,48,384]{3,2,1,0:T(8,128)(2,1)} %get-tuple-element.76), channel_id=1, source_target_pairs={{0,1},{1,0},{2,3},{3,2},{4,5},{5,4},{6,7},{7,6},{8,9},{9,8},{10,11... | collective-permute-start | bytes 1769480 | tf_op jit(solution)/shard_map/ppermute | solution.py:475
  126.3 37.8 %all-to-all-start.2 = ((bf16[8,128,384]{2,1,0:T(8,128)(2,1)}), bf16[8,128,384]{2,1,0:T(8,128)(2,1)}, u32[]{:S(2)}, u32[]{:S(2)}) async-start(bf16[8,128,384]{2,1,0:T(8,128)(2,1)} %pack_message.1), calls=%async_computation.2 | async-start | bytes 1572864 | tf_op jit(solution)/shard_map/all_to_all | solution.py:515
  131.5 56.6 %collective-permute-start.24 = (bf16[32,48]{1,0:T(8,128)(2,1)S(1)}, bf16[32,48]{1,0:T(8,128)(2,1)S(1)}, u32[]{:S(2)}, u32[]{:S(2)}) collective-permute-start(bf16[32,48]{1,0:T(8,128)(2,1)S(1)} %multiply_convert_fusion.refs_12_), channel_id=1, source_target_pairs={{0,2},{1,3},{2,0},{3,1},{4,6},{5,7},{6,4},{7,5},{8,10},{9,11},{10,... | collective-permute-start | bytes 9224 | tf_op jit(solution)/shard_map/ppermute | solution.py:475
  133.0 56.6 %collective-permute-start.25 = (bf16[32,48]{1,0:T(8,128)(2,1)S(1)}, bf16[32,48]{1,0:T(8,128)(2,1)S(1)}, u32[]{:S(2)}, u32[]{:S(2)}) collective-permute-start(bf16[32,48]{1,0:T(8,128)(2,1)S(1)} %multiply_convert_fusion.refs_12_), channel_id=1, source_target_pairs={{0,1},{1,0},{2,3},{3,2},{4,5},{5,4},{6,7},{7,6},{8,9},{9,8},{10,11... | collective-permute-start | bytes 9224 | tf_op jit(solution)/shard_map/ppermute | solution.py:475
  133.1 15.4 %collective-permute-start.15 = (bf16[4,48,384]{2,1,0:T(8,128)(2,1)S(1)}, bf16[4,48,384]{2,1,0:T(8,128)(2,1)S(1)}, u32[]{:S(2)}, u32[]{:S(2)}) collective-permute-start(bf16[4,48,384]{2,1,0:T(8,128)(2,1)S(1)} %get-tuple-element.106), channel_id=1, source_target_pairs={{0,8},{4,12},{8,0},{12,4},{16,24},{20,28},{24,16},{28,20},{1,9},{5... | collective-permute-start | bytes 442376 | tf_op jit(solution)/shard_map/ppermute | solution.py:475
  135.2 27.3 %collective-permute-start.16 = (bf16[4,48,384]{2,1,0:T(8,128)(2,1)S(1)}, bf16[4,48,384]{2,1,0:T(8,128)(2,1)S(1)}, u32[]{:S(2)}, u32[]{:S(2)}) collective-permute-start(bf16[4,48,384]{2,1,0:T(8,128)(2,1)S(1)} %get-tuple-element.108), channel_id=1, source_target_pairs={{0,16},{4,20},{8,24},{12,28},{16,0},{20,4},{24,8},{28,12},{1,17},{... | collective-permute-start | bytes 442376 | tf_op jit(solution)/shard_map/ppermute | solution.py:475
  137.5 24.9 %collective-permute-start.17 = (bf16[4,48,384]{2,1,0:T(8,128)(2,1)S(1)}, bf16[4,48,384]{2,1,0:T(8,128)(2,1)S(1)}, u32[]{:S(2)}, u32[]{:S(2)}) collective-permute-start(bf16[4,48,384]{2,1,0:T(8,128)(2,1)S(1)} %get-tuple-element.107), channel_id=1, source_target_pairs={{0,24},{4,28},{8,16},{12,20},{16,8},{20,12},{24,0},{28,4},{1,25},{... | collective-permute-start | bytes 442376 | tf_op jit(solution)/shard_map/ppermute | solution.py:475
  148.6 41.6 %collective-permute-start.26 = (bf16[32,48]{1,0:T(8,128)(2,1)S(1)}, bf16[32,48]{1,0:T(8,128)(2,1)S(1)}, u32[]{:S(2)}, u32[]{:S(2)}) collective-permute-start(bf16[32,48]{1,0:T(8,128)(2,1)S(1)} %multiply_convert_fusion.refs_12_), channel_id=1, source_target_pairs={{0,3},{1,2},{2,1},{3,0},{4,7},{5,6},{6,5},{7,4},{8,11},{9,10},{10,... | collective-permute-start | bytes 9224 | tf_op jit(solution)/shard_map/ppermute | solution.py:475
  162.5 27.7 %collective-permute-start.18 = (bf16[4,48,384]{2,1,0:T(8,128)(2,1)S(1)}, bf16[4,48,384]{2,1,0:T(8,128)(2,1)S(1)}, u32[]{:S(2)}, u32[]{:S(2)}) collective-permute-start(bf16[4,48,384]{2,1,0:T(8,128)(2,1)S(1)} %fusion.2.refs_4_), channel_id=1, source_target_pairs={{0,2},{1,3},{2,0},{3,1},{4,6},{5,7},{6,4},{7,5},{8,10},{9,11},{10,... | collective-permute-start | bytes 442376 | tf_op jit(solution)/shard_map/ppermute | solution.py:475
  166.0 15.6 %collective-permute-start.12 = (bf16[2,56,384]{2,1,0:T(8,128)(2,1)}, bf16[2,56,384]{2,1,0:T(8,128)(2,1)S(1)}, u32[]{:S(2)}, u32[]{:S(2)}) collective-permute-start(bf16[2,56,384]{2,1,0:T(8,128)(2,1)} %get-tuple-element.83.refs_0_), channel_id=1, source_target_pairs={{0,2},{1,3},{2,0},{3,1},{4,6},{5,7},{6,4},{7,5},{8,10},{9,11},{10,... | collective-permute-start | bytes 258056 | tf_op jit(solution)/shard_map/ppermute | solution.py:475
  168.4 11.3 %all-to-all-start.3 = ((f32[8,1,192]{2,1,0:T(1,128)}), f32[8,1,192]{2,1,0:T(1,128)S(1)}, u32[]{:S(2)}, u32[]{:S(2)}) async-start(f32[8,1,192]{2,1,0:T(1,128)} %reshape.247), calls=%async_computation.3 | async-start | bytes 16384 | tf_op jit(solution)/shard_map/all_to_all | solution.py:515
  181.7 1.5 collective-permute-start.13
  183.2 4.7 %collective-permute-start.14 = (bf16[2,56,384]{2,1,0:T(8,128)(2,1)}, bf16[2,56,384]{2,1,0:T(8,128)(2,1)S(1)}, u32[]{:S(2)}, u32[]{:S(2)}) collective-permute-start(bf16[2,56,384]{2,1,0:T(8,128)(2,1)} %get-tuple-element.83.refs_0_), channel_id=1, source_target_pairs={{0,3},{1,2},{2,1},{3,0},{4,7},{5,6},{6,5},{7,4},{8,11},{9,10},{10,... | collective-permute-start | bytes 258056 | tf_op jit(solution)/shard_map/ppermute | solution.py:475
  187.9 4.6 %collective-permute-start.19 = (bf16[4,48,384]{2,1,0:T(8,128)(2,1)S(1)}, bf16[4,48,384]{2,1,0:T(8,128)(2,1)S(1)}, u32[]{:S(2)}, u32[]{:S(2)}) collective-permute-start(bf16[4,48,384]{2,1,0:T(8,128)(2,1)S(1)} %fusion.2.refs_4_), channel_id=1, source_target_pairs={{0,1},{1,0},{2,3},{3,2},{4,5},{5,4},{6,7},{7,6},{8,9},{9,8},{10,11... | collective-permute-start | bytes 442376 | tf_op jit(solution)/shard_map/ppermute | solution.py:475
  188.1 5.8 %collective-permute-start.20 = (bf16[4,48,384]{2,1,0:T(8,128)(2,1)S(1)}, bf16[4,48,384]{2,1,0:T(8,128)(2,1)S(1)}, u32[]{:S(2)}, u32[]{:S(2)}) collective-permute-start(bf16[4,48,384]{2,1,0:T(8,128)(2,1)S(1)} %fusion.2.refs_4_), channel_id=1, source_target_pairs={{0,3},{1,2},{2,1},{3,0},{4,7},{5,6},{6,5},{7,4},{8,11},{9,10},{10,... | collective-permute-start | bytes 442376 | tf_op jit(solution)/shard_map/ppermute | solution.py:475
  189.6 8.4 %collective-permute-start.21 = (bf16[32,2304]{1,0:T(8,128)(2,1)}, bf16[32,2304]{1,0:T(8,128)(2,1)S(1)}, u32[]{:S(2)}, u32[]{:S(2)}) collective-permute-start(bf16[32,2304]{1,0:T(8,128)(2,1)} %get-tuple-element.82.refs_8_), channel_id=1, source_target_pairs={{0,2},{1,3},{2,0},{3,1},{4,6},{5,7},{6,4},{7,5},{8,10},{9,11},{10,... | collective-permute-start | bytes 442376 | tf_op jit(solution)/shard_map/ppermute | solution.py:475
  190.2 7.8 %collective-permute-start.22 = (bf16[32,2304]{1,0:T(8,128)(2,1)}, bf16[32,2304]{1,0:T(8,128)(2,1)S(1)}, u32[]{:S(2)}, u32[]{:S(2)}) collective-permute-start(bf16[32,2304]{1,0:T(8,128)(2,1)} %get-tuple-element.82.refs_8_), channel_id=1, source_target_pairs={{0,1},{1,0},{2,3},{3,2},{4,5},{5,4},{6,7},{7,6},{8,9},{9,8},{10,11... | collective-permute-start | bytes 442376 | tf_op jit(solution)/shard_map/ppermute | solution.py:475
  190.2 9.9 %collective-permute-start.23 = (bf16[32,2304]{1,0:T(8,128)(2,1)}, bf16[32,2304]{1,0:T(8,128)(2,1)S(1)}, u32[]{:S(2)}, u32[]{:S(2)}) collective-permute-start(bf16[32,2304]{1,0:T(8,128)(2,1)} %get-tuple-element.82.refs_8_), channel_id=1, source_target_pairs={{0,3},{1,2},{2,1},{3,0},{4,7},{5,6},{6,5},{7,4},{8,11},{9,10},{10,... | collective-permute-start | bytes 442376 | tf_op jit(solution)/shard_map/ppermute | solution.py:475
  (26 other events, 419.0 us)
